TPU v7x, 32 devices: a whole 2x2x4 slice. The times are simulated.
32 devices in a mesh: atm: 4 (over y, x), ocn: 8 (over z, core).
Axes of the slice: x: 2, y: 2, z: 4, core: 2. Of those that a mesh axis runs over, the one named last changes fastest.
Arguments:
- atm_flux: float32 [8, 221184], P(None, ('atm', 'ocn')), may hold values from -6 to 6
- send_cell: int32 [32, 32, 512], P(('atm', 'ocn')), may hold values from 0 to 6911, as said below
- send_weight: float32 [32, 32, 512], P(('atm', 'ocn')), may hold values from 0 to 1, as said below
- recv_cell: int32 [32, 32, 512], P(('atm', 'ocn')), may hold values from 0 to 8191, as said below
- temp: float32 [20, 128, 2048], P(None, 'ocn', 'atm'), may hold values from -6 to 6
- salt: float32 [20, 128, 2048], P(None, 'ocn', 'atm'), may hold values from -6 to 6
- uvel: float32 [20, 128, 2048], P(None, 'ocn', 'atm'), may hold values from -4 to 4
- vvel: float32 [20, 128, 2048], P(None, 'ocn', 'atm'), may hold values from -4 to 4
- wet_mask: int32 [128, 2048], P('ocn', 'atm'), may hold values 0 or 1
- vert_mix: float32 [19, 128, 2048], P(None, 'ocn', 'atm'), may hold values from 0.05 to 5
Outputs:
- temp_out: float32 [20, 128, 2048], P(None, 'ocn', 'atm')
- salt_out: float32 [20, 128, 2048], P(None, 'ocn', 'atm')
- uvel_out: float32 [20, 128, 2048], P(None, 'ocn', 'atm')
- vvel_out: float32 [20, 128, 2048], P(None, 'ocn', 'atm')
- atm_surface: float32 [4, 221184], P(None, ('atm', 'ocn'))
Inputs may be any that keep to these rules, and one draw needn't show every extreme that they name: Slot c of send_cell[s, d], send_weight[s, d] and recv_cell[d, s] is one intersection between a cell of source device s and a cell of destination device d. Each pair of devices uses a leading run of 128 to 512 slots; one destination device receives all 512 slots from every source. Empty slots hold cell 0 and weight 0. `recv_cell`: local ocean cell numbers, as described for send_cell. `send_weight`: zero exactly in empty slots, else at least 0.02.
All inputs are finite; a program needn't handle non-finite values. No bound on the sum of `wet_mask` on one device may be relied on, other than what follows from the above.
Results may differ from a plain program's by a relative error of at most 0.00002.
Values sent between devices are 32-bit elements; how exact they have to be, the bound alone decides.
No kernel may reach another device: no remote copies, remote signals or barrier semaphores. Data moves between devices by JAX's collectives and lax.ppermute only.
A program may use at most 128 MiB of HBM per device.

v0:
```python
import jax
import jax.numpy as jnp
from jax import lax
from jax.sharding import PartitionSpec as P

STEPS = 2


courant_scale = 0.05
diffusion = 0.15
viscosity = 0.15
coriolis = 0.1
heat_gain = 0.25
water_gain = 0.25
stress_gain = 0.25


def partner(block, axis, distance):
    count = lax.axis_size(axis)
    route = []
    for low in range(count):
        high = low | 1 << distance
        if high != low and high < count:
            route += [(low, high), (high, low)]
    return lax.ppermute(block, axis, route)


def padded(cells, sides, width, closed):
    for axis, dim in sides:
        count = lax.axis_size(axis)
        ends = count if closed else count - 1
        head = lax.slice_in_dim(cells, 0, width, axis=dim)
        tail = lax.slice_in_dim(cells, cells.shape[dim] - width, cells.shape[dim], axis=dim)
        cells = jnp.concatenate(
            [
                lax.ppermute(tail, axis, [(i, (i + 1) % count) for i in range(ends)]),
                cells,
                lax.ppermute(head, axis, [((i + 1) % count, i) for i in range(ends)]),
            ],
            axis=dim,
        )
    return cells


def make_sign(levels):
    return jnp.concatenate(
        [
            jnp.ones((2 * levels,), jnp.float32),
            -jnp.ones((2 * levels,), jnp.float32),
            jnp.ones((1,), jnp.float32),
        ]
    )


def coriolis_profile(row_ids, total_rows):
    mirrored = jnp.where(row_ids >= total_rows, 2 * total_rows - 1 - row_ids, row_ids)
    latitude = jnp.pi * ((mirrored.astype(jnp.float32) + 0.5) / total_rows - 0.5)
    return (coriolis * jnp.sin(latitude))[:, None]


def tendency(centre, east_cells, west_cells, north_cells, south_cells, coriolis_rows, levels):
    wet_cells = centre[-1]
    gate_east = east_cells[-1] * wet_cells
    gate_west = west_cells[-1] * wet_cells
    gate_north = north_cells[-1] * wet_cells
    gate_south = south_cells[-1] * wet_cells
    fields = centre[:-1]
    diff_east = gate_east * (east_cells[:-1] - fields)
    diff_west = gate_west * (fields - west_cells[:-1])
    diff_north = gate_north * (north_cells[:-1] - fields)
    diff_south = gate_south * (fields - south_cells[:-1])
    laplace = diff_east - diff_west + diff_north - diff_south
    plane_shape = fields.shape[1:]
    velocity_east = fields[2 * levels : 3 * levels]
    velocity_north = fields[3 * levels : 4 * levels]
    courant_east = courant_scale * velocity_east
    courant_north = courant_scale * velocity_north

    def tracer_part(values_in):
        return values_in[: 2 * levels].reshape((2, levels) + plane_shape)

    upwind = (
        jnp.maximum(courant_east, 0.0) * tracer_part(diff_west)
        + jnp.minimum(courant_east, 0.0) * tracer_part(diff_east)
        + jnp.maximum(courant_north, 0.0) * tracer_part(diff_south)
        + jnp.minimum(courant_north, 0.0) * tracer_part(diff_north)
    )
    tracers = tracer_part(fields) + wet_cells * (diffusion * tracer_part(laplace) - upwind)
    east_next = velocity_east + wet_cells * (
        viscosity * laplace[2 * levels : 3 * levels] + coriolis_rows * velocity_north
    )
    north_next = velocity_north + wet_cells * (
        viscosity * laplace[3 * levels : 4 * levels] - coriolis_rows * velocity_east
    )
    return jnp.concatenate(
        [tracers.reshape((2 * levels,) + plane_shape), east_next, north_next, centre[-1:]], 0
    )


def surface_forcing(flux):
    heat_flux = flux[0] + flux[1] + flux[2] + flux[3]
    water_flux = flux[4] - flux[5]
    return jnp.stack(
        [
            heat_gain * heat_flux,
            water_gain * water_flux,
            stress_gain * flux[6],
            stress_gain * flux[7],
        ]
    )


def vertical_solve(fields, mixing):
    levels = fields.shape[1]
    factors = []
    partial_rows = []
    for level_index in range(levels):
        upper_mix = mixing[level_index - 1] if level_index > 0 else jnp.zeros_like(mixing[0])
        lower_mix = mixing[level_index] if level_index < levels - 1 else jnp.zeros_like(mixing[0])
        diagonal = 1.0 + upper_mix + lower_mix
        if level_index == 0:
            pivot_value = diagonal
            right_side = fields[:, 0]
        else:
            pivot_value = diagonal + upper_mix * factors[-1]
            right_side = fields[:, level_index] + upper_mix * partial_rows[-1]
        factors.append(-lower_mix / pivot_value)
        partial_rows.append(right_side / pivot_value)
    solved = [partial_rows[-1]]
    for level_index in range(levels - 2, -1, -1):
        solved.append(partial_rows[level_index] - factors[level_index] * solved[-1])
    return jnp.stack(solved[::-1], 1)


def mirror_partner(top_rows):
    mirrored = top_rows
    for bit_number in range(lax.axis_size("atm").bit_length() - 1):
        mirrored = partner(mirrored, "atm", bit_number)
    return mirrored


def extend(state_stack, margin_width, fold_sign):
    widened = padded(state_stack, (("atm", 2),), margin_width, True)
    top_rows = widened[:, widened.shape[1] - margin_width :, :]
    ghost_rows = mirror_partner(top_rows)[:, ::-1, ::-1] * fold_sign[:, None, None]
    heightened = padded(widened, (("ocn", 1),), margin_width, False)
    split_at = heightened.shape[1] - margin_width
    on_top = lax.axis_index("ocn") == lax.axis_size("ocn") - 1
    upper_rows = jnp.where(on_top, ghost_rows, heightened[:, split_at:, :])
    return jnp.concatenate([heightened[:, :split_at, :], upper_rows], 1)


def advance(extended, first_row, levels, block_rows):
    row_count = extended.shape[1] - 2
    row_ids = (
        lax.axis_index("ocn") * block_rows + first_row + jnp.arange(row_count, dtype=jnp.int32)
    )
    coriolis_rows = coriolis_profile(row_ids, block_rows * lax.axis_size("ocn"))
    return tendency(
        extended[:, 1:-1, 1:-1],
        extended[:, 1:-1, 2:],
        extended[:, 1:-1, :-2],
        extended[:, 2:, 1:-1],
        extended[:, :-2, 1:-1],
        coriolis_rows,
        levels,
    )


def per_device(
    atm_flux, send_cell, send_weight, recv_cell, temp, salt, uvel, vvel, wet_mask, vert_mix
):
    levels, block_rows, block_cols = temp.shape
    slot_cells = send_cell[0]
    slot_weights = send_weight[0]
    arrival_cells = recv_cell[0]
    owners, capacity = slot_cells.shape
    atm_cells = atm_flux.shape[1]
    field_count = atm_flux.shape[0]
    outgoing = (
        jnp.take(atm_flux, slot_cells.reshape(-1), axis=1).reshape(field_count, owners, capacity)
        * slot_weights[None]
    )
    incoming = lax.all_to_all(outgoing, ("atm", "ocn"), split_axis=1, concat_axis=1, tiled=True)
    ocean_flux = (
        jnp.zeros((field_count, block_rows * block_cols), jnp.float32)
        .at[:, arrival_cells.reshape(-1)]
        .add(incoming.reshape(field_count, -1))
        .reshape(field_count, block_rows, block_cols)
    )
    wet_cells = wet_mask.astype(jnp.float32)
    state_stack = jnp.concatenate([temp, salt, uvel, vvel, wet_cells[None]], 0)
    fold_sign = make_sign(levels)
    for step_index in range(STEPS):
        state_stack = advance(extend(state_stack, 1, fold_sign), 0, levels, block_rows)
    fields = state_stack[: 4 * levels].reshape(4, levels, block_rows, block_cols)
    surface_push = surface_forcing(ocean_flux) * wet_cells
    fields = fields.at[:, 0].add(surface_push)
    fields = vertical_solve(fields, vert_mix)
    surface = fields[:, 0].reshape(4, block_rows * block_cols)
    leaving = jnp.take(surface, arrival_cells.reshape(-1), axis=1).reshape(4, owners, capacity)
    returning = lax.all_to_all(leaving, ("atm", "ocn"), split_axis=1, concat_axis=1, tiled=True)
    weighted = returning * slot_weights[None]
    gathered_sum = (
        jnp.zeros((4, atm_cells), jnp.float32)
        .at[:, slot_cells.reshape(-1)]
        .add(weighted.reshape(4, -1))
    )
    weight_total = (
        jnp.zeros((atm_cells,), jnp.float32)
        .at[slot_cells.reshape(-1)]
        .add(slot_weights.reshape(-1))
    )
    atm_surface = gathered_sum / jnp.maximum(weight_total, 1.0)
    return (fields[0], fields[1], fields[2], fields[3], atm_surface)


def solution(mesh):
    in_specs = (
        P(None, ("atm", "ocn")),
        P(("atm", "ocn"), None, None),
        P(("atm", "ocn"), None, None),
        P(("atm", "ocn"), None, None),
        P(None, "ocn", "atm"),
        P(None, "ocn", "atm"),
        P(None, "ocn", "atm"),
        P(None, "ocn", "atm"),
        P("ocn", "atm"),
        P(None, "ocn", "atm"),
    )
    out_specs = (
        P(None, "ocn", "atm"),
        P(None, "ocn", "atm"),
        P(None, "ocn", "atm"),
        P(None, "ocn", "atm"),
        P(None, ("atm", "ocn")),
    )
    return jax.shard_map(
        per_device, mesh=mesh, in_specs=in_specs, out_specs=out_specs, check_vma=False
    )
```

profile of v0, /device:TPU:0, one launch (start us, length us, event | category | flops | bytes accessed | tf_op | source)
XLA Modules:
  0.0 708.5 jit_solution(15868452302978179485)
XLA Ops:
  5.9 1.4 copy-done.5
  9.8 3.9 collective-permute-start
  14.4 3.3 copy.196
  18.4 56.8 %gather_fusion = f32[16384,8]{1,0:T(8,128)} fusion(f32[8,6912]{0,1:T(8,128)} %copy.196, s32[16384]{0:T(1024)S(1)} %get-tuple-element.239), kind=kCustom, calls=%fused_computation | custom fusion | bytes 1114112 | tf_op jit(solution)/shard_map/jit(_take)/gather | solution.py:181
  75.2 5.9 copy.197
  81.1 2.0 select_multiply_fusion
  83.0 6.4 all-to-all-start
  104.7 2.8 pad_maximum_fusion.42
  107.5 1.7 collective-permute-start.2
  109.2 1.5 slice_bitcast_fusion.25
  112.0 2.9 collective-permute-done.2
  114.9 1.7 collective-permute-start.3
  128.2 2.0 collective-permute-start.5
  130.2 3.9 reverse
  134.2 1.8 broadcast_select_fusion.1
  136.9 4.7 add_subtract_fusion.1
  141.8 1.5 multiply_maximum_fusion.1
  148.1 1.5 collective-permute-start.6
  151.3 1.4 copy.266
  178.8 1.4 copy.226
  196.8 1.4 copy.249
  207.8 1.4 copy.222
  217.4 96.9 %scatter_custom_fusion.2 = f32[6912]{0:T(1024)S(1)} fusion(s32[16384]{0:T(1024)} %bitcast.498, f32[16384]{0:T(1024)S(1)} %bitcast.560, f32[]{:T(128)} %constant.83.clone.1), kind=kCustom, calls=%fused_computation.330 | custom fusion | flops 16384 | bytes 28160 | tf_op jit(solution)/shard_map/scatter-add | solution.py:212
  315.4 1.9 copy.193
  317.3 3.0 pad_maximum_fusion.39
  321.7 4.1 collective-permute-start.11
  329.8 6.4 collective-permute-done.9
  336.2 3.9 reverse.1
  340.1 1.6 broadcast_select_fusion
  341.7 1.6 fusion.50
  343.3 16.0 %add_subtract_fusion = (f32[80,16,512]{2,1,0:T(8,128)}, f32[80,16,512]{2,1,0:T(8,128)}, f32[80,16,512]{2,1,0:T(8,128)}, f32[80,16,512]{2,1,0:T(8,128)}, f32[80,16,512]{2,1,0:T(8,128)}) fusion(f32[1,16,512]{2,1,0:T(8,128)} %copy-done.19, f32[20,16,512]{2,1,0:T(8,128)S(1)} %get-tuple-element.128, f32[20,16,512]{2,1,0:T(8,128)S(1)} %get-tuple-element.104, ...), kind=kLoop, calls=%fused_computation.63 | loop fusion | flops 21626880 | bytes 16235920 | tf_op jit(solution)/shard_map/sub | solution.py:72
  359.4 1.9 fusion.43
  362.3 3.8 fusion.29
  366.5 5.7 copy.198
  372.2 109.0 %scatter_custom_fusion = f32[8,8192]{0,1:T(8,128)} fusion(s32[16384]{0:T(1024)} %bitcast.501, f32[16384,8]{1,0:T(8,128)} %copy.198, f32[]{:T(128)} %constant.83.clone.1), kind=kCustom, calls=%fused_computation.65 | custom fusion | flops 131072 | bytes 262656 | tf_op jit(solution)/shard_map/scatter-add | solution.py:188
  481.2 24.1 %fusion.5 = (f32[8192]{0:T(1024)S(1)}, f32[8192]{0:T(1024)S(1)}, f32[8192]{0:T(1024)S(1)}, f32[8192]{0:T(1024)S(1)}) fusion(f32[8,8192]{0,1:T(8,128)} %scatter_custom_fusion), kind=kLoop, calls=%fused_computation.14 | loop fusion | flops 65536 | bytes 393216 | tf_op jit(solution)/shard_map/mul | solution.py:105
  507.8 2.3 subtract_dynamic-update-slice_fusion
  514.1 3.0 multiply_subtract_fusion
  517.2 2.7 copy.199
  519.9 57.0 %gather_fusion.1 = f32[16384,4]{1,0:T(8,128)} fusion(f32[4,8192]{0,1:T(8,128)} %copy.199, s32[16384]{0:T(1024)S(1)} %copy-done.57), kind=kCustom, calls=%fused_computation.1 | custom fusion | bytes 589824 | tf_op jit(solution)/shard_map/jit(_take)/gather | solution.py:201
  576.9 5.4 copy.200
  583.1 3.2 all-to-all-start.1
  586.9 1.5 slice_bitcast_fusion
  588.5 8.2 %all-to-all-done.1 = f32[4,32,512]{2,0,1:T(4,128)S(1)} async-done(((f32[4,32,512]{2,0,1:T(4,128)}), f32[4,32,512]{2,0,1:T(4,128)S(1)}, u32[]{:S(2)}, u32[]{:S(2)}) %all-to-all-start.1) | async-done | bytes 262176 | tf_op jit(solution)/shard_map/all_to_all | solution.py:202
  596.8 5.1 copy.201
  601.9 98.7 %scatter_custom_fusion.1 = f32[4,6912]{0,1:T(8,128)S(1)} fusion(s32[16384]{0:T(1024)} %bitcast.499, f32[16384,4]{1,0:T(8,128)} %copy.201, f32[]{:T(128)} %constant.83.clone.1), kind=kCustom, calls=%fused_computation.68 | custom fusion | flops 65536 | bytes 111104 | tf_op jit(solution)/shard_map/scatter-add | solution.py:207
  700.7 4.4 broadcast_divide_fusion
  705.1 3.2 copy.202
  (372 shorter events, 119.7 us)
Async XLA Ops:
  5.8 8.2 %copy-start.54 = (s32[1,32,512]{2,1,0:T(8,128)S(1)}, s32[1,32,512]{2,1,0:T(8,128)}, u32[]{:S(2)}) copy-start(s32[1,32,512]{2,1,0:T(8,128)} %param.13) | copy-start | bytes 196612
  5.9 8.4 %copy-start.55 = (s32[1,32,512]{2,1,0:T(8,128)S(1)}, s32[1,32,512]{2,1,0:T(8,128)}, u32[]{:S(2)}) copy-start(s32[1,32,512]{2,1,0:T(8,128)} %param.15) | copy-start | bytes 196612
  9.8 93.3 %collective-permute-start = (f32[81,16,1]{0,1,2:T(8,128)S(1)}, f32[81,16,1]{0,1,2:T(8,128)S(1)}, u32[]{:S(2)}, u32[]{:S(2)}) collective-permute-start(f32[81,16,1]{0,1,2:T(8,128)S(1)} %copy.184), channel_id=1, source_target_pairs={{8,0},{16,8},{24,16},{0,24},{9,1},{17,9},{25,17},{1,25},{10,2},{18... | collective-permute-start | bytes 15560 | tf_op jit(solution)/shard_map/ppermute | solution.py:38
  14.0 89.5 %collective-permute-start.1 = (f32[81,16,1]{0,1,2:T(8,128)S(1)}, f32[81,16,1]{0,1,2:T(8,128)S(1)}, u32[]{:S(2)}, u32[]{:S(2)}) collective-permute-start(f32[81,16,1]{0,1,2:T(8,128)S(1)} %copy.186), channel_id=1, source_target_pairs={{0,8},{8,16},{16,24},{24,0},{1,9},{9,17},{17,25},{25,1},{2,10},{10... | collective-permute-start | bytes 15560 | tf_op jit(solution)/shard_map/ppermute | solution.py:36
  14.2 60.9 %copy-start.58 = (s32[16384,1]{0,1:T(1,128)}, s32[16384,1]{0,1:T(1,128)S(1)}, u32[]{:S(2)}) copy-start(s32[16384,1]{0,1:T(1,128)S(1)} %compare_select_fusion) | copy-start | bytes 196612
  14.4 60.8 %copy-start.59 = (s32[16384,1]{0,1:T(1,128)}, s32[16384,1]{0,1:T(1,128)S(1)}, u32[]{:S(2)}) copy-start(s32[16384,1]{0,1:T(1,128)S(1)} %compare_select_fusion.1) | copy-start | bytes 196612
  75.2 5.9 copy-start.23
  75.2 14.3 %copy-start.3 = (f32[19,16,512]{2,1,0:T(8,128)S(1)}, f32[19,16,512]{2,1,0:T(8,128)}, u32[]{:S(2)}) copy-start(f32[19,16,512]{2,1,0:T(8,128)} %param.21) | copy-start | bytes 1867780
  83.0 283.4 %all-to-all-start = ((f32[8,32,512]{2,0,1:T(8,128)}), f32[8,32,512]{2,0,1:T(8,128)}, u32[]{:S(2)}, u32[]{:S(2)}) async-start(f32[8,32,512]{2,0,1:T(8,128)} %select_multiply_fusion), calls=%async_computation | async-start | bytes 1048576 | tf_op jit(solution)/shard_map/all_to_all | solution.py:184
  90.1 12.2 %copy-start.28 = (f32[1,16,512]{2,1,0:T(8,128)}, f32[1,16,512]{2,1,0:T(8,128)S(1)}, u32[]{:S(2)}) copy-start(f32[1,16,512]{2,1,0:T(8,128)S(1)} %get-tuple-element.47) | copy-start | bytes 98308
  92.5 9.1 %copy-start.30 = (f32[1,16,512]{2,1,0:T(8,128)}, f32[1,16,512]{2,1,0:T(8,128)S(1)}, u32[]{:S(2)}) copy-start(f32[1,16,512]{2,1,0:T(8,128)S(1)} %get-tuple-element.49) | copy-start | bytes 98308
  93.2 9.8 %copy-start.32 = (f32[1,16,512]{2,1,0:T(8,128)}, f32[1,16,512]{2,1,0:T(8,128)S(1)}, u32[]{:S(2)}) copy-start(f32[1,16,512]{2,1,0:T(8,128)S(1)} %get-tuple-element.51) | copy-start | bytes 98308
  93.8 9.2 %copy-start.33 = (f32[1,16,512]{2,1,0:T(8,128)}, f32[1,16,512]{2,1,0:T(8,128)S(1)}, u32[]{:S(2)}) copy-start(f32[1,16,512]{2,1,0:T(8,128)S(1)} %get-tuple-element.53) | copy-start | bytes 98308
  94.4 8.5 %copy-start.34 = (f32[1,16,512]{2,1,0:T(8,128)}, f32[1,16,512]{2,1,0:T(8,128)S(1)}, u32[]{:S(2)}) copy-start(f32[1,16,512]{2,1,0:T(8,128)S(1)} %get-tuple-element.55) | copy-start | bytes 98308
  95.1 7.9 %copy-start.35 = (f32[1,16,512]{2,1,0:T(8,128)}, f32[1,16,512]{2,1,0:T(8,128)S(1)}, u32[]{:S(2)}) copy-start(f32[1,16,512]{2,1,0:T(8,128)S(1)} %get-tuple-element.57) | copy-start | bytes 98308
  95.7 7.2 %copy-start.36 = (f32[1,16,512]{2,1,0:T(8,128)}, f32[1,16,512]{2,1,0:T(8,128)S(1)}, u32[]{:S(2)}) copy-start(f32[1,16,512]{2,1,0:T(8,128)S(1)} %get-tuple-element.59) | copy-start | bytes 98308
  96.4 6.6 copy-start.37
  97.0 6.0 copy-start.38
  97.7 5.3 copy-start.39
  98.3 4.7 copy-start.40
  99.0 4.0 copy-start.41
  103.1 16.2 %copy-start.21 = (f32[1,16,512]{2,1,0:T(8,128)}, f32[1,16,512]{2,1,0:T(8,128)S(1)}, u32[]{:S(2)}) copy-start(f32[1,16,512]{2,1,0:T(8,128)S(1)} %get-tuple-element.81) | copy-start | bytes 98308
  104.7 29.5 %copy-start.102 = (f32[81]{0:T(128)S(1)}, f32[81]{0:T(128)}, u32[]{:S(2)}) copy-start(f32[81]{0:T(128)} %constant.80.clone.1) | copy-start | bytes 976
  107.5 7.3 %copy-start.60 = (f32[81,1,514]{2,1,0:T(1,128)}, f32[81,1,514]{2,1,0:T(1,128)S(1)}, u32[]{:S(2)}) copy-start(f32[81,1,514]{2,1,0:T(1,128)S(1)} %get-tuple-element.123) | copy-start | bytes 499612
  107.5 7.3 %collective-permute-start.2 = (f32[81,1,514]{2,1,0:T(1,128)S(1)}, f32[81,1,514]{2,1,0:T(1,128)}, u32[]{:S(2)}, u32[]{:S(2)}) collective-permute-start(f32[81,1,514]{2,1,0:T(1,128)S(1)} %get-tuple-element.123), channel_id=1, source_target_pairs={{0,8},{8,0},{16,24},{24,16},{1,9},{9,1},{17,25},{25,17},{2,10},{10... | collective-permute-start | bytes 499616 | tf_op jit(solution)/shard_map/ppermute | solution.py:25
  110.7 23.5 %collective-permute-start.4 = (f32[81,1,514]{2,1,0:T(1,128)}, f32[81,1,514]{2,1,0:T(1,128)}, u32[]{:S(2)}, u32[]{:S(2)}) collective-permute-start(f32[81,1,514]{2,1,0:T(1,128)} %get-tuple-element.124), channel_id=1, source_target_pairs={{1,0},{2,1},{3,2},{4,3},{5,4},{6,5},{7,6},{9,8},{10,9},{11,10},{12... | collective-permute-start | bytes 499616 | tf_op jit(solution)/shard_map/ppermute | solution.py:38
  114.9 15.3 %collective-permute-start.3 = (f32[81,1,514]{2,1,0:T(1,128)}, f32[81,1,514]{2,1,0:T(1,128)}, u32[]{:S(2)}, u32[]{:S(2)}) collective-permute-start(f32[81,1,514]{2,1,0:T(1,128)} %collective-permute-done.2), channel_id=1, source_target_pairs={{0,16},{16,0},{8,24},{24,8},{1,17},{17,1},{9,25},{25,9},{2,18},{18... | collective-permute-start | bytes 499616 | tf_op jit(solution)/shard_map/ppermute | solution.py:25
  116.5 212.5 %copy-start.19 = (f32[1,16,512]{2,1,0:T(8,128)}, f32[1,16,512]{2,1,0:T(8,128)S(1)}, u32[]{:S(2)}) copy-start(f32[1,16,512]{2,1,0:T(8,128)S(1)} %get-tuple-element.236) | copy-start | bytes 98308
  128.2 13.4 %copy-start.103 = (f32[16]{0:T(128)}, f32[16]{0:T(128)S(1)}, u32[]{:S(2)}) copy-start(f32[16]{0:T(128)S(1)} %fusion.68) | copy-start | bytes 196
  128.2 7.7 %collective-permute-start.5 = (f32[81,1,514]{2,1,0:T(1,128)}, f32[81,1,514]{2,1,0:T(1,128)}, u32[]{:S(2)}, u32[]{:S(2)}) collective-permute-start(f32[81,1,514]{2,1,0:T(1,128)} %copy-done.60), channel_id=1, source_target_pairs={{0,1},{1,2},{2,3},{3,4},{4,5},{5,6},{6,7},{8,9},{9,10},{10,11},{11... | collective-permute-start | bytes 499616 | tf_op jit(solution)/shard_map/ppermute | solution.py:36
  136.9 4.8 copy-start.16
  136.9 4.8 copy-start.18
  146.7 66.6 %copy-start.31 = (f32[1,16,512]{2,1,0:T(8,128)S(1)}, f32[1,16,512]{2,1,0:T(8,128)}, u32[]{:S(2)}) copy-start(f32[1,16,512]{2,1,0:T(8,128)} %copy-done.30) | copy-start | bytes 98308
  146.7 68.6 %copy-start.29 = (f32[1,16,512]{2,1,0:T(8,128)S(1)}, f32[1,16,512]{2,1,0:T(8,128)}, u32[]{:S(2)}) copy-start(f32[1,16,512]{2,1,0:T(8,128)} %copy-done.28) | copy-start | bytes 98308
  148.1 166.2 %collective-permute-start.6 = (f32[81,16,1]{0,1,2:T(8,128)S(1)}, f32[81,16,1]{0,1,2:T(8,128)}, u32[]{:S(2)}, u32[]{:S(2)}) collective-permute-start(f32[81,16,1]{0,1,2:T(8,128)S(1)} %copy.190), channel_id=1, source_target_pairs={{8,0},{16,8},{24,16},{0,24},{9,1},{17,9},{25,17},{1,25},{10,2},{18... | collective-permute-start | bytes 15560 | tf_op jit(solution)/shard_map/ppermute | solution.py:38
  150.5 164.9 %collective-permute-start.7 = (f32[81,16,1]{0,1,2:T(8,128)}, f32[81,16,1]{0,1,2:T(8,128)}, u32[]{:S(2)}, u32[]{:S(2)}) collective-permute-start(f32[81,16,1]{0,1,2:T(8,128)} %copy.192), channel_id=1, source_target_pairs={{0,8},{8,16},{16,24},{24,0},{1,9},{9,17},{17,25},{25,1},{2,10},{10... | collective-permute-start | bytes 15560 | tf_op jit(solution)/shard_map/ppermute | solution.py:36
  315.4 5.7 copy-start.56
  317.3 11.7 %copy-start = (f32[81,16,1]{2,1,0:T(8,128)S(1)}, f32[81,16,1]{2,1,0:T(8,128)}, u32[]{:S(2)}) copy-start(f32[81,16,1]{2,1,0:T(8,128)} %copy.193) | copy-start | bytes 15556
  320.3 8.1 %collective-permute-start.8 = (f32[81,1,514]{2,1,0:T(1,128)}, f32[81,1,514]{2,1,0:T(1,128)S(1)}, u32[]{:S(2)}, u32[]{:S(2)}) collective-permute-start(f32[81,1,514]{2,1,0:T(1,128)} %get-tuple-element.121), channel_id=1, source_target_pairs={{0,8},{8,0},{16,24},{24,16},{1,9},{9,1},{17,25},{25,17},{2,10},{10... | collective-permute-start | bytes 499616 | tf_op jit(solution)/shard_map/ppermute | solution.py:25
  321.7 20.0 %collective-permute-start.11 = (f32[81,1,514]{2,1,0:T(1,128)}, f32[81,1,514]{2,1,0:T(1,128)}, u32[]{:S(2)}, u32[]{:S(2)}) collective-permute-start(f32[81,1,514]{2,1,0:T(1,128)} %get-tuple-element.121), channel_id=1, source_target_pairs={{0,1},{1,2},{2,3},{3,4},{4,5},{5,6},{6,7},{8,9},{9,10},{10,11},{11... | collective-permute-start | bytes 499616 | tf_op jit(solution)/shard_map/ppermute | solution.py:36
  325.8 14.3 %collective-permute-start.10 = (f32[81,1,514]{2,1,0:T(1,128)}, f32[81,1,514]{2,1,0:T(1,128)}, u32[]{:S(2)}, u32[]{:S(2)}) collective-permute-start(f32[81,1,514]{2,1,0:T(1,128)} %get-tuple-element.122), channel_id=1, source_target_pairs={{1,0},{2,1},{3,2},{4,3},{5,4},{6,5},{7,6},{9,8},{10,9},{11,10},{12... | collective-permute-start | bytes 499616 | tf_op jit(solution)/shard_map/ppermute | solution.py:38
  328.4 7.8 %collective-permute-start.9 = (f32[81,1,514]{2,1,0:T(1,128)S(1)}, f32[81,1,514]{2,1,0:T(1,128)}, u32[]{:S(2)}, u32[]{:S(2)}) collective-permute-start(f32[81,1,514]{2,1,0:T(1,128)S(1)} %collective-permute-done.8), channel_id=1, source_target_pairs={{0,16},{16,0},{8,24},{24,8},{1,17},{17,1},{9,25},{25,9},{2,18},{18... | collective-permute-start | bytes 499616 | tf_op jit(solution)/shard_map/ppermute | solution.py:25
  481.2 26.6 %copy-start.22 = (f32[1,16,512]{2,1,0:T(8,128)S(1)}, f32[1,16,512]{2,1,0:T(8,128)}, u32[]{:S(2)}) copy-start(f32[1,16,512]{2,1,0:T(8,128)} %copy-done.21) | copy-start | bytes 98308
  481.2 26.6 %copy-start.25 = (f32[16,512]{1,0:T(8,128)S(1)}, f32[16,512]{1,0:T(8,128)}, u32[]{:S(2)}) copy-start(f32[16,512]{1,0:T(8,128)} %get-tuple-element.232) | copy-start | bytes 98308
  576.9 5.5 copy-start.101
  576.9 10.1 %copy-start.8 = (f32[4,20,16,512]{3,2,1,0:T(8,128)S(1)}, f32[4,20,16,512]{3,2,1,0:T(8,128)}, u32[]{:S(2)}) copy-start(f32[4,20,16,512]{3,2,1,0:T(8,128)} %copy-done.7) | copy-start | bytes 7864324
  583.1 13.6 %all-to-all-start.1 = ((f32[4,32,512]{2,0,1:T(4,128)}), f32[4,32,512]{2,0,1:T(4,128)S(1)}, u32[]{:S(2)}, u32[]{:S(2)}) async-start(f32[4,32,512]{2,0,1:T(4,128)} %broadcast_select_fusion.2), calls=%async_computation.1 | async-start | bytes 524288 | tf_op jit(solution)/shard_map/all_to_all | solution.py:202
  586.9 9.8 %copy-start.24 = (f32[1,32,512]{2,1,0:T(8,128)S(1)}, f32[1,32,512]{2,1,0:T(8,128)}, u32[]{:S(2)}) copy-start(f32[1,32,512]{2,1,0:T(8,128)} %param.14) | copy-start | bytes 196612
  (70 other events, 150.0 us)
where the time goes:
time: 718 us; the launch traced here: 708 us
  other arithmetic  405 us (56%)
  local copies, waits for them, and re-layouts  253 us (35%)
  starting transfers between devices  29.2 us (4%)
  waiting for transfers between devices  18.8 us (3%)
    scatter-add x1, other arithmetic, per_device(): ocean_flux = jnp.zeros((field_count, block_rows * block_cols), jnp.float3...  109 us
    unnamed x304, local copies, waits for them, and re-layouts  101 us
    scatter-add x1, other arithmetic, per_device(): gathered_sum = jnp.zeros((4, atm_cells), jnp.float32).at[:, slot_cells.re...  98.7 us
    scatter-add x1, other arithmetic, per_device(): weight_total = jnp.zeros((atm_cells,), jnp.float32).at[slot_cells.reshape...  96.9 us
    gather x2, local copies, waits for them, and re-layouts, per_device(): jnp.take(atm_flux, slot_cells.reshape(-1), axis=1)  62.7 us
    gather x2, local copies, waits for them, and re-layouts, per_device(): jnp.take(surface, arrival_cells.reshape(-1), axis=1)  62.4 us
    mul x1, other arithmetic, surface_forcing(): heat_gain * heat_flux  24.1 us
    sub x2, other arithmetic, tendency(): laplace = diff_east - diff_west + diff_north - diff_south  20.8 us
  transfers between devices with their start and end apart: 14, of which 4 were waited for; matrix products, arithmetic and copies ran while one was open for 45% of the time, Pallas kernels for 0%

commit v1 on v0

--- a/solution.py
+++ b/solution.py
@@ -1,9 +1,236 @@
 import jax
 import jax.numpy as jnp
 from jax import lax
+from jax.experimental import pallas as pl
+from jax.experimental.pallas import tpu as pltpu
 from jax.sharding import PartitionSpec as P
 
 STEPS = 2
+
+
+LANES = 256
+TERMS = 3
+GROUP = 8
+
+
+def cut(values):
+    terms = []
+    rest = values
+    for term_index in range(TERMS):
+        term = rest.astype(jnp.bfloat16)
+        terms.append(term)
+        if term_index < TERMS - 1:
+            rest = rest - term.astype(jnp.float32)
+    return terms
+
+
+def one_hot(positions, count):
+    slots = positions.shape[1]
+    base = positions - lax.broadcasted_iota(jnp.int32, (8, slots), 0)
+    rows = [jnp.where(base == 8 * j, 1.0, 0.0) for j in range(count // 8)]
+    return jnp.concatenate(rows, 0).astype(jnp.bfloat16)
+
+
+def each_owner(owners, body):
+    def outer(group, carry):
+        body(group)
+        return carry
+
+    lax.fori_loop(0, owners // GROUP, outer, 0)
+
+
+def send_kernel(flux_ref, cell_ref, weight_ref, out_ref, raw_ref, table_ref):
+    owners, slots = cell_ref.shape
+    blocks = flux_ref.shape[1] // LANES
+    raw_ref[...] = jnp.zeros_like(raw_ref)
+    for block in range(blocks):
+        x = flux_ref[:, block * LANES : (block + 1) * LANES]
+        heat = heat_gain * (x[0:1] + x[1:2] + x[2:3] + x[3:4])
+        water = water_gain * (x[4:5] - x[5:6])
+        raw_ref[4 * block : 4 * block + 4, :] = jnp.concatenate(
+            [heat, water, stress_gain * x[6:8]], 0
+        )
+    rows = raw_ref.shape[0]
+    for term_index, term in enumerate(cut(raw_ref[...])):
+        table_ref[term_index * rows : (term_index + 1) * rows, :] = term
+
+    def body(group):
+        first = pl.multiple_of(group * GROUP, GROUP)
+        cells = cell_ref[pl.ds(first, GROUP), :]
+        weights = weight_ref[pl.ds(first, GROUP), :]
+        for k in range(GROUP):
+            cell = cells[k : k + 1]
+            found = jnp.dot(
+                table_ref[...],
+                one_hot(cell & (LANES - 1), LANES),
+                preferred_element_type=jnp.float32,
+            )
+            base = cell // LANES - lax.broadcasted_iota(jnp.int32, (8, slots), 0) // 4
+            total = jnp.zeros((8, slots), jnp.float32)
+            for j in range(rows // 8):
+                value = found[8 * j : 8 * j + 8]
+                for t in range(1, TERMS):
+                    value = value + found[t * rows + 8 * j : t * rows + 8 * j + 8]
+                total = total + jnp.where(base == 2 * j, value, 0.0)
+            out_ref[first + k] = (total[0:4] + total[4:8]) * weights[k : k + 1]
+
+    each_owner(owners, body)
+
+
+def collect_kernel(come_ref, cell_ref, out_ref, sum_ref):
+    owners, slots = cell_ref.shape
+    rows, cols = out_ref.shape[1:]
+    high = rows * cols // LANES
+    sum_ref[...] = jnp.zeros_like(sum_ref)
+
+    def body(group):
+        first = pl.multiple_of(group * GROUP, GROUP)
+        cells = cell_ref[pl.ds(first, GROUP), :]
+        for k in range(GROUP):
+            cell = cells[k : k + 1]
+            col = cell % cols
+            spot = (col // LANES) * rows + cell // cols
+            mask = lax.broadcasted_iota(jnp.int32, (high, slots), 0) == spot
+            left = []
+            for term in cut(come_ref[first + k]):
+                wide = term.astype(jnp.float32)
+                for f in range(4):
+                    left.append(jnp.where(mask, wide[f : f + 1], 0.0))
+            sum_ref[...] += lax.dot_general(
+                jnp.concatenate(left, 0).astype(jnp.bfloat16),
+                one_hot(col % LANES, LANES),
+                (((1,), (1,)), ((), ())),
+                preferred_element_type=jnp.float32,
+            )
+
+    each_owner(owners, body)
+    for f in range(4):
+        for b in range(cols // LANES):
+            value = 0.0
+            for t in reversed(range(TERMS)):
+                at = (t * 4 + f) * high + b * rows
+                value = value + sum_ref[at : at + rows, :]
+            out_ref[f, :, b * LANES : (b + 1) * LANES] = value
+
+
+def surface_kernel(surface_ref, cell_ref, out_ref, table_ref):
+    owners, slots = cell_ref.shape
+    rows, cols = surface_ref.shape[1:]
+    high = rows * cols // LANES
+    for f in range(4):
+        for b in range(cols // LANES):
+            part = surface_ref[f, :, b * LANES : (b + 1) * LANES]
+            for t, term in enumerate(cut(part)):
+                at = (t * 4 + f) * high + b * rows
+                table_ref[at : at + rows, :] = term
+
+    def body(group):
+        first = pl.multiple_of(group * GROUP, GROUP)
+        cells = cell_ref[pl.ds(first, GROUP), :]
+        for k in range(GROUP):
+            cell = cells[k : k + 1]
+            col = cell % cols
+            spot = (col // LANES) * rows + cell // cols
+            found = jnp.dot(
+                table_ref[...],
+                one_hot(col % LANES, LANES),
+                preferred_element_type=jnp.float32,
+            )
+            base = spot - lax.broadcasted_iota(jnp.int32, (8, slots), 0)
+            masks = [base == 8 * j for j in range(high // 8)]
+            picked = []
+            for f in range(4):
+                total = jnp.zeros((8, slots), jnp.float32)
+                for j in range(high // 8):
+                    at = f * high + 8 * j
+                    value = found[at : at + 8]
+                    for t in range(1, TERMS):
+                        value = value + found[t * 4 * high + at : t * 4 * high + at + 8]
+                    total = total + jnp.where(masks[j], value, 0.0)
+                picked.append(jnp.sum(total, axis=0, keepdims=True))
+            out_ref[first + k] = jnp.concatenate(picked, 0)
+
+    each_owner(owners, body)
+
+
+def weight_kernel(cell_ref, weight_ref, out_ref, sum_ref):
+    owners, slots = cell_ref.shape
+    high = sum_ref.shape[0] // TERMS
+    sum_ref[...] = jnp.zeros_like(sum_ref)
+
+    def body(group):
+        first = pl.multiple_of(group * GROUP, GROUP)
+        cells = cell_ref[pl.ds(first, GROUP), :]
+        weights = weight_ref[pl.ds(first, GROUP), :]
+        for k in range(GROUP):
+            cell = cells[k : k + 1]
+            mask = lax.broadcasted_iota(jnp.int32, (high, slots), 0) == cell // LANES
+            left = [
+                jnp.where(mask, term.astype(jnp.float32), 0.0)
+                for term in cut(weights[k : k + 1])
+            ]
+            sum_ref[...] += lax.dot_general(
+                jnp.concatenate(left, 0).astype(jnp.bfloat16),
+                one_hot(cell & (LANES - 1), LANES),
+                (((1,), (1,)), ((), ())),
+                preferred_element_type=jnp.float32,
+            )
+
+    each_owner(owners, body)
+    value = 0.0
+    for t in reversed(range(TERMS)):
+        value = value + sum_ref[t * high : (t + 1) * high, :]
+    out_ref[...] = 1.0 / jnp.maximum(value, 1.0)
+
+
+def return_kernel(come_ref, cell_ref, weight_ref, inverse_ref, out_ref, sum_ref):
+    owners, slots = cell_ref.shape
+    blocks = out_ref.shape[1] // LANES
+    rows = sum_ref.shape[0] // TERMS
+    sum_ref[...] = jnp.zeros_like(sum_ref)
+
+    def body(group):
+        first = pl.multiple_of(group * GROUP, GROUP)
+        cells = cell_ref[pl.ds(first, GROUP), :]
+        weights = weight_ref[pl.ds(first, GROUP), :]
+        for k in range(GROUP):
+            cell = cells[k : k + 1]
+            base = cell // LANES - lax.broadcasted_iota(jnp.int32, (8, slots), 0) // 4
+            left = []
+            for term in cut(come_ref[first + k] * weights[k : k + 1]):
+                wide = term.astype(jnp.float32)
+                wide = jnp.concatenate([wide, wide], 0)
+                for j in range(rows // 8):
+                    left.append(jnp.where(base == 2 * j, wide, 0.0))
+            sum_ref[...] += lax.dot_general(
+                jnp.concatenate(left, 0).astype(jnp.bfloat16),
+                one_hot(cell & (LANES - 1), LANES),
+                (((1,), (1,)), ((), ())),
+                preferred_element_type=jnp.float32,
+            )
+
+    each_owner(owners, body)
+    for block in range(blocks):
+        value = 0.0
+        for t in reversed(range(TERMS)):
+            at = t * rows + 4 * block
+            value = value + sum_ref[at : at + 4, :]
+        out_ref[:, block * LANES : (block + 1) * LANES] = (
+            value * inverse_ref[block : block + 1, :]
+        )
+
+
+def up_to(count, step):
+    return (count + step - 1) // step * step
+
+
+def call(kernel, out_shape, scratch, *operands):
+    return pl.pallas_call(
+        kernel,
+        out_shape=jax.ShapeDtypeStruct(out_shape, jnp.float32),
+        scratch_shapes=[pltpu.VMEM(shape, dtype) for shape, dtype in scratch],
+        compiler_params=pltpu.CompilerParams(vmem_limit_bytes=40 * 2**20),
+    )(*operands)
 
 
 courant_scale = 0.05
@@ -94,19 +321,6 @@
     )
     return jnp.concatenate(
         [tracers.reshape((2 * levels,) + plane_shape), east_next, north_next, centre[-1:]], 0
-    )
-
-
-def surface_forcing(flux):
-    heat_flux = flux[0] + flux[1] + flux[2] + flux[3]
-    water_flux = flux[4] - flux[5]
-    return jnp.stack(
-        [
-            heat_gain * heat_flux,
-            water_gain * water_flux,
-            stress_gain * flux[6],
-            stress_gain * flux[7],
-        ]
     )
 
 
@@ -176,17 +390,31 @@
     arrival_cells = recv_cell[0]
     owners, capacity = slot_cells.shape
     atm_cells = atm_flux.shape[1]
-    field_count = atm_flux.shape[0]
-    outgoing = (
-        jnp.take(atm_flux, slot_cells.reshape(-1), axis=1).reshape(field_count, owners, capacity)
-        * slot_weights[None]
-    )
-    incoming = lax.all_to_all(outgoing, ("atm", "ocn"), split_axis=1, concat_axis=1, tiled=True)
-    ocean_flux = (
-        jnp.zeros((field_count, block_rows * block_cols), jnp.float32)
-        .at[:, arrival_cells.reshape(-1)]
-        .add(incoming.reshape(field_count, -1))
-        .reshape(field_count, block_rows, block_cols)
+    blocks = atm_cells // LANES
+    rows = up_to(4 * blocks, 16)
+    high = block_rows * block_cols // LANES
+    outgoing = call(
+        send_kernel,
+        (owners, 4, capacity),
+        [((rows, LANES), jnp.float32), ((TERMS * rows, LANES), jnp.bfloat16)],
+        atm_flux,
+        slot_cells,
+        slot_weights,
+    )
+    incoming = lax.all_to_all(outgoing, ("atm", "ocn"), split_axis=0, concat_axis=0, tiled=True)
+    inverse = call(
+        weight_kernel,
+        (up_to(blocks, 16), LANES),
+        [((TERMS * up_to(blocks, 16), LANES), jnp.float32)],
+        slot_cells,
+        slot_weights,
+    )
+    push = call(
+        collect_kernel,
+        (4, block_rows, block_cols),
+        [((TERMS * 4 * high, LANES), jnp.float32)],
+        incoming,
+        arrival_cells,
     )
     wet_cells = wet_mask.astype(jnp.float32)
     state_stack = jnp.concatenate([temp, salt, uvel, vvel, wet_cells[None]], 0)
@@ -194,24 +422,25 @@
     for step_index in range(STEPS):
         state_stack = advance(extend(state_stack, 1, fold_sign), 0, levels, block_rows)
     fields = state_stack[: 4 * levels].reshape(4, levels, block_rows, block_cols)
-    surface_push = surface_forcing(ocean_flux) * wet_cells
-    fields = fields.at[:, 0].add(surface_push)
+    fields = fields.at[:, 0].add(push * wet_cells)
     fields = vertical_solve(fields, vert_mix)
-    surface = fields[:, 0].reshape(4, block_rows * block_cols)
-    leaving = jnp.take(surface, arrival_cells.reshape(-1), axis=1).reshape(4, owners, capacity)
-    returning = lax.all_to_all(leaving, ("atm", "ocn"), split_axis=1, concat_axis=1, tiled=True)
-    weighted = returning * slot_weights[None]
-    gathered_sum = (
-        jnp.zeros((4, atm_cells), jnp.float32)
-        .at[:, slot_cells.reshape(-1)]
-        .add(weighted.reshape(4, -1))
-    )
-    weight_total = (
-        jnp.zeros((atm_cells,), jnp.float32)
-        .at[slot_cells.reshape(-1)]
-        .add(slot_weights.reshape(-1))
-    )
-    atm_surface = gathered_sum / jnp.maximum(weight_total, 1.0)
+    leaving = call(
+        surface_kernel,
+        (owners, 4, capacity),
+        [((TERMS * 4 * high, LANES), jnp.bfloat16)],
+        fields[:, 0],
+        arrival_cells,
+    )
+    returning = lax.all_to_all(leaving, ("atm", "ocn"), split_axis=0, concat_axis=0, tiled=True)
+    atm_surface = call(
+        return_kernel,
+        (4, atm_cells),
+        [((TERMS * rows, LANES), jnp.float32)],
+        returning,
+        slot_cells,
+        slot_weights,
+        inverse,
+    )
     return (fields[0], fields[1], fields[2], fields[3], atm_surface)
 
 

time: 718 us -> 180 us (0.25)
  other arithmetic: 405 us -> 75.5 us
  local copies, waits for them, and re-layouts: 253 us -> 34.7 us
  Pallas kernels: 0 us -> 20.9 us
  waiting for transfers between devices: 18.8 us -> 11.3 us
    scatter-add x3 -> x0, other arithmetic: 305 us -> none  [the longest x1 109 us: per_device(): ocean_flux = jnp.zeros((field_count, block_rows * block_cols), jnp.float3...]
    gather x4 -> x0, local copies, waits for them, and re-layouts: 125 us -> none  [the longest x2 62.7 us: per_device(): jnp.take(atm_flux, slot_cells.reshape(-1), axis=1)]
    unnamed x304 -> x185, local copies, waits for them, and re-layouts: 101 us -> 19.7 us
    pallas_call x0 -> x5, Pallas kernels: none -> 20.9 us  [call(): pl.pallas_call(kernel, out_shape=jax.ShapeDtypeStruct(out_shape, jnp.floa...]
    mul x3 -> x9, other arithmetic: 26.1 us -> 13.3 us  [vertical_solve(): solved.append(partial_rows[level_index] - factors[level_index] * solved[-1])]
    reshape x2 -> x0, local copies, waits for them, and re-layouts: 10.9 us -> none  [the longest x1 5.73 us: per_device(): incoming.reshape(field_count, -1)]
    unnamed x32 -> x10, other arithmetic: 17.7 us -> 8.53 us
  transfers between devices with their start and end apart: 14 -> 14, of which waited for: 4 -> 5; matrix products, arithmetic and copies ran while one was open for 45% -> 33% of each run, Pallas kernels for 0% -> 7%
where the time goes in v1:
time: 180 us; the launch traced here: 178 us
  other arithmetic  75.5 us (42%)
  local copies, waits for them, and re-layouts  34.7 us (19%)
  starting transfers between devices  33.5 us (19%)
  Pallas kernels  20.9 us (12%)
  waiting for transfers between devices  11.3 us (6%)
    pallas_call x5, Pallas kernels, call(): pl.pallas_call(kernel, out_shape=jax.ShapeDtypeStruct(out_shape, jnp.floa...  20.9 us
    sub x2, other arithmetic, tendency(): laplace = diff_east - diff_west + diff_north - diff_south  20.7 us
    unnamed x185, local copies, waits for them, and re-layouts  19.7 us
    mul x9, other arithmetic, vertical_solve(): solved.append(partial_rows[level_index] - factors[level_index] * solved[-1])  13.3 us
    ppermute x4, starting transfers between devices, padded(): lax.ppermute(head, axis, [((i + 1) % count, i) for i in range(ends)])  8.95 us
    unnamed x10, other arithmetic  8.53 us
    all_to_all x1, starting transfers between devices, per_device(): lax.all_to_all(leaving, ('atm', 'ocn'), split_axis=0, concat_axis=0, tile...  7.88 us
    ppermute x4, starting transfers between devices, partner(): return lax.ppermute(block, axis, route)  6.92 us
  transfers between devices with their start and end apart: 14, of which 5 were waited for; matrix products, arithmetic and copies ran while one was open for 33% of the time, Pallas kernels for 7%

profile of v1, /device:TPU:0, one launch (start us, length us, event | category | flops | bytes accessed | tf_op | source)
XLA Modules:
  0.0 177.6 jit_solution(4005175452328081102)
XLA Ops:
  5.9 1.4 copy-done.10
  8.7 1.4 copy.35
  10.1 3.9 %collective-permute-start = (f32[81,16,1]{0,1,2:T(8,128)S(1)}, f32[81,16,1]{0,1,2:T(8,128)S(1)}, u32[]{:S(2)}, u32[]{:S(2)}) collective-permute-start(f32[81,16,1]{0,1,2:T(8,128)S(1)} %copy.35), channel_id=1, source_target_pairs={{8,0},{16,8},{24,16},{0,24},{9,1},{17,9},{25,17},{1,25},{10,2},{18... | collective-permute-start | bytes 15560 | tf_op jit(solution)/shard_map/ppermute | solution.py:265
  14.0 1.4 copy.37
  15.4 4.4 %shard_map.137 = f32[32,4,512]{2,1,0:T(4,128)} custom-call(f32[8,6912]{1,0:T(8,128)S(1)} %copy-done.3, s32[32,512]{1,0:T(8,128)S(1)} %bitcast.468, f32[32,512]{1,0:T(8,128)S(1)} %bitcast.471), custom_call_target="tpu_custom_call" | custom-call | tf_op jit(solution)/shard_map/pallas_call | solution.py:228
  19.8 6.3 %all-to-all-start = ((f32[32,4,512]{2,1,0:T(4,128)}), f32[32,4,512]{2,1,0:T(4,128)S(1)}, u32[]{:S(2)}, u32[]{:S(2)}) async-start(f32[32,4,512]{2,1,0:T(4,128)} %shard_map.137), calls=%async_computation | async-start | bytes 524288 | tf_op jit(solution)/shard_map/all_to_all | solution.py:404
  26.1 1.4 fusion.102
  27.6 1.4 fusion.104
  29.0 1.4 fusion.106
  30.5 1.4 fusion.108
  31.9 1.7 fusion.110
  33.7 1.5 fusion.112
  35.2 1.4 fusion.114
  36.6 1.4 fusion.116
  40.5 3.1 %pad_maximum_fusion.42 = (f32[81,1,514]{2,1,0:T(1,128)S(1)}, f32[81,1,514]{2,1,0:T(1,128)}) fusion(f32[81,16,1]{2,1,0:T(8,128)} %copy.36, f32[81,16,512]{2,1,0:T(8,128)S(1)} %constant_dynamic-update-slice_fusion, f32[81,16,1]{2,1,0:T(8,128)} %copy.38), kind=kLoop, calls=%fused_computation.112 | loop fusion | flops 166536 | bytes 2997648 | tf_op jit(solution)/shard_map/slice | solution.py:260
  43.6 1.8 %collective-permute-start.2 = (f32[81,1,514]{2,1,0:T(1,128)S(1)}, f32[81,1,514]{2,1,0:T(1,128)}, u32[]{:S(2)}, u32[]{:S(2)}) collective-permute-start(f32[81,1,514]{2,1,0:T(1,128)S(1)} %get-tuple-element.85), channel_id=1, source_target_pairs={{0,8},{8,0},{16,24},{24,16},{1,9},{9,1},{17,25},{25,17},{2,10},{10... | collective-permute-start | bytes 499616 | tf_op jit(solution)/shard_map/ppermute | solution.py:252
  45.5 1.4 add_bitcast_fusion
  48.2 2.9 %collective-permute-done.2 = f32[81,1,514]{2,1,0:T(1,128)} collective-permute-done((f32[81,1,514]{2,1,0:T(1,128)S(1)}, f32[81,1,514]{2,1,0:T(1,128)}, u32[]{:S(2)}, u32[]{:S(2)}) %collective-permute-start.2) | collective-permute-done | bytes 166568 | tf_op jit(solution)/shard_map/ppermute | solution.py:252
  51.1 1.7 collective-permute-start.3
  53.3 2.0 %collective-permute-start.5 = (f32[81,1,514]{2,1,0:T(1,128)}, f32[81,1,514]{2,1,0:T(1,128)}, u32[]{:S(2)}, u32[]{:S(2)}) collective-permute-start(f32[81,1,514]{2,1,0:T(1,128)} %copy-done.81), channel_id=1, source_target_pairs={{0,1},{1,2},{2,3},{3,4},{4,5},{5,6},{6,7},{8,9},{9,10},{10,11},{11... | collective-permute-start | bytes 499616 | tf_op jit(solution)/shard_map/ppermute | solution.py:263
  55.3 2.5 %collective-permute-done.3 = f32[81,1,514]{2,1,0:T(1,128)S(1)} collective-permute-done((f32[81,1,514]{2,1,0:T(1,128)}, f32[81,1,514]{2,1,0:T(1,128)S(1)}, u32[]{:S(2)}, u32[]{:S(2)}) %collective-permute-start.3) | collective-permute-done | bytes 166568 | tf_op jit(solution)/shard_map/ppermute | solution.py:252
  58.5 3.3 %reverse = f32[81,1,640]{2,1,0:T(1,128)S(1)} reverse(f32[81,1,640]{2,1,0:T(1,128)} %bitcast.516), dimensions={1,2} | reverse | bytes 414720
  61.9 1.7 broadcast_select_fusion.1
  64.5 4.6 %add_subtract_fusion.1 = (f32[80,16,512]{2,1,0:T(8,128)S(1)}, f32[80,16,512]{2,1,0:T(8,128)S(1)}, f32[80,16,512]{2,1,0:T(8,128)S(1)}, f32[80,16,512]{2,1,0:T(8,128)S(1)}, f32[80,16,512]{2,1,0:T(8,128)S(1)}) fusion(f32[80,16,512]{2,1,0:T(8,128)S(1)} %copy-done.11, f32[81,16,512]{2,1,0:T(8,128)S(1)} %constant_dynamic-update-slice_fusion, ...), kind=kLoop, calls=%fused_computation.47 | loop fusion | flops 12451840 | bytes 18857360 | tf_op jit(solution)/shard_map/sub | solution.py:299
  69.3 2.8 %multiply_maximum_fusion.1 = (f32[20,16,512]{2,1,0:T(8,128)}, f32[20,16,512]{2,1,0:T(8,128)S(1)}, f32[20,16,512]{2,1,0:T(8,128)}, f32[20,16,512]{2,1,0:T(8,128)S(1)}) fusion(f32[20,16,512]{2,1,0:T(8,128)S(1)} %copy-done.19, f32[20,16,512]{2,1,0:T(8,128)} %param.19, f32[16]{0:T(128)S(1)} %copy-done.84, f32[80,16,512]{2,1,0:T(8,128)S(1)} %get-tuple-element.74, ...), kind=kLoop, calls=%fused_computation.97 | loop fusion | flops 2293760 | bytes 5275712 | tf_op jit(solution)/shard_map/max | solution.py:310
  72.1 1.4 fusion.25
  76.2 2.5 %collective-permute-start.6 = (f32[81,16,1]{0,1,2:T(8,128)S(1)}, f32[81,16,1]{0,1,2:T(8,128)S(1)}, u32[]{:S(2)}, u32[]{:S(2)}) collective-permute-start(f32[81,16,1]{0,1,2:T(8,128)S(1)} %copy.41), channel_id=1, source_target_pairs={{8,0},{16,8},{24,16},{0,24},{9,1},{17,9},{25,17},{1,25},{10,2},{18... | collective-permute-start | bytes 15560 | tf_op jit(solution)/shard_map/ppermute | solution.py:265
  78.7 1.4 copy.43
  80.3 1.7 add_bitcast_fusion.1
  82.0 3.1 %shard_map.140.inverse_ref = f32[32,256]{1,0:T(8,128)S(1)} custom-call(s32[32,512]{1,0:T(8,128)S(1)} %bitcast.469, f32[32,512]{1,0:T(8,128)S(1)} %bitcast.472), custom_call_target="tpu_custom_call" | custom-call | tf_op jit(solution)/shard_map/pallas_call | solution.py:228
  87.6 3.2 %pad_maximum_fusion.39 = (f32[81,1,514]{2,1,0:T(1,128)}, f32[81,1,514]{2,1,0:T(1,128)}) fusion(f32[81,16,1]{2,1,0:T(8,128)} %copy.42, f32[81,16,1]{2,1,0:T(8,128)} %copy.44, f32[1,16,512]{2,1,0:T(8,128)S(1)} %get-tuple-element.148, f32[20,16,512]{2,1,0:T(8,128)S(1)} %get-tuple-element.90, f32[20,16,512]{2,1,0:T(8,128)S(1)} %get-tuple-element.66, ...), kind=kLoop, calls=%fused_computation.109 | loop fusion | flops 416340 | bytes 2997648 | tf_op jit(solution)/shard_map/slice | solution.py:260
  90.8 2.0 %collective-permute-start.8 = (f32[81,1,514]{2,1,0:T(1,128)}, f32[81,1,514]{2,1,0:T(1,128)}, u32[]{:S(2)}, u32[]{:S(2)}) collective-permute-start(f32[81,1,514]{2,1,0:T(1,128)} %get-tuple-element.83), channel_id=1, source_target_pairs={{0,8},{8,0},{16,24},{24,16},{1,9},{9,1},{17,25},{25,17},{2,10},{10... | collective-permute-start | bytes 499616 | tf_op jit(solution)/shard_map/ppermute | solution.py:252
  92.8 1.4 fusion.118
  96.9 1.4 collective-permute-start.9
  99.0 4.2 %shard_map.138 = f32[4,16,512]{2,1,0:T(8,128)S(1)} custom-call(f32[32,4,512]{2,1,0:T(4,128)S(1)} %all-to-all-done.come_ref, s32[32,512]{1,0:T(8,128)S(1)} %bitcast.474), custom_call_target="tpu_custom_call" | custom-call | tf_op jit(solution)/shard_map/pallas_call | solution.py:228
  103.3 3.9 %reverse.1 = f32[81,1,640]{2,1,0:T(1,128)} reverse(f32[81,1,640]{2,1,0:T(1,128)} %bitcast.437), dimensions={1,2} | reverse | bytes 414720
  107.3 1.6 broadcast_select_fusion
  108.9 1.5 fusion.85
  110.4 16.0 %add_subtract_fusion = (f32[80,16,512]{2,1,0:T(8,128)}, f32[80,16,512]{2,1,0:T(8,128)}, f32[80,16,512]{2,1,0:T(8,128)}, f32[80,16,512]{2,1,0:T(8,128)}, f32[80,16,512]{2,1,0:T(8,128)}) fusion(f32[1,16,512]{2,1,0:T(8,128)S(1)} %get-tuple-element.148, f32[20,16,512]{2,1,0:T(8,128)S(1)} %get-tuple-element.90, f32[20,16,512]{2,1,0:T(8,128)S(1)} %get-tuple-element.66, ...), kind=kLoop, calls=%fused_computation.46 | loop fusion | flops 21626880 | bytes 16235920 | tf_op jit(solution)/shard_map/sub | solution.py:299
  126.4 1.9 %fusion.33 = (f32[20,16,512]{2,1,0:T(8,128)S(1)}, f32[20,16,512]{2,1,0:T(8,128)S(1)}, f32[20,16,512]{2,1,0:T(8,128)S(1)}, f32[20,16,512]{2,1,0:T(8,128)S(1)}) fusion(f32[20,16,512]{2,1,0:T(8,128)S(1)} %get-tuple-element.66, f32[80,16,512]{2,1,0:T(8,128)} %get-tuple-element.69, f32[20,16,512]{2,1,0:T(8,128)S(1)} %get-tuple-element.90, f32[16]{0:T(128)S(1)} %copy-done.85, ...), kind=kLoop, calls=%fused_computation.85 | loop fusion | flops 2293760 | bytes 5275712 | tf_op jit(solution)/shard_map/add | solution.py:316
  129.3 3.8 %fusion.19 = f32[40,16,512]{2,1,0:T(8,128)S(1)} fusion(f32[40,16,512]{2,1,0:T(8,128)S(1)} %fusion.25, f32[80,16,512]{2,1,0:T(8,128)} %get-tuple-element.72, f32[80,16,512]{2,1,0:T(8,128)} %get-tuple-element.73, f32[80,16,512]{2,1,0:T(8,128)} %get-tuple-element.71, f32[80,16,512]{2,1,0:T(8,128)S(1)} %copy-done.9, f32[80,16,512]{2,1,0:T(8,128)S(1)} %copy-done.8, ...), kind=kLoop, calls=%fused_computation.52 | loop fusion | flops 3604480 | bytes 11829248 | tf_op jit(solution)/shard_map/add | solution.py:315
  134.5 1.8 %multiply_subtract_fusion = (f32[4,16,512]{2,1,0:T(8,128)S(1)}, f32[4,1,16,512]{3,2,0,1:T(8,128)S(1)}) fusion(f32[4,20,16,512]{3,2,1,0:T(8,128)S(1)} %bitcast.476, f32[16,512]{1,0:T(8,128)S(1)} %copy-done.22, f32[16,512]{1,0:T(8,128)S(1)} %copy-done.23, f32[16,512]{1,0:T(8,128)S(1)} %copy-done.58, f32[16,512]{1,0:T(8,128)S(1)} %bitcast.500, ...), kind=kLoop, calls=%fused_computation.198 | loop fusion | flops 3211264 | bytes 4947968 | tf_op jit(solution)/shard_map/sub | solution.py:345
  136.3 2.5 %subtract_dynamic-update-slice_fusion = (f32[4,20,16,512]{3,2,0,1:T(8,128)}, f32[4,1,16,512]{3,2,0,1:T(8,128)S(1)}, f32[4,1,16,512]{3,2,0,1:T(8,128)S(1)}, f32[4...) fusion(f32[16,512]{1,0:T(8,128)} %get-tuple-element.147, ...), kind=kLoop, calls=%fused_computation.199 | loop fusion | flops 3145727 | bytes 7012352
  150.1 4.8 %shard_map.139 = f32[32,4,512]{2,1,0:T(4,128)} custom-call(f32[4,16,512]{2,1,0:T(8,128)S(1)} %get-tuple-element.17.surface_ref, s32[32,512]{1,0:T(8,128)S(1)} %bitcast.475), custom_call_target="tpu_custom_call" | custom-call | tf_op jit(solution)/shard_map/pallas_call | solution.py:228
  154.9 7.9 %all-to-all-start.1 = ((f32[32,4,512]{2,1,0:T(4,128)}), f32[32,4,512]{2,1,0:T(4,128)S(1)}, u32[]{:S(2)}, u32[]{:S(2)}) async-start(f32[32,4,512]{2,1,0:T(4,128)} %shard_map.139), calls=%async_computation.1 | async-start | bytes 524288 | tf_op jit(solution)/shard_map/all_to_all | solution.py:434
  164.2 3.3 %slice_bitcast_fusion = (f32[20,16,512]{2,1,0:T(8,128)}, f32[20,16,512]{2,1,0:T(8,128)}, f32[20,16,512]{2,1,0:T(8,128)}, f32[20,16,512]{2,1,0:T(8,128)}) fusion(f32[4,20,16,512]{3,2,0,1:T(8,128)} %constant_dynamic-update-slice_fusion.9), kind=kLoop, calls=%fused_computation.74 | loop fusion | bytes 5242880 | tf_op jit(solution)/shard_map/squeeze | solution.py:444
  167.5 5.7 %all-to-all-done.1.come_ref = f32[32,4,512]{2,1,0:T(4,128)S(1)} async-done(((f32[32,4,512]{2,1,0:T(4,128)}), f32[32,4,512]{2,1,0:T(4,128)S(1)}, u32[]{:S(2)}, u32[]{:S(2)}) %all-to-all-start.1) | async-done | bytes 262176 | tf_op jit(solution)/shard_map/all_to_all | solution.py:434
  173.2 4.4 %shard_map.141 = f32[4,6912]{1,0:T(4,128)} custom-call(f32[32,4,512]{2,1,0:T(4,128)S(1)} %all-to-all-done.1.come_ref, s32[32,512]{1,0:T(8,128)S(1)} %bitcast.470, f32[32,512]{1,0:T(8,128)S(1)} %bitcast.473, f32[32,256]{1,0:T(8,128)S(1)} %shard_map.140.inverse_ref), custom_call_target="tpu_custom_call" | custom-call | tf_op jit(solution)/shard_map/pallas_call | solution.py:228
  (223 shorter events, 36.1 us)
Async XLA Ops:
  5.8 9.5 %copy-start = (s32[1,32,512]{2,1,0:T(8,128)S(1)}, s32[1,32,512]{2,1,0:T(8,128)}, u32[]{:S(2)}) copy-start(s32[1,32,512]{2,1,0:T(8,128)} %param.13) | copy-start | bytes 196612
  5.9 9.5 %copy-start.1 = (f32[1,32,512]{2,1,0:T(8,128)S(1)}, f32[1,32,512]{2,1,0:T(8,128)}, u32[]{:S(2)}) copy-start(f32[1,32,512]{2,1,0:T(8,128)} %param.14) | copy-start | bytes 196612
  5.9 9.5 %copy-start.3 = (f32[8,6912]{1,0:T(8,128)S(1)}, f32[8,6912]{1,0:T(8,128)}, u32[]{:S(2)}) copy-start(f32[8,6912]{1,0:T(8,128)} %flux_ref.1) | copy-start | bytes 663556
  10.1 28.0 %collective-permute-start = (f32[81,16,1]{0,1,2:T(8,128)S(1)}, f32[81,16,1]{0,1,2:T(8,128)S(1)}, u32[]{:S(2)}, u32[]{:S(2)}) collective-permute-start(f32[81,16,1]{0,1,2:T(8,128)S(1)} %copy.35), channel_id=1, source_target_pairs={{8,0},{16,8},{24,16},{0,24},{9,1},{17,9},{25,17},{1,25},{10,2},{18... | collective-permute-start | bytes 15560 | tf_op jit(solution)/shard_map/ppermute | solution.py:265
  15.3 24.0 %collective-permute-start.1 = (f32[81,16,1]{0,1,2:T(8,128)S(1)}, f32[81,16,1]{0,1,2:T(8,128)S(1)}, u32[]{:S(2)}, u32[]{:S(2)}) collective-permute-start(f32[81,16,1]{0,1,2:T(8,128)S(1)} %copy.37), channel_id=1, source_target_pairs={{0,8},{8,16},{16,24},{24,0},{1,9},{9,17},{17,25},{25,1},{2,10},{10... | collective-permute-start | bytes 15560 | tf_op jit(solution)/shard_map/ppermute | solution.py:263
  19.8 79.2 %all-to-all-start = ((f32[32,4,512]{2,1,0:T(4,128)}), f32[32,4,512]{2,1,0:T(4,128)S(1)}, u32[]{:S(2)}, u32[]{:S(2)}) async-start(f32[32,4,512]{2,1,0:T(4,128)} %shard_map.137), calls=%async_computation | async-start | bytes 524288 | tf_op jit(solution)/shard_map/all_to_all | solution.py:404
  27.6 7.6 %copy-start.42 = (f32[1,16,512]{2,1,0:T(8,128)}, f32[1,16,512]{2,1,0:T(8,128)S(1)}, u32[]{:S(2)}) copy-start(f32[1,16,512]{2,1,0:T(8,128)S(1)} %get-tuple-element.40) | copy-start | bytes 98308
  29.0 14.5 %copy-start.24 = (f32[1,16,512]{2,1,0:T(8,128)}, f32[1,16,512]{2,1,0:T(8,128)S(1)}, u32[]{:S(2)}) copy-start(f32[1,16,512]{2,1,0:T(8,128)S(1)} %get-tuple-element.42) | copy-start | bytes 98308
  29.0 14.5 %copy-start.26 = (f32[1,16,512]{2,1,0:T(8,128)}, f32[1,16,512]{2,1,0:T(8,128)S(1)}, u32[]{:S(2)}) copy-start(f32[1,16,512]{2,1,0:T(8,128)S(1)} %get-tuple-element.43) | copy-start | bytes 98308
  30.5 13.1 %copy-start.28 = (f32[1,16,512]{2,1,0:T(8,128)}, f32[1,16,512]{2,1,0:T(8,128)S(1)}, u32[]{:S(2)}) copy-start(f32[1,16,512]{2,1,0:T(8,128)S(1)} %get-tuple-element.45) | copy-start | bytes 98308
  30.5 13.1 %copy-start.30 = (f32[1,16,512]{2,1,0:T(8,128)}, f32[1,16,512]{2,1,0:T(8,128)S(1)}, u32[]{:S(2)}) copy-start(f32[1,16,512]{2,1,0:T(8,128)S(1)} %get-tuple-element.46) | copy-start | bytes 98308
  31.9 11.7 %copy-start.32 = (f32[1,16,512]{2,1,0:T(8,128)}, f32[1,16,512]{2,1,0:T(8,128)S(1)}, u32[]{:S(2)}) copy-start(f32[1,16,512]{2,1,0:T(8,128)S(1)} %get-tuple-element.48) | copy-start | bytes 98308
  31.9 11.7 %copy-start.34 = (f32[1,16,512]{2,1,0:T(8,128)}, f32[1,16,512]{2,1,0:T(8,128)S(1)}, u32[]{:S(2)}) copy-start(f32[1,16,512]{2,1,0:T(8,128)S(1)} %get-tuple-element.49) | copy-start | bytes 98308
  33.7 3.0 %copy-start.52 = (f32[1,16,512]{2,1,0:T(8,128)}, f32[1,16,512]{2,1,0:T(8,128)S(1)}, u32[]{:S(2)}) copy-start(f32[1,16,512]{2,1,0:T(8,128)S(1)} %get-tuple-element.51) | copy-start | bytes 98308
  35.2 8.4 %copy-start.54 = (f32[1,16,512]{2,1,0:T(8,128)}, f32[1,16,512]{2,1,0:T(8,128)S(1)}, u32[]{:S(2)}) copy-start(f32[1,16,512]{2,1,0:T(8,128)S(1)} %get-tuple-element.54) | copy-start | bytes 98308
  36.6 7.0 %copy-start.36 = (f32[1,16,512]{2,1,0:T(8,128)}, f32[1,16,512]{2,1,0:T(8,128)S(1)}, u32[]{:S(2)}) copy-start(f32[1,16,512]{2,1,0:T(8,128)S(1)} %get-tuple-element.57) | copy-start | bytes 98308
  38.1 7.4 %copy-start.38 = (f32[1,16,512]{2,1,0:T(8,128)}, f32[1,16,512]{2,1,0:T(8,128)S(1)}, u32[]{:S(2)}) copy-start(f32[1,16,512]{2,1,0:T(8,128)S(1)} %get-tuple-element.60) | copy-start | bytes 98308
  40.5 21.4 %copy-start.83 = (f32[81]{0:T(128)S(1)}, f32[81]{0:T(128)}, u32[]{:S(2)}) copy-start(f32[81]{0:T(128)} %constant.48.clone.1) | copy-start | bytes 976
  43.6 7.5 %copy-start.81 = (f32[81,1,514]{2,1,0:T(1,128)}, f32[81,1,514]{2,1,0:T(1,128)S(1)}, u32[]{:S(2)}) copy-start(f32[81,1,514]{2,1,0:T(1,128)S(1)} %get-tuple-element.85) | copy-start | bytes 499612
  43.6 7.5 %collective-permute-start.2 = (f32[81,1,514]{2,1,0:T(1,128)S(1)}, f32[81,1,514]{2,1,0:T(1,128)}, u32[]{:S(2)}, u32[]{:S(2)}) collective-permute-start(f32[81,1,514]{2,1,0:T(1,128)S(1)} %get-tuple-element.85), channel_id=1, source_target_pairs={{0,8},{8,0},{16,24},{24,16},{1,9},{9,1},{17,25},{25,17},{2,10},{10... | collective-permute-start | bytes 499616 | tf_op jit(solution)/shard_map/ppermute | solution.py:252
  46.9 14.9 %collective-permute-start.4 = (f32[81,1,514]{2,1,0:T(1,128)}, f32[81,1,514]{2,1,0:T(1,128)}, u32[]{:S(2)}, u32[]{:S(2)}) collective-permute-start(f32[81,1,514]{2,1,0:T(1,128)} %get-tuple-element.86), channel_id=1, source_target_pairs={{1,0},{2,1},{3,2},{4,3},{5,4},{6,5},{7,6},{9,8},{10,9},{11,10},{12... | collective-permute-start | bytes 499616 | tf_op jit(solution)/shard_map/ppermute | solution.py:265
  51.1 6.7 %collective-permute-start.3 = (f32[81,1,514]{2,1,0:T(1,128)}, f32[81,1,514]{2,1,0:T(1,128)S(1)}, u32[]{:S(2)}, u32[]{:S(2)}) collective-permute-start(f32[81,1,514]{2,1,0:T(1,128)} %collective-permute-done.2), channel_id=1, source_target_pairs={{0,16},{16,0},{8,24},{24,8},{1,17},{17,1},{9,25},{25,9},{2,18},{18... | collective-permute-start | bytes 499616 | tf_op jit(solution)/shard_map/ppermute | solution.py:252
  53.3 10.2 %collective-permute-start.5 = (f32[81,1,514]{2,1,0:T(1,128)}, f32[81,1,514]{2,1,0:T(1,128)}, u32[]{:S(2)}, u32[]{:S(2)}) collective-permute-start(f32[81,1,514]{2,1,0:T(1,128)} %copy-done.81), channel_id=1, source_target_pairs={{0,1},{1,2},{2,3},{3,4},{4,5},{5,6},{6,7},{8,9},{9,10},{10,11},{11... | collective-permute-start | bytes 499616 | tf_op jit(solution)/shard_map/ppermute | solution.py:263
  64.5 4.7 %copy-start.19 = (f32[20,16,512]{2,1,0:T(8,128)S(1)}, f32[20,16,512]{2,1,0:T(8,128)}, u32[]{:S(2)}) copy-start(f32[20,16,512]{2,1,0:T(8,128)} %param.18) | copy-start | bytes 1966084
  64.5 4.7 %copy-start.84 = (f32[16]{0:T(128)S(1)}, f32[16]{0:T(128)}, u32[]{:S(2)}) copy-start(f32[16]{0:T(128)} %fusion.100) | copy-start | bytes 196
  69.2 2.8 %copy-start.12 = (f32[20,16,512]{2,1,0:T(8,128)S(1)}, f32[20,16,512]{2,1,0:T(8,128)}, u32[]{:S(2)}) copy-start(f32[20,16,512]{2,1,0:T(8,128)} %param.16) | copy-start | bytes 1966084
  69.2 2.8 %copy-start.13 = (f32[20,16,512]{2,1,0:T(8,128)S(1)}, f32[20,16,512]{2,1,0:T(8,128)}, u32[]{:S(2)}) copy-start(f32[20,16,512]{2,1,0:T(8,128)} %param.17) | copy-start | bytes 1966084
  69.2 2.8 %copy-start.14 = (f32[20,16,512]{2,1,0:T(8,128)S(1)}, f32[20,16,512]{2,1,0:T(8,128)}, u32[]{:S(2)}) copy-start(f32[20,16,512]{2,1,0:T(8,128)} %get-tuple-element.105) | copy-start | bytes 1966084
  69.2 2.8 %copy-start.15 = (f32[20,16,512]{2,1,0:T(8,128)S(1)}, f32[20,16,512]{2,1,0:T(8,128)}, u32[]{:S(2)}) copy-start(f32[20,16,512]{2,1,0:T(8,128)} %get-tuple-element.106) | copy-start | bytes 1966084
  73.5 6.8 %copy-start.59 = (f32[1,16,512]{2,1,0:T(8,128)S(1)}, f32[1,16,512]{2,1,0:T(8,128)}, u32[]{:S(2)}) copy-start(f32[1,16,512]{2,1,0:T(8,128)} %get-tuple-element.52) | copy-start | bytes 98308
  73.5 6.8 %copy-start.61 = (f32[1,16,512]{2,1,0:T(8,128)S(1)}, f32[1,16,512]{2,1,0:T(8,128)}, u32[]{:S(2)}) copy-start(f32[1,16,512]{2,1,0:T(8,128)} %get-tuple-element.58) | copy-start | bytes 98308
  73.5 6.8 %copy-start.63 = (f32[1,16,512]{2,1,0:T(8,128)S(1)}, f32[1,16,512]{2,1,0:T(8,128)}, u32[]{:S(2)}) copy-start(f32[1,16,512]{2,1,0:T(8,128)} %get-tuple-element.61) | copy-start | bytes 98308
  73.5 6.8 %copy-start.65 = (f32[1,16,512]{2,1,0:T(8,128)S(1)}, f32[1,16,512]{2,1,0:T(8,128)}, u32[]{:S(2)}) copy-start(f32[1,16,512]{2,1,0:T(8,128)} %get-tuple-element.64) | copy-start | bytes 98308
  73.5 6.8 %copy-start.67 = (f32[1,16,512]{2,1,0:T(8,128)S(1)}, f32[1,16,512]{2,1,0:T(8,128)}, u32[]{:S(2)}) copy-start(f32[1,16,512]{2,1,0:T(8,128)} %get-tuple-element.55) | copy-start | bytes 98308
  76.2 8.9 %collective-permute-start.6 = (f32[81,16,1]{0,1,2:T(8,128)S(1)}, f32[81,16,1]{0,1,2:T(8,128)S(1)}, u32[]{:S(2)}, u32[]{:S(2)}) collective-permute-start(f32[81,16,1]{0,1,2:T(8,128)S(1)} %copy.41), channel_id=1, source_target_pairs={{8,0},{16,8},{24,16},{0,24},{9,1},{17,9},{25,17},{1,25},{10,2},{18... | collective-permute-start | bytes 15560 | tf_op jit(solution)/shard_map/ppermute | solution.py:265
  80.0 6.3 %collective-permute-start.7 = (f32[81,16,1]{0,1,2:T(8,128)S(1)}, f32[81,16,1]{0,1,2:T(8,128)S(1)}, u32[]{:S(2)}, u32[]{:S(2)}) collective-permute-start(f32[81,16,1]{0,1,2:T(8,128)S(1)} %copy.43), channel_id=1, source_target_pairs={{0,8},{8,16},{16,24},{24,0},{1,9},{9,17},{17,25},{25,1},{2,10},{10... | collective-permute-start | bytes 15560 | tf_op jit(solution)/shard_map/ppermute | solution.py:263
  86.3 6.4 %copy-start.44 = (f32[1,16,512]{2,1,0:T(8,128)S(1)}, f32[1,16,512]{2,1,0:T(8,128)}, u32[]{:S(2)}) copy-start(f32[1,16,512]{2,1,0:T(8,128)} %get-tuple-element.63) | copy-start | bytes 98308
  87.5 10.8 %copy-start.4 = (f32[81,16,1]{2,1,0:T(8,128)S(1)}, f32[81,16,1]{2,1,0:T(8,128)}, u32[]{:S(2)}) copy-start(f32[81,16,1]{2,1,0:T(8,128)} %copy.42) | copy-start | bytes 15556
  87.6 10.8 %copy-start.5 = (f32[81,16,1]{2,1,0:T(8,128)S(1)}, f32[81,16,1]{2,1,0:T(8,128)}, u32[]{:S(2)}) copy-start(f32[81,16,1]{2,1,0:T(8,128)} %copy.44) | copy-start | bytes 15556
  90.8 8.3 %copy-start.2 = (s32[1,32,512]{2,1,0:T(8,128)S(1)}, s32[1,32,512]{2,1,0:T(8,128)}, u32[]{:S(2)}) copy-start(s32[1,32,512]{2,1,0:T(8,128)} %param.15) | copy-start | bytes 196612
  90.8 6.1 %collective-permute-start.8 = (f32[81,1,514]{2,1,0:T(1,128)}, f32[81,1,514]{2,1,0:T(1,128)}, u32[]{:S(2)}, u32[]{:S(2)}) collective-permute-start(f32[81,1,514]{2,1,0:T(1,128)} %get-tuple-element.83), channel_id=1, source_target_pairs={{0,8},{8,0},{16,24},{24,16},{1,9},{9,1},{17,25},{25,17},{2,10},{10... | collective-permute-start | bytes 499616 | tf_op jit(solution)/shard_map/ppermute | solution.py:252
  94.2 14.7 %collective-permute-start.11 = (f32[81,1,514]{2,1,0:T(1,128)}, f32[81,1,514]{2,1,0:T(1,128)S(1)}, u32[]{:S(2)}, u32[]{:S(2)}) collective-permute-start(f32[81,1,514]{2,1,0:T(1,128)} %get-tuple-element.83), channel_id=1, source_target_pairs={{0,1},{1,2},{2,3},{3,4},{4,5},{5,6},{6,7},{8,9},{9,10},{10,11},{11... | collective-permute-start | bytes 499616 | tf_op jit(solution)/shard_map/ppermute | solution.py:263
  95.5 11.8 %collective-permute-start.10 = (f32[81,1,514]{2,1,0:T(1,128)}, f32[81,1,514]{2,1,0:T(1,128)}, u32[]{:S(2)}, u32[]{:S(2)}) collective-permute-start(f32[81,1,514]{2,1,0:T(1,128)} %get-tuple-element.84), channel_id=1, source_target_pairs={{1,0},{2,1},{3,2},{4,3},{5,4},{6,5},{7,6},{9,8},{10,9},{11,10},{12... | collective-permute-start | bytes 499616 | tf_op jit(solution)/shard_map/ppermute | solution.py:265
  96.9 6.4 %collective-permute-start.9 = (f32[81,1,514]{2,1,0:T(1,128)}, f32[81,1,514]{2,1,0:T(1,128)}, u32[]{:S(2)}, u32[]{:S(2)}) collective-permute-start(f32[81,1,514]{2,1,0:T(1,128)} %collective-permute-done.8), channel_id=1, source_target_pairs={{0,16},{16,0},{8,24},{24,8},{1,17},{17,1},{9,25},{25,9},{2,18},{18... | collective-permute-start | bytes 499616 | tf_op jit(solution)/shard_map/ppermute | solution.py:252
  107.3 3.1 %copy-start.82 = (f32[16,512]{1,0:T(8,128)S(1)}, f32[16,512]{1,0:T(8,128)}, u32[]{:S(2)}) copy-start(f32[16,512]{1,0:T(8,128)} %get-tuple-element.93) | copy-start | bytes 98308
  110.4 16.0 %copy-start.85 = (f32[16]{0:T(128)S(1)}, f32[16]{0:T(128)}, u32[]{:S(2)}) copy-start(f32[16]{0:T(128)} %fusion.100) | copy-start | bytes 196
  126.4 2.9 %copy-start.9 = (f32[80,16,512]{2,1,0:T(8,128)S(1)}, f32[80,16,512]{2,1,0:T(8,128)}, u32[]{:S(2)}) copy-start(f32[80,16,512]{2,1,0:T(8,128)} %get-tuple-element.70) | copy-start | bytes 7864324
  154.9 18.3 %all-to-all-start.1 = ((f32[32,4,512]{2,1,0:T(4,128)}), f32[32,4,512]{2,1,0:T(4,128)S(1)}, u32[]{:S(2)}, u32[]{:S(2)}) async-start(f32[32,4,512]{2,1,0:T(4,128)} %shard_map.139), calls=%async_computation.1 | async-start | bytes 524288 | tf_op jit(solution)/shard_map/all_to_all | solution.py:434
  (52 other events, 62.4 us)

commit v2 on v1

v2 whole, which is shorter than its diff:
```python
import functools
import math

import jax
import jax.numpy as jnp
from jax import lax
from jax.experimental import pallas as pl
from jax.experimental.pallas import tpu as pltpu
from jax.sharding import PartitionSpec as P

courant_scale = 0.05
diffusion = 0.15
viscosity = 0.15
coriolis = 0.1
heat_gain = 0.25
water_gain = 0.25
stress_gain = 0.25


LANES = 256
TERMS = 3
GROUP = 8
VMEM_BYTES = 60 * 2**20
SMALL_BYTES = 24 * 2**20


def cut(values):
    terms = []
    rest = values
    for term_index in range(TERMS):
        term = rest.astype(jnp.bfloat16)
        terms.append(term)
        if term_index < TERMS - 1:
            rest = rest - term.astype(jnp.float32)
    return terms


def one_hot(positions, count):
    slots = positions.shape[1]
    base = positions - lax.broadcasted_iota(jnp.int32, (8, slots), 0)
    rows = [jnp.where(base == 8 * j, 1.0, 0.0) for j in range(count // 8)]
    return jnp.concatenate(rows, 0).astype(jnp.bfloat16)


def each_owner(owners, body):
    def outer(group, carry):
        body(group)
        return carry

    lax.fori_loop(0, owners // GROUP, outer, 0)


def send_kernel(
    flux_in, cell_in, weight_in, out_ref, flux_ref, cell_ref, weight_ref, raw_ref, table_ref, sem
):
    owners, slots = cell_ref.shape
    copies = [
        pltpu.make_async_copy(flux_in, flux_ref, sem.at[0]),
        pltpu.make_async_copy(cell_in, cell_ref, sem.at[1]),
        pltpu.make_async_copy(weight_in, weight_ref, sem.at[2]),
    ]
    for copy in copies:
        copy.start()
    blocks = flux_ref.shape[1] // LANES
    raw_ref[...] = jnp.zeros_like(raw_ref)
    copies[0].wait()
    for block in range(blocks):
        x = flux_ref[:, block * LANES : (block + 1) * LANES]
        heat = heat_gain * (x[0:1] + x[1:2] + x[2:3] + x[3:4])
        water = water_gain * (x[4:5] - x[5:6])
        raw_ref[4 * block : 4 * block + 4, :] = jnp.concatenate(
            [heat, water, stress_gain * x[6:8]], 0
        )
    rows = raw_ref.shape[0]
    for term_index, term in enumerate(cut(raw_ref[...])):
        table_ref[term_index * rows : (term_index + 1) * rows, :] = term
    copies[1].wait()
    copies[2].wait()

    def body(group):
        first = pl.multiple_of(group * GROUP, GROUP)
        cells = cell_ref[pl.ds(first, GROUP), :]
        weights = weight_ref[pl.ds(first, GROUP), :]
        for k in range(GROUP):
            cell = cells[k : k + 1]
            found = jnp.dot(
                table_ref[...],
                one_hot(cell & (LANES - 1), LANES),
                preferred_element_type=jnp.float32,
            )
            base = cell // LANES - lax.broadcasted_iota(jnp.int32, (8, slots), 0) // 4
            total = jnp.zeros((8, slots), jnp.float32)
            for j in range(rows // 8):
                value = found[8 * j : 8 * j + 8]
                for t in range(1, TERMS):
                    value = value + found[t * rows + 8 * j : t * rows + 8 * j + 8]
                total = total + jnp.where(base == 2 * j, value, 0.0)
            out_ref[first + k] = (total[0:4] + total[4:8]) * weights[k : k + 1]

    each_owner(owners, body)


def exchange_kernel(come_ref, cell_ref, top_ref, push_ref, out_ref, sum_ref, table_ref):
    owners, slots = cell_ref.shape
    rows, cols = top_ref.shape[1:]
    high = rows * cols // LANES
    sum_ref[...] = jnp.zeros_like(sum_ref)

    def add(group):
        first = pl.multiple_of(group * GROUP, GROUP)
        cells = cell_ref[pl.ds(first, GROUP), :]
        for k in range(GROUP):
            cell = cells[k : k + 1]
            col = cell % cols
            spot = (col // LANES) * rows + cell // cols
            mask = lax.broadcasted_iota(jnp.int32, (high, slots), 0) == spot
            left = []
            for term in cut(come_ref[first + k]):
                wide = term.astype(jnp.float32)
                for f in range(4):
                    left.append(jnp.where(mask, wide[f : f + 1], 0.0))
            sum_ref[...] += lax.dot_general(
                jnp.concatenate(left, 0).astype(jnp.bfloat16),
                one_hot(col % LANES, LANES),
                (((1,), (1,)), ((), ())),
                preferred_element_type=jnp.float32,
            )

    each_owner(owners, add)
    for f in range(4):
        for b in range(cols // LANES):
            span = slice(b * LANES, (b + 1) * LANES)
            value = 0.0
            for t in reversed(range(TERMS)):
                at = (t * 4 + f) * high + b * rows
                value = value + sum_ref[at : at + rows, :]
            push_ref[f, :, span] = value
            surface = top_ref[f, :, span] + value * top_ref[4, :, span]
            for t, term in enumerate(cut(surface)):
                at = (t * 4 + f) * high + b * rows
                table_ref[at : at + rows, :] = term

    def pick(group):
        first = pl.multiple_of(group * GROUP, GROUP)
        cells = cell_ref[pl.ds(first, GROUP), :]
        for k in range(GROUP):
            cell = cells[k : k + 1]
            col = cell % cols
            spot = (col // LANES) * rows + cell // cols
            found = jnp.dot(
                table_ref[...],
                one_hot(col % LANES, LANES),
                preferred_element_type=jnp.float32,
            )
            base = spot - lax.broadcasted_iota(jnp.int32, (8, slots), 0)
            masks = [base == 8 * j for j in range(high // 8)]
            picked = []
            for f in range(4):
                total = jnp.zeros((8, slots), jnp.float32)
                for j in range(high // 8):
                    at = f * high + 8 * j
                    value = found[at : at + 8]
                    for t in range(1, TERMS):
                        value = value + found[t * 4 * high + at : t * 4 * high + at + 8]
                    total = total + jnp.where(masks[j], value, 0.0)
                picked.append(jnp.sum(total, axis=0, keepdims=True))
            out_ref[first + k] = jnp.concatenate(picked, 0)

    each_owner(owners, pick)


def weight_kernel(cell_ref, weight_ref, out_ref, sum_ref):
    owners, slots = cell_ref.shape
    high = sum_ref.shape[0] // TERMS
    sum_ref[...] = jnp.zeros_like(sum_ref)

    def body(group):
        first = pl.multiple_of(group * GROUP, GROUP)
        cells = cell_ref[pl.ds(first, GROUP), :]
        weights = weight_ref[pl.ds(first, GROUP), :]
        for k in range(GROUP):
            cell = cells[k : k + 1]
            mask = lax.broadcasted_iota(jnp.int32, (high, slots), 0) == cell // LANES
            left = [
                jnp.where(mask, term.astype(jnp.float32), 0.0)
                for term in cut(weights[k : k + 1])
            ]
            sum_ref[...] += lax.dot_general(
                jnp.concatenate(left, 0).astype(jnp.bfloat16),
                one_hot(cell & (LANES - 1), LANES),
                (((1,), (1,)), ((), ())),
                preferred_element_type=jnp.float32,
            )

    each_owner(owners, body)
    value = 0.0
    for t in reversed(range(TERMS)):
        value = value + sum_ref[t * high : (t + 1) * high, :]
    out_ref[...] = 1.0 / jnp.maximum(value, 1.0)


def return_kernel(come_ref, cell_ref, weight_ref, inverse_ref, out_ref, sum_ref):
    owners, slots = cell_ref.shape
    blocks = out_ref.shape[1] // LANES
    rows = sum_ref.shape[0] // TERMS
    sum_ref[...] = jnp.zeros_like(sum_ref)

    def body(group):
        first = pl.multiple_of(group * GROUP, GROUP)
        cells = cell_ref[pl.ds(first, GROUP), :]
        weights = weight_ref[pl.ds(first, GROUP), :]
        for k in range(GROUP):
            cell = cells[k : k + 1]
            base = cell // LANES - lax.broadcasted_iota(jnp.int32, (8, slots), 0) // 4
            left = []
            for term in cut(come_ref[first + k] * weights[k : k + 1]):
                wide = term.astype(jnp.float32)
                wide = jnp.concatenate([wide, wide], 0)
                for j in range(rows // 8):
                    left.append(jnp.where(base == 2 * j, wide, 0.0))
            sum_ref[...] += lax.dot_general(
                jnp.concatenate(left, 0).astype(jnp.bfloat16),
                one_hot(cell & (LANES - 1), LANES),
                (((1,), (1,)), ((), ())),
                preferred_element_type=jnp.float32,
            )

    each_owner(owners, body)
    for block in range(blocks):
        value = 0.0
        for t in reversed(range(TERMS)):
            at = t * rows + 4 * block
            value = value + sum_ref[at : at + 4, :]
        out_ref[:, block * LANES : (block + 1) * LANES] = (
            value * inverse_ref[block : block + 1, :]
        )


def up_to(count, step):
    return (count + step - 1) // step * step


def call(kernel, out_shapes, scratch, *operands, far=0, copies=0, limit=VMEM_BYTES, flops=0):
    vmem = pl.BlockSpec(memory_space=pltpu.VMEM)
    return pl.pallas_call(
        kernel,
        out_shape=[jax.ShapeDtypeStruct(shape, jnp.float32) for shape in out_shapes],
        in_specs=[pl.BlockSpec(memory_space=pltpu.HBM)] * far + [vmem] * (len(operands) - far),
        scratch_shapes=[pltpu.VMEM(shape, dtype) for shape, dtype in scratch]
        + [pltpu.SemaphoreType.DMA((copies,))] * (copies > 0),
        compiler_params=pltpu.CompilerParams(vmem_limit_bytes=limit),
        cost_estimate=pl.CostEstimate(
            flops=flops,
            transcendentals=0,
            bytes_accessed=sum(x.size * x.dtype.itemsize for x in operands)
            + sum(4 * math.prod(shape) for shape in out_shapes),
        ),
    )(*operands)


HALO = 2
EDGE = 128


def edge_kernel(t_ref, s_ref, u_ref, v_ref, wet_ref, west_ref, east_ref, left, right, wet, sem):
    levels, rows, cols = t_ref.shape
    count = levels * rows
    copies = []
    for f, ref in enumerate((t_ref, s_ref, u_ref, v_ref)):
        copies.append(
            (
                pltpu.make_async_copy(ref.at[:, :, :EDGE], left.at[f], sem.at[2 * f]),
                pltpu.make_async_copy(ref.at[:, :, cols - EDGE :], right.at[f], sem.at[2 * f + 1]),
            )
        )
    copies.append((pltpu.make_async_copy(wet_ref, wet, sem.at[8]),))
    for group in copies:
        for copy in group:
            copy.start()

    def sides(left, right):
        side = lax.broadcasted_iota(jnp.int32, left.shape, 1) < EDGE // 2
        turned = jnp.where(side, left, right).T
        return turned[:HALO], turned[EDGE - HALO :]

    for f in range(4):
        for copy in copies[f]:
            copy.wait()
        west, east = sides(left[f].reshape(count, EDGE), right[f].reshape(count, EDGE))
        west_ref[HALO * f : HALO * f + HALO, :] = west
        east_ref[HALO * f : HALO * f + HALO, :] = east
    copies[4][0].wait()
    west, east = sides(
        wet[:, :EDGE].astype(jnp.float32), wet[:, cols - EDGE :].astype(jnp.float32)
    )
    west_ref[HALO * 4 : HALO * 5, :] = jnp.zeros((HALO, count), jnp.float32)
    east_ref[HALO * 4 : HALO * 5, :] = jnp.zeros((HALO, count), jnp.float32)
    west_ref[HALO * 4 : HALO * 5, :rows] = west
    east_ref[HALO * 4 : HALO * 5, :rows] = east


def rows_kernel(t_ref, s_ref, u_ref, v_ref, wet_ref, from_west_ref, from_east_ref,
                down_ref, up_ref, side_ref):
    levels, rows, cols = t_ref.shape

    def turned(f, count):
        return jnp.concatenate(
            [
                from_east_ref[HALO * f : HALO * f + HALO, :count],
                jnp.zeros((EDGE - 2 * HALO, count), jnp.float32),
                from_west_ref[HALO * f : HALO * f + HALO, :count],
            ],
            0,
        ).T

    for f, ref in enumerate((t_ref, s_ref, u_ref, v_ref)):
        span = slice(f * levels, (f + 1) * levels)
        side = turned(f, levels * rows).reshape(levels, rows, EDGE)
        side_ref[span] = side
        down_ref[span, :, :cols] = ref[:, :HALO, :]
        up_ref[span, :, :cols] = ref[:, rows - HALO :, :]
        down_ref[span, :, cols:] = side[:, :HALO, :]
        up_ref[span, :, cols:] = side[:, rows - HALO :, :]
    side = turned(4, rows)
    wet = wet_ref[...].astype(jnp.float32)
    side_ref[4 * levels] = side
    down_ref[4 * levels, :, :cols] = wet[:HALO]
    up_ref[4 * levels, :, :cols] = wet[rows - HALO :]
    down_ref[4 * levels, :, cols:] = side[:HALO]
    up_ref[4 * levels, :, cols:] = side[rows - HALO :]


def ocean_kernel(total_rows, t_in, s_in, u_in, v_in, wet_in, side_in, north_in, fold_in,
                 south_in, mix_in, part_out, factor_out, reply_out, top_ref,
                 t_ref, s_ref, u_ref, v_ref, wet_ref, side_ref, north_ref, fold_ref, south_ref,
                 mix_ref, part_ref, scale_ref, factor_ref, reply_ref, east_gate, north_gate,
                 turn_ref, state_ref, middle_ref, before_ref, in_sem, out_sem):
    levels, rows, cols = t_ref.shape
    tall = rows + 8
    tiles = cols // EDGE
    spans = [slice(j * EDGE, (j + 1) * EDGE) for j in range(tiles + 1)]
    stripe = lax.axis_index("ocn")
    on_top = stripe == lax.axis_size("ocn") - 1
    copies = [
        pltpu.make_async_copy(source, target, in_sem.at[i])
        for i, (source, target) in enumerate(
            (
                (mix_in, mix_ref),
                (wet_in, wet_ref),
                (north_in, north_ref),
                (south_in, south_ref),
                (fold_in, fold_ref),
                (side_in, side_ref),
                (t_in, t_ref),
                (s_in, s_ref),
                (u_in, u_ref),
                (v_in, v_ref),
            )
        )
    ]
    for copy in copies:
        copy.start()

    copies[0].wait()
    above = jnp.zeros((rows, cols), jnp.float32)
    factor = above
    reply = None
    for k in range(levels):
        below = mix_ref[k] if k < levels - 1 else jnp.zeros_like(above)
        scale = 1.0 / (1.0 + above + below + above * factor)
        factor = -below * scale
        reply = scale if k == 0 else above * reply * scale
        scale_ref[k] = scale
        factor_ref[k] = factor
        reply_ref[k] = reply
        above = below
    factor_copy = pltpu.make_async_copy(factor_ref, factor_out, out_sem.at[1])
    factor_copy.start()
    copies[1].wait()
    open_water = wet_ref[...].astype(jnp.float32)
    for k in range(levels - 2, -1, -1):
        reply_ref[k + 1] = reply * open_water
        reply = reply_ref[k] - factor_ref[k] * reply
    reply_ref[0] = reply * open_water
    top_ref[4] = reply * open_water
    reply_copy = pltpu.make_async_copy(reply_ref, reply_out, out_sem.at[2])
    reply_copy.start()
    for copy in copies[2:]:
        copy.wait()

    @pl.when(on_top)
    def _():
        flip = EDGE - 1 - lax.broadcasted_iota(jnp.int32, (8, EDGE), 1)
        order = list(range(tiles))[::-1] + [tiles]
        blank = jnp.zeros((8 - HALO, EDGE), jnp.float32)

        def mirror(channel, sign):
            fold = fold_ref[channel]
            for j, span in enumerate(spans):
                part = fold[:, spans[order[j]]]
                part = jnp.concatenate([part[1:2], part[0:1], blank], 0)
                part = jnp.take_along_axis(part, flip, axis=1)
                north_ref[channel, :, span] = part[:HALO] * sign

        def mirror_level(k, carry):
            for f in range(4):
                mirror(f * levels + k, 1.0 if f < 2 else -1.0)
            return carry

        lax.fori_loop(0, levels, mirror_level, 0)
        mirror(4 * levels, 1.0)

    gap = jnp.zeros((8 - 2 * HALO, EDGE), jnp.float32)

    def beyond(channel, span):
        return jnp.concatenate([north_ref[channel, :, span], gap, south_ref[channel, :, span]], 0)

    lane = lax.broadcasted_iota(jnp.int32, (tall, EDGE), 1)
    first = lane == 0
    final = lane == EDGE - 1
    count = tiles + 1

    def ring(ref, centre, outer):
        ref[8 : 8 + rows] = centre
        ref[8 + rows : 8 + tall] = outer
        ref[0:8] = outer
        ref[8 + tall : 16 + tall] = centre[0:8]

    def ahead(x):
        return pltpu.roll(x, EDGE - 1, 1)

    def behind(x):
        return pltpu.roll(x, 1, 1)

    row = lax.broadcasted_iota(jnp.int32, (tall, EDGE), 0)
    row = jnp.where(row >= tall - HALO, row - tall, row) + stripe * rows
    row = jnp.where(row >= total_rows, 2 * total_rows - 1 - row, row)
    latitude = jnp.pi * ((row.astype(jnp.float32) + 0.5) / total_rows - 0.5)
    turn = coriolis * jnp.sin(latitude)
    for j, span in enumerate(spans):
        ring(
            state_ref.at[0, j],
            open_water[:, span] if j < tiles else side_ref[4 * levels],
            beyond(4 * levels, span),
        )
    for j in range(count):
        wet = state_ref[0, j, 8 : 8 + tall]
        after = state_ref[0, (j + 1) % count, 8 : 8 + tall]
        east_gate[j] = wet * jnp.where(final, ahead(after), ahead(wet))
        north = wet * state_ref[0, j, 9 : 9 + tall]
        ring(north_gate.at[j], north[:rows], north[rows:])
        turn_ref[j] = turn * wet

    def substep(source, order, height, put):
        def rolled(j):
            return [ahead(source[f, j, 8 : 8 + height]) for f in range(4)]

        def eastward(j, here, after):
            gate = east_gate[j, :height]
            return [
                gate
                * (jnp.where(final[:height], after[f], here[f]) - source[f, j, 8 : 8 + height])
                for f in range(4)
            ]

        here = rolled(order[0])
        passed = [behind(x) for x in eastward(order[-1], rolled(order[-1]), here)]
        for j in order[:-1]:
            after = rolled((j + 1) % count)
            east = eastward(j, here, after)
            here = after
            before, passed = passed, [behind(x) for x in east]
            west = [jnp.where(first[:height], p, q) for p, q in zip(before, passed)]
            north_open = north_gate[j, 8 : 8 + height]
            south_open = north_gate[j, 7 : 7 + height]
            value = [source[f, j, 8 : 8 + height] for f in range(4)]
            north = [
                north_open * (source[f, j, 9 : 9 + height] - value[f]) for f in range(4)
            ]
            south = [
                south_open * (value[f] - source[f, j, 7 : 7 + height]) for f in range(4)
            ]
            cx = courant_scale * value[2]
            cy = courant_scale * value[3]
            to_east = diffusion - jnp.minimum(cx, 0.0)
            to_west = diffusion + jnp.maximum(cx, 0.0)
            to_north = diffusion - jnp.minimum(cy, 0.0)
            to_south = diffusion + jnp.maximum(cy, 0.0)
            for f in range(2):
                put(
                    f,
                    j,
                    value[f]
                    + (
                        (to_east * east[f] - to_west * west[f])
                        + (to_north * north[f] - to_south * south[f])
                    ),
                )
            turning = turn_ref[j, :height]
            for f, other in ((2, turning * value[3]), (3, -turning * value[2])):
                put(
                    f,
                    j,
                    value[f]
                    + (viscosity * ((east[f] - west[f]) + (north[f] - south[f])) + other),
                )

    def level(k, carry):
        for f, ref in enumerate((t_ref, s_ref, u_ref, v_ref)):
            channel = f * levels + k
            for j, span in enumerate(spans):
                ring(
                    state_ref.at[f, j],
                    ref[k, :, span] if j < tiles else side_ref[channel],
                    beyond(channel, span),
                )

        def put_middle(f, j, value):
            middle_ref[k, f, j, 8 : 8 + tall] = value
            middle_ref[k, f, j, 0:8] = value[rows:]

        substep(state_ref, [tiles] + list(range(tiles)) + [tiles - 1], tall, put_middle)
        return carry

    def last_level(k, carry):
        before = jnp.maximum(k - 1, 0)
        start = jnp.where(k > 0, 1.0, 0.0)

        def put_part(f, j, value):
            span = spans[j]
            above = start * mix_ref[before, :, span]
            value = (value + above * before_ref[f, :, span]) * scale_ref[k, :, span]
            before_ref[f, :, span] = value
            part_ref[k, f, :, span] = value

        substep(middle_ref.at[k], list(range(tiles)) + [tiles], rows, put_part)
        pltpu.make_async_copy(part_ref.at[k], part_out.at[k], out_sem.at[0]).start()
        return carry

    before_ref[...] = jnp.zeros_like(before_ref)
    lax.fori_loop(0, levels, level, 0)
    lax.fori_loop(0, levels, last_level, 0)

    def back(j, solved):
        k = levels - 2 - j
        factor = factor_ref[k]
        return tuple(part_ref[k, f] - factor * solved[f] for f in range(4))

    solved = lax.fori_loop(0, levels - 1, back, tuple(part_ref[levels - 1, f] for f in range(4)))
    for f in range(4):
        top_ref[f] = solved[f]
    pltpu.make_async_copy(part_ref, part_out, out_sem.at[0]).wait()
    factor_copy.wait()
    reply_copy.wait()


def finish_kernel(part_ref, factor_ref, reply_ref, push_ref, t_out, s_out, u_out, v_out):
    levels = t_out.shape[0]
    outs = (t_out, s_out, u_out, v_out)
    last = levels - 1
    for f in range(4):
        outs[f][last] = part_ref[last, f] + push_ref[f] * reply_ref[last]

    def back(j, solved):
        k = last - 1 - j
        factor = factor_ref[k]
        reply = reply_ref[k]
        solved = tuple(part_ref[k, f] - factor * solved[f] for f in range(4))
        for f in range(4):
            outs[f][k] = solved[f] + push_ref[f] * reply
        return solved

    lax.fori_loop(0, last, back, tuple(part_ref[last, f] for f in range(4)))


def per_device(
    atm_flux, send_cell, send_weight, recv_cell, temp, salt, uvel, vvel, wet_mask, vert_mix
):
    levels, block_rows, block_cols = temp.shape
    slot_cells = send_cell[0]
    slot_weights = send_weight[0]
    arrival_cells = recv_cell[0]
    owners, capacity = slot_cells.shape
    atm_cells = atm_flux.shape[1]
    blocks = atm_cells // LANES
    rows = up_to(4 * blocks, 16)
    high = block_rows * block_cols // LANES
    wide = block_cols + EDGE
    columns = lax.axis_size("atm")
    stripes = lax.axis_size("ocn")
    whole = (levels, block_rows, block_cols)
    ocean = (temp, salt, uvel, vvel)

    edge = (5 * HALO, levels * block_rows)
    strips = (4, levels, block_rows, EDGE)
    west, east = call(
        edge_kernel,
        [edge, edge],
        [
            (strips, jnp.float32),
            (strips, jnp.float32),
            ((block_rows, block_cols), jnp.int32),
        ],
        *ocean,
        wet_mask,
        far=5,
        copies=9,
    )
    from_east = lax.ppermute(west, "atm", [((i + 1) % columns, i) for i in range(columns)])
    from_west = lax.ppermute(east, "atm", [(i, (i + 1) % columns) for i in range(columns)])

    strip = (4 * levels + 1, HALO, wide)
    down, up, side = call(
        rows_kernel,
        [strip, strip, (4 * levels + 1, block_rows, EDGE)],
        [],
        *ocean,
        wet_mask,
        from_west,
        from_east,
    )
    north = lax.ppermute(down, "ocn", [(i + 1, i) for i in range(stripes - 1)])
    south = lax.ppermute(up, "ocn", [(i, i + 1) for i in range(stripes - 1)])
    last = stripes - 1
    fold = lax.ppermute(
        up,
        ("atm", "ocn"),
        [(i * stripes + last, (columns - 1 - i) * stripes + last) for i in range(columns)],
    )
    (outgoing,) = call(
        send_kernel,
        [(owners, 4, capacity)],
        [
            (atm_flux.shape, jnp.float32),
            (slot_cells.shape, jnp.int32),
            (slot_cells.shape, jnp.float32),
            ((rows, LANES), jnp.float32),
            ((TERMS * rows, LANES), jnp.bfloat16),
        ],
        atm_flux,
        slot_cells,
        slot_weights,
        far=3,
        copies=3,
        flops=2 * TERMS * rows * LANES * owners * capacity,
    )
    outgoing, north, south, fold = lax.optimization_barrier((outgoing, north, south, fold))
    incoming = lax.all_to_all(outgoing, ("atm", "ocn"), split_axis=0, concat_axis=0, tiled=True)
    (inverse,) = call(
        weight_kernel,
        [(up_to(blocks, 16), LANES)],
        [((TERMS * up_to(blocks, 16), LANES), jnp.float32)],
        slot_cells,
        slot_weights,
        limit=SMALL_BYTES,
        flops=2 * TERMS * up_to(blocks, 16) * LANES * owners * capacity,
    )
    vmem = pl.BlockSpec(memory_space=pltpu.VMEM)
    far = pl.BlockSpec(memory_space=pltpu.HBM)
    tall = block_rows + 8
    tiles = wide // EDGE
    plane = (block_rows, block_cols)
    shapes = [(levels, 4, *plane), whole, whole, (5, *plane)]
    part, factor, reply, top = pl.pallas_call(
        functools.partial(ocean_kernel, block_rows * stripes),
        out_shape=[jax.ShapeDtypeStruct(shape, jnp.float32) for shape in shapes],
        in_specs=[far] * 10,
        out_specs=[far] * 3 + [vmem],
        scratch_shapes=[
            *[pltpu.VMEM(whole, jnp.float32)] * 4,
            pltpu.VMEM(plane, jnp.int32),
            pltpu.VMEM(side.shape, jnp.float32),
            pltpu.VMEM(strip, jnp.float32),
            pltpu.VMEM(strip, jnp.float32),
            pltpu.VMEM(strip, jnp.float32),
            pltpu.VMEM(vert_mix.shape, jnp.float32),
            pltpu.VMEM(shapes[0], jnp.float32),
            pltpu.VMEM(whole, jnp.float32),
            pltpu.VMEM(whole, jnp.float32),
            pltpu.VMEM(whole, jnp.float32),
            pltpu.VMEM((tiles, tall, EDGE), jnp.float32),
            pltpu.VMEM((tiles, tall + 16, EDGE), jnp.float32),
            pltpu.VMEM((tiles, tall, EDGE), jnp.float32),
            pltpu.VMEM((4, tiles, tall + 16, EDGE), jnp.float32),
            pltpu.VMEM((levels, 4, tiles, tall + 16, EDGE), jnp.float32),
            pltpu.VMEM((4, *plane), jnp.float32),
            pltpu.SemaphoreType.DMA((10,)),
            pltpu.SemaphoreType.DMA((3,)),
        ],
        compiler_params=pltpu.CompilerParams(vmem_limit_bytes=VMEM_BYTES),
        cost_estimate=pl.CostEstimate(
            flops=80 * 4 * 2 * temp.size, transcendentals=0, bytes_accessed=4 * 13 * temp.size
        ),
    )(*ocean, wet_mask, side, north, fold, south, vert_mix)

    push, leaving = call(
        exchange_kernel,
        [(4, block_rows, block_cols), (owners, 4, capacity)],
        [
            ((TERMS * 4 * high, LANES), jnp.float32),
            ((TERMS * 4 * high, LANES), jnp.bfloat16),
        ],
        incoming,
        arrival_cells,
        top,
        limit=SMALL_BYTES,
        flops=2 * 2 * TERMS * 4 * high * LANES * owners * capacity,
    )
    returning = lax.all_to_all(leaving, ("atm", "ocn"), split_axis=0, concat_axis=0, tiled=True)
    finished = call(finish_kernel, [whole] * 4, [], part, factor, reply, push)
    (atm_surface,) = call(
        return_kernel,
        [(4, atm_cells)],
        [((TERMS * rows, LANES), jnp.float32)],
        returning,
        slot_cells,
        slot_weights,
        inverse,
        limit=SMALL_BYTES,
        flops=2 * TERMS * rows * LANES * owners * capacity,
    )
    return (*finished, atm_surface)


def solution(mesh):
    in_specs = (
        P(None, ("atm", "ocn")),
        P(("atm", "ocn"), None, None),
        P(("atm", "ocn"), None, None),
        P(("atm", "ocn"), None, None),
        P(None, "ocn", "atm"),
        P(None, "ocn", "atm"),
        P(None, "ocn", "atm"),
        P(None, "ocn", "atm"),
        P("ocn", "atm"),
        P(None, "ocn", "atm"),
    )
    out_specs = (
        P(None, "ocn", "atm"),
        P(None, "ocn", "atm"),
        P(None, "ocn", "atm"),
        P(None, "ocn", "atm"),
        P(None, ("atm", "ocn")),
    )
    return jax.shard_map(
        per_device, mesh=mesh, in_specs=in_specs, out_specs=out_specs, check_vma=False
    )
```

time: 180 us -> 80.9 us (0.45); the launches traced: 178 us -> 80.4 us
  other arithmetic: 75.5 us -> 0 us
  local copies, waits for them, and re-layouts: 34.7 us -> 2.2 us
  Pallas kernels: 20.9 us -> 47.1 us
  starting transfers between devices: 33.5 us -> 24.1 us
  waiting for transfers between devices: 11.3 us -> 6.22 us
    pallas_call x5 -> x8, Pallas kernels: 20.9 us -> 47.1 us  [the longest x7 31.5 us: call(): pl.pallas_call(kernel, out_shape=[jax.ShapeDtypeStruct(shape, jnp.float32...]
    sub x3 -> x0, other arithmetic: 22.4 us -> none  [the longest x2 20.7 us: tendency(): laplace = diff_east - diff_west + diff_north - diff_south]
    unnamed x185 -> x20, local copies, waits for them, and re-layouts: 19.7 us -> 2.2 us
    mul x13 -> x0, other arithmetic: 17 us -> none  [the longest x9 13.3 us: vertical_solve(): solved.append(partial_rows[level_index] - factors[level_index] * solved[-1])]
    ppermute x12 -> x5, starting transfers between devices: 19.4 us -> 7.29 us  [the longest x1 2.99 us: per_device(): lax.ppermute(east, 'atm', [(i, (i + 1) % columns) for i in range(columns)])]
    unnamed x10 -> x0, other arithmetic: 8.53 us -> none
    slice x3 -> x0, other arithmetic: 7.56 us -> none  [the longest x2 6.27 us: padded(): lax.slice_in_dim(cells, cells.shape[dim] - width, cells.shape[dim], axis=...]
    add x3 -> x0, other arithmetic: 7.13 us -> none  [the longest x2 5.25 us: tendency(): tracer_part(fields)]
  transfers between devices with their start and end apart: 14 -> 7, of which waited for: 5 -> 3; matrix products, arithmetic and copies ran while one was open for 33% -> 0% of each run, Pallas kernels for 7% -> 35%
where the time goes in v2:
time: 80.9 us; the launch traced here: 80.4 us
  Pallas kernels  47.1 us (58%)
  starting transfers between devices  24.1 us (30%)
  waiting for transfers between devices  6.22 us (8%)
  local copies, waits for them, and re-layouts  2.2 us (3%)
  between operations  0.83 us (1%)
    pallas_call x7, Pallas kernels, call(): pl.pallas_call(kernel, out_shape=[jax.ShapeDtypeStruct(shape, jnp.float32...  31.5 us
    pallas_call x1, Pallas kernels, per_device(): pl.pallas_call(functools.partial(ocean_kernel, block_rows * stripes), out...  15.6 us
    all_to_all x1, starting transfers between devices, per_device(): lax.all_to_all(outgoing, ('atm', 'ocn'), split_axis=0, concat_axis=0, til...  9.42 us
    all_to_all x1, starting transfers between devices, per_device(): lax.all_to_all(leaving, ('atm', 'ocn'), split_axis=0, concat_axis=0, tile...  7.41 us
    all_to_all x1, waiting for transfers between devices, per_device(): lax.all_to_all(leaving, ('atm', 'ocn'), split_axis=0, concat_axis=0, tile...  3.2 us
    ppermute x1, starting transfers between devices, per_device(): lax.ppermute(east, 'atm', [(i, (i + 1) % columns) for i in range(columns)])  2.99 us
    unnamed x20, local copies, waits for them, and re-layouts  2.2 us
    ppermute x1, waiting for transfers between devices, per_device(): lax.ppermute(east, 'atm', [(i, (i + 1) % columns) for i in range(columns)])  1.95 us
  transfers between devices with their start and end apart: 7, of which 3 were waited for; matrix products, arithmetic and copies ran while one was open for 0% of the time, Pallas kernels for 35%

profile of v2, /device:TPU:0, one launch (start us, length us, event | category | flops | bytes accessed | tf_op | source)
XLA Modules:
  0.0 80.4 jit_solution(17141297598167560515)
XLA Ops:
  0.6 2.4 %shard_map.137 = (f32[10,320]{1,0:T(8,128)}, f32[10,320]{1,0:T(8,128)}) custom-call(f32[20,16,512]{2,1,0:T(8,128)} %t_in.1, f32[20,16,512]{2,1,0:T(8,128)} %s_in.1, f32[20,16,512]{2,1,0:T(8,128)} %u_in.1, f32[20,16,512]{2,1,0:T(8,128)} %v_in.1, s32[16,512]{1,0:T(8,128)} %wet_in.1), custom_call_target="tpu_custom_call" | custom-call | bytes 2679808 | tf_op jit(solution)/shard_map/pallas_call | solution.py:245
  3.0 3.0 %collective-permute-start = (f32[10,320]{1,0:T(8,128)}, f32[10,320]{1,0:T(8,128)S(1)}, u32[]{:S(2)}, u32[]{:S(2)}) collective-permute-start(f32[10,320]{1,0:T(8,128)} %get-tuple-element.24), channel_id=1, source_target_pairs={{0,8},{8,16},{16,24},{24,0},{1,9},{9,17},{17,25},{25,1},{2,10},{10... | collective-permute-start | bytes 38408 | tf_op jit(solution)/shard_map/ppermute | solution.py:610
  6.0 1.0 %collective-permute-start.1 = (f32[10,320]{1,0:T(8,128)}, f32[10,320]{1,0:T(8,128)S(1)}, u32[]{:S(2)}, u32[]{:S(2)}) collective-permute-start(f32[10,320]{1,0:T(8,128)} %get-tuple-element.25), channel_id=1, source_target_pairs={{8,0},{16,8},{24,16},{0,24},{9,1},{17,9},{25,17},{1,25},{10,2},{18... | collective-permute-start | bytes 38408 | tf_op jit(solution)/shard_map/ppermute | solution.py:609
  7.0 2.0 %collective-permute-done.from_west_ref = f32[10,320]{1,0:T(8,128)S(1)} collective-permute-done((f32[10,320]{1,0:T(8,128)}, f32[10,320]{1,0:T(8,128)S(1)}, u32[]{:S(2)}, u32[]{:S(2)}) %collective-permute-start) | collective-permute-done | bytes 12832 | tf_op jit(solution)/shard_map/ppermute | solution.py:610
  9.0 0.0 copy-start.8
  9.0 1.1 %collective-permute-done.1.from_east_ref = f32[10,320]{1,0:T(8,128)S(1)} collective-permute-done((f32[10,320]{1,0:T(8,128)}, f32[10,320]{1,0:T(8,128)S(1)}, u32[]{:S(2)}, u32[]{:S(2)}) %collective-permute-start.1) | collective-permute-done | bytes 12832 | tf_op jit(solution)/shard_map/ppermute | solution.py:609
  10.0 0.0 copy-done.8
  10.0 0.0 copy-start.9
  10.0 0.6 copy-done.9
  10.6 3.1 %shard_map.138 = (f32[81,2,640]{2,1,0:T(2,128)}, f32[81,2,640]{2,1,0:T(2,128)}, f32[81,16,128]{2,1,0:T(8,128)}) custom-call(f32[20,16,512]{2,1,0:T(8,128)} %t_in.1, f32[20,16,512]{2,1,0:T(8,128)} %s_in.1, f32[20,16,512]{2,1,0:T(8,128)} %u_in.1, f32[20,16,512]{2,1,0:T(8,128)} %v_in.1, s32[16,512]{1,0:T(8,128)} %wet_in.1, f32[10,320]{1,0:T(8,128)} %copy-done.8, ...), custom_call_target="tpu_custom_call" | custom-call | bytes 4172800 | tf_op jit(solution)/shard_map/pallas_call | solution.py:245
  13.7 1.3 %collective-permute-start.3 = (f32[81,2,640]{2,1,0:T(2,128)}, f32[81,2,640]{2,1,0:T(2,128)S(1)}, u32[]{:S(2)}, u32[]{:S(2)}) collective-permute-start(f32[81,2,640]{2,1,0:T(2,128)} %get-tuple-element.28), channel_id=1, source_target_pairs={{0,1},{1,2},{2,3},{3,4},{4,5},{5,6},{6,7},{8,9},{9,10},{10,11},{11... | collective-permute-start | bytes 1244168 | tf_op jit(solution)/shard_map/ppermute | solution.py:623
  15.1 0.7 collective-permute-start.4
  15.8 1.3 %collective-permute-start.2 = (f32[81,2,640]{2,1,0:T(2,128)}, f32[81,2,640]{2,1,0:T(2,128)S(1)}, u32[]{:S(2)}, u32[]{:S(2)}) collective-permute-start(f32[81,2,640]{2,1,0:T(2,128)} %get-tuple-element.27), channel_id=1, source_target_pairs={{1,0},{2,1},{3,2},{4,3},{5,4},{6,5},{7,6},{9,8},{10,9},{11,10},{12... | collective-permute-start | bytes 1244168 | tf_op jit(solution)/shard_map/ppermute | solution.py:622
  17.1 5.4 %shard_map.139 = f32[32,4,512]{2,1,0:T(4,128)} custom-call(f32[8,6912]{1,0:T(8,128)} %flux_in.1, s32[32,512]{1,0:T(8,128)} %bitcast.4, f32[32,512]{1,0:T(8,128)} %bitcast.7), custom_call_target="tpu_custom_call" | custom-call | flops 2818572288 | bytes 614400 | tf_op jit(solution)/shard_map/pallas_call | solution.py:245
  22.5 0.0 collective-permute-done.3.south_in
  22.5 0.0 copy-start.5
  22.5 0.0 collective-permute-done.4.fold_in
  22.5 0.0 copy-start.6
  22.5 0.0 collective-permute-done.2.north_in
  22.5 0.0 copy-start.7
  22.5 9.4 %all-to-all-start = ((f32[32,4,512]{2,1,0:T(4,128)}), f32[32,4,512]{2,1,0:T(4,128)S(1)}, u32[]{:S(2)}, u32[]{:S(2)}) async-start(f32[32,4,512]{2,1,0:T(4,128)} %shard_map.139), calls=%async_computation | async-start | bytes 524288 | tf_op jit(solution)/shard_map/all_to_all | solution.py:648
  32.0 0.0 copy-start.2
  32.0 0.0 copy-done.5
  32.0 0.0 copy-done.6
  32.0 0.0 copy-done.7
  32.0 15.6 %shard_map.140 = (f32[20,4,16,512]{3,2,1,0:T(8,128)}, f32[20,16,512]{2,1,0:T(8,128)}, f32[20,16,512]{2,1,0:T(8,128)}, f32[5,16,512]{2,1,0:T(8,128)}) custom-call(f32[20,16,512]{2,1,0:T(8,128)} %t_in.1, f32[20,16,512]{2,1,0:T(8,128)} %s_in.1, f32[20,16,512]{2,1,0:T(8,128)} %u_in.1, f32[20,16,512]{2,1,0:T(8,128)} %v_in.1, s32[16,512]{1,0:T(8,128)} %wet_in.1, ...), custom_call_target="tpu_custom_call" | custom-call | flops 104857600 | bytes 8519680 | tf_op jit(solution)/shard_map/pallas_call | solution.py:664
  47.6 0.0 all-to-all-done.come_ref
  47.6 0.0 copy-done.2
  47.7 0.0 copy-start.1
  47.7 0.9 %copy-done.1 = f32[5,16,512]{2,1,0:T(8,128)S(1)} copy-done((f32[5,16,512]{2,1,0:T(8,128)S(1)}, f32[5,16,512]{2,1,0:T(8,128)}, u32[]{:S(2)}) %copy-start.1) | copy-done | bytes 163864
  48.6 0.0 copy-start.3
  48.6 0.0 copy-start.4
  48.6 9.0 %shard_map.141 = (f32[4,16,512]{2,1,0:T(8,128)S(1)}, f32[32,4,512]{2,1,0:T(4,128)}) custom-call(f32[32,4,512]{2,1,0:T(4,128)S(1)} %all-to-all-done.come_ref, s32[32,512]{1,0:T(8,128)S(1)} %bitcast.3, f32[5,16,512]{2,1,0:T(8,128)S(1)} %copy-done.1), custom_call_target="tpu_custom_call" | custom-call | flops 6442450944 | bytes 884736 | tf_op jit(solution)/shard_map/pallas_call | solution.py:245
  57.6 0.0 copy-start
  57.6 0.6 copy-done
  58.3 7.4 %all-to-all-start.1 = ((f32[32,4,512]{2,1,0:T(4,128)}), f32[32,4,512]{2,1,0:T(4,128)S(1)}, u32[]{:S(2)}, u32[]{:S(2)}) async-start(f32[32,4,512]{2,1,0:T(4,128)} %get-tuple-element.42), calls=%async_computation.1 | async-start | bytes 524288 | tf_op jit(solution)/shard_map/all_to_all | solution.py:709
  65.7 0.0 copy-done.3
  65.7 0.0 copy-done.4
  65.7 3.1 %shard_map.143.inverse_ref = f32[32,256]{1,0:T(8,128)S(1)} custom-call(s32[32,512]{1,0:T(8,128)S(1)} %bitcast.5, f32[32,512]{1,0:T(8,128)S(1)} %bitcast.8), custom_call_target="tpu_custom_call" | custom-call | flops 805306368 | bytes 163840 | tf_op jit(solution)/shard_map/pallas_call | solution.py:245
  68.8 4.0 %shard_map.142 = (f32[20,16,512]{2,1,0:T(8,128)}, f32[20,16,512]{2,1,0:T(8,128)}, f32[20,16,512]{2,1,0:T(8,128)}, f32[20,16,512]{2,1,0:T(8,128)}) custom-call(f32[20,4,16,512]{3,2,1,0:T(8,128)} %get-tuple-element.32.part_ref, f32[20,16,512]{2,1,0:T(8,128)} %get-tuple-element.33.factor_ref, f32[20,16,512]{2,1,0:T(8,128)} %get-tuple-element.34.reply_ref, ...), custom_call_target="tpu_custom_call" | custom-call | bytes 6684672 | tf_op jit(solution)/shard_map/pallas_call | solution.py:245
  72.9 3.2 %all-to-all-done.1.come_ref = f32[32,4,512]{2,1,0:T(4,128)S(1)} async-done(((f32[32,4,512]{2,1,0:T(4,128)}), f32[32,4,512]{2,1,0:T(4,128)S(1)}, u32[]{:S(2)}, u32[]{:S(2)}) %all-to-all-start.1) | async-done | bytes 262176 | tf_op jit(solution)/shard_map/all_to_all | solution.py:709
  76.1 4.4 %shard_map.144 = f32[4,6912]{1,0:T(4,128)} custom-call(f32[32,4,512]{2,1,0:T(4,128)S(1)} %all-to-all-done.1.come_ref, s32[32,512]{1,0:T(8,128)S(1)} %bitcast.6, f32[32,512]{1,0:T(8,128)S(1)} %bitcast.9, f32[32,256]{1,0:T(8,128)S(1)} %shard_map.143.inverse_ref), custom_call_target="tpu_custom_call" | custom-call | flops 2818572288 | bytes 536576 | tf_op jit(solution)/shard_map/pallas_call | solution.py:245
Async XLA Ops:
  3.0 6.0 %collective-permute-start = (f32[10,320]{1,0:T(8,128)}, f32[10,320]{1,0:T(8,128)S(1)}, u32[]{:S(2)}, u32[]{:S(2)}) collective-permute-start(f32[10,320]{1,0:T(8,128)} %get-tuple-element.24), channel_id=1, source_target_pairs={{0,8},{8,16},{16,24},{24,0},{1,9},{9,17},{17,25},{25,1},{2,10},{10... | collective-permute-start | bytes 38408 | tf_op jit(solution)/shard_map/ppermute | solution.py:610
  6.0 4.0 %collective-permute-start.1 = (f32[10,320]{1,0:T(8,128)}, f32[10,320]{1,0:T(8,128)S(1)}, u32[]{:S(2)}, u32[]{:S(2)}) collective-permute-start(f32[10,320]{1,0:T(8,128)} %get-tuple-element.25), channel_id=1, source_target_pairs={{8,0},{16,8},{24,16},{0,24},{9,1},{17,9},{25,17},{1,25},{10,2},{18... | collective-permute-start | bytes 38408 | tf_op jit(solution)/shard_map/ppermute | solution.py:609
  9.0 1.1 %copy-start.8 = (f32[10,320]{1,0:T(8,128)}, f32[10,320]{1,0:T(8,128)S(1)}, u32[]{:S(2)}) copy-start(f32[10,320]{1,0:T(8,128)S(1)} %collective-permute-done.from_west_ref) | copy-start | bytes 38404
  10.0 0.6 copy-start.9
  13.7 8.7 %collective-permute-start.3 = (f32[81,2,640]{2,1,0:T(2,128)}, f32[81,2,640]{2,1,0:T(2,128)S(1)}, u32[]{:S(2)}, u32[]{:S(2)}) collective-permute-start(f32[81,2,640]{2,1,0:T(2,128)} %get-tuple-element.28), channel_id=1, source_target_pairs={{0,1},{1,2},{2,3},{3,4},{4,5},{5,6},{6,7},{8,9},{9,10},{10,11},{11... | collective-permute-start | bytes 1244168 | tf_op jit(solution)/shard_map/ppermute | solution.py:623
  15.1 7.4 %collective-permute-start.4 = (f32[81,2,640]{2,1,0:T(2,128)}, f32[81,2,640]{2,1,0:T(2,128)S(1)}, u32[]{:S(2)}, u32[]{:S(2)}) collective-permute-start(f32[81,2,640]{2,1,0:T(2,128)} %get-tuple-element.28), channel_id=1, source_target_pairs={{7,31},{15,23},{23,15},{31,7}} | collective-permute-start | bytes 1244168 | tf_op jit(solution)/shard_map/ppermute | solution.py:625
  15.8 6.8 %collective-permute-start.2 = (f32[81,2,640]{2,1,0:T(2,128)}, f32[81,2,640]{2,1,0:T(2,128)S(1)}, u32[]{:S(2)}, u32[]{:S(2)}) collective-permute-start(f32[81,2,640]{2,1,0:T(2,128)} %get-tuple-element.27), channel_id=1, source_target_pairs={{1,0},{2,1},{3,2},{4,3},{5,4},{6,5},{7,6},{9,8},{10,9},{11,10},{12... | collective-permute-start | bytes 1244168 | tf_op jit(solution)/shard_map/ppermute | solution.py:622
  22.5 9.5 %copy-start.5 = (f32[81,2,640]{2,1,0:T(2,128)}, f32[81,2,640]{2,1,0:T(2,128)S(1)}, u32[]{:S(2)}) copy-start(f32[81,2,640]{2,1,0:T(2,128)S(1)} %collective-permute-done.3.south_in) | copy-start | bytes 1244164
  22.5 9.5 %copy-start.6 = (f32[81,2,640]{2,1,0:T(2,128)}, f32[81,2,640]{2,1,0:T(2,128)S(1)}, u32[]{:S(2)}) copy-start(f32[81,2,640]{2,1,0:T(2,128)S(1)} %collective-permute-done.4.fold_in) | copy-start | bytes 1244164
  22.5 9.5 %copy-start.7 = (f32[81,2,640]{2,1,0:T(2,128)}, f32[81,2,640]{2,1,0:T(2,128)S(1)}, u32[]{:S(2)}) copy-start(f32[81,2,640]{2,1,0:T(2,128)S(1)} %collective-permute-done.2.north_in) | copy-start | bytes 1244164
  22.5 25.1 %all-to-all-start = ((f32[32,4,512]{2,1,0:T(4,128)}), f32[32,4,512]{2,1,0:T(4,128)S(1)}, u32[]{:S(2)}, u32[]{:S(2)}) async-start(f32[32,4,512]{2,1,0:T(4,128)} %shard_map.139), calls=%async_computation | async-start | bytes 524288 | tf_op jit(solution)/shard_map/all_to_all | solution.py:648
  32.0 15.7 %copy-start.2 = (s32[1,32,512]{2,1,0:T(8,128)S(1)}, s32[1,32,512]{2,1,0:T(8,128)}, u32[]{:S(2)}) copy-start(s32[1,32,512]{2,1,0:T(8,128)} %param.13) | copy-start | bytes 196612
  47.7 0.9 %copy-start.1 = (f32[5,16,512]{2,1,0:T(8,128)S(1)}, f32[5,16,512]{2,1,0:T(8,128)}, u32[]{:S(2)}) copy-start(f32[5,16,512]{2,1,0:T(8,128)} %get-tuple-element.36.top_ref) | copy-start | bytes 491524
  48.6 17.1 %copy-start.3 = (s32[1,32,512]{2,1,0:T(8,128)S(1)}, s32[1,32,512]{2,1,0:T(8,128)}, u32[]{:S(2)}) copy-start(s32[1,32,512]{2,1,0:T(8,128)} %param.11) | copy-start | bytes 196612
  48.6 17.1 %copy-start.4 = (f32[1,32,512]{2,1,0:T(8,128)S(1)}, f32[1,32,512]{2,1,0:T(8,128)}, u32[]{:S(2)}) copy-start(f32[1,32,512]{2,1,0:T(8,128)} %param.12) | copy-start | bytes 196612
  57.6 0.6 copy-start
  58.3 17.8 %all-to-all-start.1 = ((f32[32,4,512]{2,1,0:T(4,128)}), f32[32,4,512]{2,1,0:T(4,128)S(1)}, u32[]{:S(2)}, u32[]{:S(2)}) async-start(f32[32,4,512]{2,1,0:T(4,128)} %get-tuple-element.42), calls=%async_computation.1 | async-start | bytes 524288 | tf_op jit(solution)/shard_map/all_to_all | solution.py:709

commit v3 on v2

--- a/solution.py
+++ b/solution.py
@@ -18,10 +18,11 @@
 
 
 LANES = 256
-TERMS = 3
+TERMS = 2
 GROUP = 8
 VMEM_BYTES = 60 * 2**20
 SMALL_BYTES = 24 * 2**20
+SIDE_BYTES = 24 * 2**20
 
 
 def cut(values):
@@ -299,9 +300,43 @@
     east_ref[HALO * 4 : HALO * 5, :rows] = east
 
 
-def rows_kernel(t_ref, s_ref, u_ref, v_ref, wet_ref, from_west_ref, from_east_ref,
-                down_ref, up_ref, side_ref):
-    levels, rows, cols = t_ref.shape
+def strip_kernel(t_in, s_in, u_in, v_in, wet_in, down_out, up_out,
+                 field_ref, wet_ref, down_ref, up_ref, in_sem, out_sem):
+    fields, levels, rows, cols = field_ref.shape
+    copies = [
+        pltpu.make_async_copy(source, field_ref.at[f], in_sem.at[f])
+        for f, source in enumerate((t_in, s_in, u_in, v_in))
+    ]
+    copies.append(pltpu.make_async_copy(wet_in, wet_ref, in_sem.at[fields]))
+    for copy in copies:
+        copy.start()
+    leaving = []
+    for f in range(fields + 1):
+        copies[f].wait()
+        if f < fields:
+            span = slice(f * levels, (f + 1) * levels)
+            down_ref[span] = field_ref[f, :, :HALO, :]
+            up_ref[span] = field_ref[f, :, rows - HALO :, :]
+        else:
+            span = slice(fields * levels, fields * levels + 1)
+            wet = wet_ref[...].astype(jnp.float32)
+            down_ref[fields * levels] = wet[:HALO]
+            up_ref[fields * levels] = wet[rows - HALO :]
+        for i, (near, far) in enumerate(((down_ref, down_out), (up_ref, up_out))):
+            copy = pltpu.make_async_copy(
+                near.at[span], far.at[span, :, :cols], out_sem.at[2 * f + i]
+            )
+            copy.start()
+            leaving.append(copy)
+    for copy in leaving:
+        copy.wait()
+
+
+def side_kernel(from_west_ref, from_east_ref, down_in, up_in, down_out, up_out, side_out,
+                side_ref, low_ref, high_ref, sem):
+    channels, rows, _ = side_ref.shape
+    levels = (channels - 1) // 4
+    cols = down_out.shape[2] - EDGE
 
     def turned(f, count):
         return jnp.concatenate(
@@ -313,21 +348,22 @@
             0,
         ).T
 
-    for f, ref in enumerate((t_ref, s_ref, u_ref, v_ref)):
-        span = slice(f * levels, (f + 1) * levels)
-        side = turned(f, levels * rows).reshape(levels, rows, EDGE)
-        side_ref[span] = side
-        down_ref[span, :, :cols] = ref[:, :HALO, :]
-        up_ref[span, :, :cols] = ref[:, rows - HALO :, :]
-        down_ref[span, :, cols:] = side[:, :HALO, :]
-        up_ref[span, :, cols:] = side[:, rows - HALO :, :]
-    side = turned(4, rows)
-    wet = wet_ref[...].astype(jnp.float32)
-    side_ref[4 * levels] = side
-    down_ref[4 * levels, :, :cols] = wet[:HALO]
-    up_ref[4 * levels, :, :cols] = wet[rows - HALO :]
-    down_ref[4 * levels, :, cols:] = side[:HALO]
-    up_ref[4 * levels, :, cols:] = side[rows - HALO :]
+    for f in range(4):
+        side_ref[f * levels : (f + 1) * levels] = turned(f, levels * rows).reshape(
+            levels, rows, EDGE
+        )
+    side_ref[4 * levels] = turned(4, rows)
+    low_ref[...] = side_ref[:, :HALO, :]
+    high_ref[...] = side_ref[:, rows - HALO :, :]
+    copies = [
+        pltpu.make_async_copy(low_ref, down_out.at[:, :, cols:], sem.at[0]),
+        pltpu.make_async_copy(high_ref, up_out.at[:, :, cols:], sem.at[1]),
+        pltpu.make_async_copy(side_ref, side_out, sem.at[2]),
+    ]
+    for copy in copies:
+        copy.start()
+    for copy in copies:
+        copy.wait()
 
 
 def ocean_kernel(total_rows, t_in, s_in, u_in, v_in, wet_in, side_in, north_in, fold_in,
@@ -407,7 +443,7 @@
                 mirror(f * levels + k, 1.0 if f < 2 else -1.0)
             return carry
 
-        lax.fori_loop(0, levels, mirror_level, 0)
+        lax.fori_loop(0, levels, mirror_level, 0, unroll=4)
         mirror(4 * levels, 1.0)
 
     gap = jnp.zeros((8 - 2 * HALO, EDGE), jnp.float32)
@@ -610,15 +646,46 @@
     from_west = lax.ppermute(east, "atm", [(i, (i + 1) % columns) for i in range(columns)])
 
     strip = (4 * levels + 1, HALO, wide)
-    down, up, side = call(
-        rows_kernel,
-        [strip, strip, (4 * levels + 1, block_rows, EDGE)],
-        [],
-        *ocean,
-        wet_mask,
-        from_west,
-        from_east,
-    )
+    far = pl.BlockSpec(memory_space=pltpu.HBM)
+    vmem = pl.BlockSpec(memory_space=pltpu.VMEM)
+    main = (4 * levels + 1, HALO, block_cols)
+    down, up = pl.pallas_call(
+        strip_kernel,
+        out_shape=[jax.ShapeDtypeStruct(strip, jnp.float32)] * 2,
+        in_specs=[far] * 5,
+        out_specs=[far] * 2,
+        scratch_shapes=[
+            pltpu.VMEM((4, *whole), jnp.float32),
+            pltpu.VMEM((block_rows, block_cols), jnp.int32),
+            pltpu.VMEM(main, jnp.float32),
+            pltpu.VMEM(main, jnp.float32),
+            pltpu.SemaphoreType.DMA((5,)),
+            pltpu.SemaphoreType.DMA((10,)),
+        ],
+        compiler_params=pltpu.CompilerParams(vmem_limit_bytes=VMEM_BYTES),
+        cost_estimate=pl.CostEstimate(
+            flops=0, transcendentals=0, bytes_accessed=4 * 6 * temp.size
+        ),
+    )(*ocean, wet_mask)
+    side_shape = (4 * levels + 1, block_rows, EDGE)
+    down, up, side = pl.pallas_call(
+        side_kernel,
+        out_shape=[
+            jax.ShapeDtypeStruct(strip, jnp.float32),
+            jax.ShapeDtypeStruct(strip, jnp.float32),
+            jax.ShapeDtypeStruct(side_shape, jnp.float32),
+        ],
+        in_specs=[vmem] * 2 + [far] * 2,
+        out_specs=[far] * 3,
+        scratch_shapes=[
+            pltpu.VMEM(side_shape, jnp.float32),
+            pltpu.VMEM((4 * levels + 1, HALO, EDGE), jnp.float32),
+            pltpu.VMEM((4 * levels + 1, HALO, EDGE), jnp.float32),
+            pltpu.SemaphoreType.DMA((3,)),
+        ],
+        input_output_aliases={2: 0, 3: 1},
+        compiler_params=pltpu.CompilerParams(vmem_limit_bytes=SIDE_BYTES),
+    )(from_west, from_east, down, up)
     north = lax.ppermute(down, "ocn", [(i + 1, i) for i in range(stripes - 1)])
     south = lax.ppermute(up, "ocn", [(i, i + 1) for i in range(stripes - 1)])
     last = stripes - 1
@@ -655,8 +722,6 @@
         limit=SMALL_BYTES,
         flops=2 * TERMS * up_to(blocks, 16) * LANES * owners * capacity,
     )
-    vmem = pl.BlockSpec(memory_space=pltpu.VMEM)
-    far = pl.BlockSpec(memory_space=pltpu.HBM)
     tall = block_rows + 8
     tiles = wide // EDGE
     plane = (block_rows, block_cols)

time: 80.9 us -> 75.5 us (0.933)
  Pallas kernels: 47.1 us -> 44 us
  waiting for transfers between devices: 6.22 us -> 3.74 us
    pallas_call x7 -> x6, Pallas kernels: 31.5 us -> 24.8 us  [call(): pl.pallas_call(kernel, out_shape=[jax.ShapeDtypeStruct(shape, jnp.float32...]
    pallas_call x0 -> x2, Pallas kernels: none -> 3.54 us  [the longest x1 2.49 us: per_device(): pl.pallas_call(strip_kernel, out_shape=[jax.ShapeDtypeStruct(strip, jnp.f...]
    ppermute x1, waiting for transfers between devices: 1.95 us -> 0.01 us  [per_device(): lax.ppermute(east, 'atm', [(i, (i + 1) % columns) for i in range(columns)])]
    all_to_all x1, starting transfers between devices: 7.41 us -> 6.39 us  [per_device(): lax.all_to_all(leaving, ('atm', 'ocn'), split_axis=0, concat_axis=0, tile...]
    all_to_all x1, starting transfers between devices: 9.42 us -> 10.4 us  [per_device(): lax.all_to_all(outgoing, ('atm', 'ocn'), split_axis=0, concat_axis=0, til...]
    unnamed x20 -> x18, local copies, waits for them, and re-layouts: 2.2 us -> 2.43 us
  transfers between devices with their start and end apart: 7 -> 7, of which waited for: 3 -> 2; matrix products, arithmetic and copies ran while one was open for 0% -> 0% of each run, Pallas kernels for 35% -> 40%
where the time goes in v3:
time: 75.5 us; the launch traced here: 75.1 us
  Pallas kernels  44 us (58%)
  starting transfers between devices  24.1 us (32%)
  waiting for transfers between devices  3.74 us (5%)
  local copies, waits for them, and re-layouts  2.43 us (3%)
  between operations  0.86 us (1%)
    pallas_call x6, Pallas kernels, call(): pl.pallas_call(kernel, out_shape=[jax.ShapeDtypeStruct(shape, jnp.float32...  24.8 us
    pallas_call x1, Pallas kernels, per_device(): pl.pallas_call(functools.partial(ocean_kernel, block_rows * stripes), out...  15.6 us
    all_to_all x1, starting transfers between devices, per_device(): lax.all_to_all(outgoing, ('atm', 'ocn'), split_axis=0, concat_axis=0, til...  10.4 us
    all_to_all x1, starting transfers between devices, per_device(): lax.all_to_all(leaving, ('atm', 'ocn'), split_axis=0, concat_axis=0, tile...  6.39 us
    all_to_all x1, waiting for transfers between devices, per_device(): lax.all_to_all(leaving, ('atm', 'ocn'), split_axis=0, concat_axis=0, tile...  3.22 us
    ppermute x1, starting transfers between devices, per_device(): lax.ppermute(east, 'atm', [(i, (i + 1) % columns) for i in range(columns)])  2.99 us
    pallas_call x1, Pallas kernels, per_device(): pl.pallas_call(strip_kernel, out_shape=[jax.ShapeDtypeStruct(strip, jnp.f...  2.49 us
    unnamed x18, local copies, waits for them, and re-layouts  2.43 us
  transfers between devices with their start and end apart: 7, of which 2 were waited for; matrix products, arithmetic and copies ran while one was open for 0% of the time, Pallas kernels for 40%

profile of v3, /device:TPU:0, one launch (start us, length us, event | category | flops | bytes accessed | tf_op | source)
XLA Modules:
  0.0 75.1 jit_solution(2481123645177531938)
XLA Ops:
  0.6 2.4 %shard_map.137 = (f32[10,320]{1,0:T(8,128)}, f32[10,320]{1,0:T(8,128)}) custom-call(f32[20,16,512]{2,1,0:T(8,128)} %t_in.3, f32[20,16,512]{2,1,0:T(8,128)} %s_in.3, f32[20,16,512]{2,1,0:T(8,128)} %u_in.3, f32[20,16,512]{2,1,0:T(8,128)} %v_in.3, s32[16,512]{1,0:T(8,128)} %wet_in.3), custom_call_target="tpu_custom_call" | custom-call | bytes 2679808 | tf_op jit(solution)/shard_map/pallas_call | solution.py:246
  3.0 3.0 %collective-permute-start = (f32[10,320]{1,0:T(8,128)}, f32[10,320]{1,0:T(8,128)S(1)}, u32[]{:S(2)}, u32[]{:S(2)}) collective-permute-start(f32[10,320]{1,0:T(8,128)} %get-tuple-element.26), channel_id=1, source_target_pairs={{0,8},{8,16},{16,24},{24,0},{1,9},{9,17},{17,25},{25,1},{2,10},{10... | collective-permute-start | bytes 38408 | tf_op jit(solution)/shard_map/ppermute | solution.py:646
  6.0 1.0 %collective-permute-start.1 = (f32[10,320]{1,0:T(8,128)}, f32[10,320]{1,0:T(8,128)S(1)}, u32[]{:S(2)}, u32[]{:S(2)}) collective-permute-start(f32[10,320]{1,0:T(8,128)} %get-tuple-element.27), channel_id=1, source_target_pairs={{8,0},{16,8},{24,16},{0,24},{9,1},{17,9},{25,17},{1,25},{10,2},{18... | collective-permute-start | bytes 38408 | tf_op jit(solution)/shard_map/ppermute | solution.py:645
  7.0 2.5 %shard_map.138 = (f32[81,2,640]{2,1,0:T(2,128)}, f32[81,2,640]{2,1,0:T(2,128)}) custom-call(f32[20,16,512]{2,1,0:T(8,128)} %t_in.3, f32[20,16,512]{2,1,0:T(8,128)} %s_in.3, f32[20,16,512]{2,1,0:T(8,128)} %u_in.3, f32[20,16,512]{2,1,0:T(8,128)} %v_in.3, s32[16,512]{1,0:T(8,128)} %wet_in.3), custom_call_target="tpu_custom_call" | custom-call | bytes 3932160 | tf_op jit(solution)/shard_map/pallas_call | solution.py:652
  9.5 0.0 collective-permute-done.from_west_ref
  9.5 0.5 collective-permute-done.1.from_east_ref
  10.0 1.0 %shard_map.139 = (f32[81,2,640]{2,1,0:T(2,128)}, f32[81,2,640]{2,1,0:T(2,128)}, f32[81,16,128]{2,1,0:T(8,128)S(1)}) custom-call(f32[10,320]{1,0:T(8,128)S(1)} %collective-permute-done.from_west_ref, f32[10,320]{1,0:T(8,128)S(1)} %collective-permute-done.1.from_east_ref, ...), custom_call_target="tpu_custom_call", output_to_operand_aliasing={{0}: (2, {}), {1}: (3, {})} | custom-call | tf_op jit(solution)/shard_map/pallas_call | solution.py:671
  11.1 0.0 copy-start
  11.1 0.8 %copy-done = f32[81,16,128]{2,1,0:T(8,128)} copy-done((f32[81,16,128]{2,1,0:T(8,128)}, f32[81,16,128]{2,1,0:T(8,128)S(1)}, u32[]{:S(2)}) %copy-start) | copy-done | bytes 663576
  11.9 1.3 %collective-permute-start.3 = (f32[81,2,640]{2,1,0:T(2,128)}, f32[81,2,640]{2,1,0:T(2,128)S(1)}, u32[]{:S(2)}, u32[]{:S(2)}) collective-permute-start(f32[81,2,640]{2,1,0:T(2,128)} %get-tuple-element.32), channel_id=1, source_target_pairs={{0,1},{1,2},{2,3},{3,4},{4,5},{5,6},{6,7},{8,9},{9,10},{10,11},{11... | collective-permute-start | bytes 1244168 | tf_op jit(solution)/shard_map/ppermute | solution.py:690
  13.2 0.7 collective-permute-start.4
  13.9 1.3 %collective-permute-start.2 = (f32[81,2,640]{2,1,0:T(2,128)}, f32[81,2,640]{2,1,0:T(2,128)S(1)}, u32[]{:S(2)}, u32[]{:S(2)}) collective-permute-start(f32[81,2,640]{2,1,0:T(2,128)} %get-tuple-element.31), channel_id=1, source_target_pairs={{1,0},{2,1},{3,2},{4,3},{5,4},{6,5},{7,6},{9,8},{10,9},{11,10},{12... | collective-permute-start | bytes 1244168 | tf_op jit(solution)/shard_map/ppermute | solution.py:689
  15.2 4.4 %shard_map.140 = f32[32,4,512]{2,1,0:T(4,128)} custom-call(f32[8,6912]{1,0:T(8,128)} %flux_in.1, s32[32,512]{1,0:T(8,128)} %bitcast.4, f32[32,512]{1,0:T(8,128)} %bitcast.7), custom_call_target="tpu_custom_call" | custom-call | flops 1879048192 | bytes 614400 | tf_op jit(solution)/shard_map/pallas_call | solution.py:246
  19.7 0.0 collective-permute-done.3.south_in
  19.7 0.0 copy-start.6
  19.7 0.0 collective-permute-done.4.fold_in
  19.7 0.0 copy-start.7
  19.7 0.0 collective-permute-done.2.north_in
  19.7 0.0 copy-start.8
  19.8 10.4 %all-to-all-start = ((f32[32,4,512]{2,1,0:T(4,128)}), f32[32,4,512]{2,1,0:T(4,128)S(1)}, u32[]{:S(2)}, u32[]{:S(2)}) async-start(f32[32,4,512]{2,1,0:T(4,128)} %shard_map.140), calls=%async_computation | async-start | bytes 524288 | tf_op jit(solution)/shard_map/all_to_all | solution.py:715
  30.2 0.0 copy-start.3
  30.2 0.0 copy-done.6
  30.2 0.0 copy-done.7
  30.2 0.0 copy-done.8
  30.2 15.6 %shard_map.141 = (f32[20,4,16,512]{3,2,1,0:T(8,128)}, f32[20,16,512]{2,1,0:T(8,128)}, f32[20,16,512]{2,1,0:T(8,128)}, f32[5,16,512]{2,1,0:T(8,128)}) custom-call(f32[20,16,512]{2,1,0:T(8,128)} %t_in.3, f32[20,16,512]{2,1,0:T(8,128)} %s_in.3, f32[20,16,512]{2,1,0:T(8,128)} %u_in.3, f32[20,16,512]{2,1,0:T(8,128)} %v_in.3, s32[16,512]{1,0:T(8,128)} %wet_in.3, ...), custom_call_target="tpu_custom_call" | custom-call | flops 104857600 | bytes 8519680 | tf_op jit(solution)/shard_map/pallas_call | solution.py:729
  45.8 0.0 all-to-all-done.come_ref
  45.8 0.0 copy-done.3
  45.8 0.0 copy-start.2
  45.9 0.9 %copy-done.2 = f32[5,16,512]{2,1,0:T(8,128)S(1)} copy-done((f32[5,16,512]{2,1,0:T(8,128)S(1)}, f32[5,16,512]{2,1,0:T(8,128)}, u32[]{:S(2)}) %copy-start.2) | copy-done | bytes 163864
  46.8 0.0 copy-start.4
  46.8 0.0 copy-start.5
  46.8 6.9 %shard_map.142 = (f32[4,16,512]{2,1,0:T(8,128)S(1)}, f32[32,4,512]{2,1,0:T(4,128)}) custom-call(f32[32,4,512]{2,1,0:T(4,128)S(1)} %all-to-all-done.come_ref, s32[32,512]{1,0:T(8,128)S(1)} %bitcast.3, f32[5,16,512]{2,1,0:T(8,128)S(1)} %copy-done.2), custom_call_target="tpu_custom_call" | custom-call | flops 4294967296 | bytes 884736 | tf_op jit(solution)/shard_map/pallas_call | solution.py:246
  53.7 0.0 copy-start.1
  53.7 0.6 copy-done.1
  54.3 6.4 %all-to-all-start.1 = ((f32[32,4,512]{2,1,0:T(4,128)}), f32[32,4,512]{2,1,0:T(4,128)S(1)}, u32[]{:S(2)}, u32[]{:S(2)}) async-start(f32[32,4,512]{2,1,0:T(4,128)} %get-tuple-element.46), calls=%async_computation.1 | async-start | bytes 524288 | tf_op jit(solution)/shard_map/all_to_all | solution.py:774
  60.7 0.0 copy-done.4
  60.7 0.0 copy-done.5
  60.7 3.1 %shard_map.144.inverse_ref = f32[32,256]{1,0:T(8,128)S(1)} custom-call(s32[32,512]{1,0:T(8,128)S(1)} %bitcast.5, f32[32,512]{1,0:T(8,128)S(1)} %bitcast.8), custom_call_target="tpu_custom_call" | custom-call | flops 536870912 | bytes 163840 | tf_op jit(solution)/shard_map/pallas_call | solution.py:246
  63.8 4.0 %shard_map.143 = (f32[20,16,512]{2,1,0:T(8,128)}, f32[20,16,512]{2,1,0:T(8,128)}, f32[20,16,512]{2,1,0:T(8,128)}, f32[20,16,512]{2,1,0:T(8,128)}) custom-call(f32[20,4,16,512]{3,2,1,0:T(8,128)} %get-tuple-element.36.part_ref, f32[20,16,512]{2,1,0:T(8,128)} %get-tuple-element.37.factor_ref, f32[20,16,512]{2,1,0:T(8,128)} %get-tuple-element.38.reply_ref, ...), custom_call_target="tpu_custom_call" | custom-call | bytes 6684672 | tf_op jit(solution)/shard_map/pallas_call | solution.py:246
  67.9 3.2 %all-to-all-done.1.come_ref = f32[32,4,512]{2,1,0:T(4,128)S(1)} async-done(((f32[32,4,512]{2,1,0:T(4,128)}), f32[32,4,512]{2,1,0:T(4,128)S(1)}, u32[]{:S(2)}, u32[]{:S(2)}) %all-to-all-start.1) | async-done | bytes 262176 | tf_op jit(solution)/shard_map/all_to_all | solution.py:774
  71.1 4.0 %shard_map.145 = f32[4,6912]{1,0:T(4,128)} custom-call(f32[32,4,512]{2,1,0:T(4,128)S(1)} %all-to-all-done.1.come_ref, s32[32,512]{1,0:T(8,128)S(1)} %bitcast.6, f32[32,512]{1,0:T(8,128)S(1)} %bitcast.9, f32[32,256]{1,0:T(8,128)S(1)} %shard_map.144.inverse_ref), custom_call_target="tpu_custom_call" | custom-call | flops 1879048192 | bytes 536576 | tf_op jit(solution)/shard_map/pallas_call | solution.py:246
Async XLA Ops:
  3.0 6.5 %collective-permute-start = (f32[10,320]{1,0:T(8,128)}, f32[10,320]{1,0:T(8,128)S(1)}, u32[]{:S(2)}, u32[]{:S(2)}) collective-permute-start(f32[10,320]{1,0:T(8,128)} %get-tuple-element.26), channel_id=1, source_target_pairs={{0,8},{8,16},{16,24},{24,0},{1,9},{9,17},{17,25},{25,1},{2,10},{10... | collective-permute-start | bytes 38408 | tf_op jit(solution)/shard_map/ppermute | solution.py:646
  6.0 4.0 %collective-permute-start.1 = (f32[10,320]{1,0:T(8,128)}, f32[10,320]{1,0:T(8,128)S(1)}, u32[]{:S(2)}, u32[]{:S(2)}) collective-permute-start(f32[10,320]{1,0:T(8,128)} %get-tuple-element.27), channel_id=1, source_target_pairs={{8,0},{16,8},{24,16},{0,24},{9,1},{17,9},{25,17},{1,25},{10,2},{18... | collective-permute-start | bytes 38408 | tf_op jit(solution)/shard_map/ppermute | solution.py:645
  11.1 0.8 %copy-start = (f32[81,16,128]{2,1,0:T(8,128)}, f32[81,16,128]{2,1,0:T(8,128)S(1)}, u32[]{:S(2)}) copy-start(f32[81,16,128]{2,1,0:T(8,128)S(1)} %get-tuple-element.30.side_in) | copy-start | bytes 1990660
  11.9 7.8 %collective-permute-start.3 = (f32[81,2,640]{2,1,0:T(2,128)}, f32[81,2,640]{2,1,0:T(2,128)S(1)}, u32[]{:S(2)}, u32[]{:S(2)}) collective-permute-start(f32[81,2,640]{2,1,0:T(2,128)} %get-tuple-element.32), channel_id=1, source_target_pairs={{0,1},{1,2},{2,3},{3,4},{4,5},{5,6},{6,7},{8,9},{9,10},{10,11},{11... | collective-permute-start | bytes 1244168 | tf_op jit(solution)/shard_map/ppermute | solution.py:690
  13.2 6.5 %collective-permute-start.4 = (f32[81,2,640]{2,1,0:T(2,128)}, f32[81,2,640]{2,1,0:T(2,128)S(1)}, u32[]{:S(2)}, u32[]{:S(2)}) collective-permute-start(f32[81,2,640]{2,1,0:T(2,128)} %get-tuple-element.32), channel_id=1, source_target_pairs={{7,31},{15,23},{23,15},{31,7}} | collective-permute-start | bytes 1244168 | tf_op jit(solution)/shard_map/ppermute | solution.py:692
  13.9 5.8 %collective-permute-start.2 = (f32[81,2,640]{2,1,0:T(2,128)}, f32[81,2,640]{2,1,0:T(2,128)S(1)}, u32[]{:S(2)}, u32[]{:S(2)}) collective-permute-start(f32[81,2,640]{2,1,0:T(2,128)} %get-tuple-element.31), channel_id=1, source_target_pairs={{1,0},{2,1},{3,2},{4,3},{5,4},{6,5},{7,6},{9,8},{10,9},{11,10},{12... | collective-permute-start | bytes 1244168 | tf_op jit(solution)/shard_map/ppermute | solution.py:689
  19.7 10.5 %copy-start.6 = (f32[81,2,640]{2,1,0:T(2,128)}, f32[81,2,640]{2,1,0:T(2,128)S(1)}, u32[]{:S(2)}) copy-start(f32[81,2,640]{2,1,0:T(2,128)S(1)} %collective-permute-done.3.south_in) | copy-start | bytes 1244164
  19.7 10.5 %copy-start.7 = (f32[81,2,640]{2,1,0:T(2,128)}, f32[81,2,640]{2,1,0:T(2,128)S(1)}, u32[]{:S(2)}) copy-start(f32[81,2,640]{2,1,0:T(2,128)S(1)} %collective-permute-done.4.fold_in) | copy-start | bytes 1244164
  19.7 10.4 %copy-start.8 = (f32[81,2,640]{2,1,0:T(2,128)}, f32[81,2,640]{2,1,0:T(2,128)S(1)}, u32[]{:S(2)}) copy-start(f32[81,2,640]{2,1,0:T(2,128)S(1)} %collective-permute-done.2.north_in) | copy-start | bytes 1244164
  19.8 26.1 %all-to-all-start = ((f32[32,4,512]{2,1,0:T(4,128)}), f32[32,4,512]{2,1,0:T(4,128)S(1)}, u32[]{:S(2)}, u32[]{:S(2)}) async-start(f32[32,4,512]{2,1,0:T(4,128)} %shard_map.140), calls=%async_computation | async-start | bytes 524288 | tf_op jit(solution)/shard_map/all_to_all | solution.py:715
  30.2 15.7 %copy-start.3 = (s32[1,32,512]{2,1,0:T(8,128)S(1)}, s32[1,32,512]{2,1,0:T(8,128)}, u32[]{:S(2)}) copy-start(s32[1,32,512]{2,1,0:T(8,128)} %param.13) | copy-start | bytes 196612
  45.8 0.9 %copy-start.2 = (f32[5,16,512]{2,1,0:T(8,128)S(1)}, f32[5,16,512]{2,1,0:T(8,128)}, u32[]{:S(2)}) copy-start(f32[5,16,512]{2,1,0:T(8,128)} %get-tuple-element.40.top_ref) | copy-start | bytes 491524
  46.8 14.0 %copy-start.4 = (s32[1,32,512]{2,1,0:T(8,128)S(1)}, s32[1,32,512]{2,1,0:T(8,128)}, u32[]{:S(2)}) copy-start(s32[1,32,512]{2,1,0:T(8,128)} %param.11) | copy-start | bytes 196612
  46.8 14.0 %copy-start.5 = (f32[1,32,512]{2,1,0:T(8,128)S(1)}, f32[1,32,512]{2,1,0:T(8,128)}, u32[]{:S(2)}) copy-start(f32[1,32,512]{2,1,0:T(8,128)} %param.12) | copy-start | bytes 196612
  53.7 0.6 copy-start.1
  54.3 16.8 %all-to-all-start.1 = ((f32[32,4,512]{2,1,0:T(4,128)}), f32[32,4,512]{2,1,0:T(4,128)S(1)}, u32[]{:S(2)}, u32[]{:S(2)}) async-start(f32[32,4,512]{2,1,0:T(4,128)} %get-tuple-element.46), calls=%async_computation.1 | async-start | bytes 524288 | tf_op jit(solution)/shard_map/all_to_all | solution.py:774

commit v4 on v3

--- a/solution.py
+++ b/solution.py
@@ -370,7 +370,7 @@
                  south_in, mix_in, part_out, factor_out, reply_out, top_ref,
                  t_ref, s_ref, u_ref, v_ref, wet_ref, side_ref, north_ref, fold_ref, south_ref,
                  mix_ref, part_ref, scale_ref, factor_ref, reply_ref, east_gate, north_gate,
-                 turn_ref, state_ref, middle_ref, before_ref, in_sem, out_sem):
+                 turn_ref, state_ref, middle_ref, keep_ref, solve_ref, before_ref, in_sem, level_sem, out_sem):
     levels, rows, cols = t_ref.shape
     tall = rows + 8
     tiles = cols // EDGE
@@ -385,17 +385,30 @@
                 (wet_in, wet_ref),
                 (north_in, north_ref),
                 (south_in, south_ref),
-                (fold_in, fold_ref),
                 (side_in, side_ref),
-                (t_in, t_ref),
-                (s_in, s_ref),
-                (u_in, u_ref),
-                (v_in, v_ref),
             )
         )
     ]
-    for copy in copies:
+    fold_copy = pltpu.make_async_copy(fold_in, fold_ref, in_sem.at[5])
+    for copy in copies[:4]:
         copy.start()
+
+    @pl.when(on_top)
+    def _():
+        fold_copy.start()
+
+    copies[4].start()
+
+    def field_copy(f, k):
+        source, target = ((t_in, t_ref), (s_in, s_ref), (u_in, u_ref), (v_in, v_ref))[f]
+        return pltpu.make_async_copy(source.at[k], target.at[k], level_sem.at[f, k])
+
+    def fetch(k, carry):
+        for f in range(4):
+            field_copy(f, k).start()
+        return carry
+
+    lax.fori_loop(0, levels, fetch, 0)
 
     copies[0].wait()
     above = jnp.zeros((rows, cols), jnp.float32)
@@ -426,6 +439,7 @@
 
     @pl.when(on_top)
     def _():
+        fold_copy.wait()
         flip = EDGE - 1 - lax.broadcasted_iota(jnp.int32, (8, EDGE), 1)
         order = list(range(tiles))[::-1] + [tiles]
         blank = jnp.zeros((8 - HALO, EDGE), jnp.float32)
@@ -487,7 +501,7 @@
         ring(north_gate.at[j], north[:rows], north[rows:])
         turn_ref[j] = turn * wet
 
-    def substep(source, order, height, put):
+    def substep(source, closed, height, put):
         def rolled(j):
             return [ahead(source[f, j, 8 : 8 + height]) for f in range(4)]
 
@@ -499,13 +513,19 @@
                 for f in range(4)
             ]
 
-        here = rolled(order[0])
-        passed = [behind(x) for x in eastward(order[-1], rolled(order[-1]), here)]
-        for j in order[:-1]:
-            after = rolled((j + 1) % count)
-            east = eastward(j, here, after)
+        here = rolled(0)
+        side = rolled(tiles)
+        side_east = eastward(tiles, side, here)
+        passed = [behind(x) for x in side_east]
+        for j in range(count if closed else tiles):
+            if j < tiles:
+                after = rolled(j + 1) if j + 1 < tiles else side
+                east = eastward(j, here, after)
+            else:
+                after, east = None, side_east
             here = after
-            before, passed = passed, [behind(x) for x in east]
+            before = passed
+            passed = [behind(x) for x in east]
             west = [jnp.where(first[:height], p, q) for p, q in zip(before, passed)]
             north_open = north_gate[j, 8 : 8 + height]
             south_open = north_gate[j, 7 : 7 + height]
@@ -542,34 +562,44 @@
                 )
 
     def level(k, carry):
+        for f in range(4):
+            field_copy(f, k).wait()
         for f, ref in enumerate((t_ref, s_ref, u_ref, v_ref)):
             channel = f * levels + k
-            for j, span in enumerate(spans):
-                ring(
-                    state_ref.at[f, j],
+            parts = [
+                (
                     ref[k, :, span] if j < tiles else side_ref[channel],
                     beyond(channel, span),
                 )
-
+                for j, span in enumerate(spans)
+            ]
+            for j in range(count):
+                ring(state_ref.at[f, j], *parts[j])
         def put_middle(f, j, value):
-            middle_ref[k, f, j, 8 : 8 + tall] = value
-            middle_ref[k, f, j, 0:8] = value[rows:]
-
-        substep(state_ref, [tiles] + list(range(tiles)) + [tiles - 1], tall, put_middle)
+            middle_ref[f, j, 8 : 8 + tall] = value
+            middle_ref[f, j, 0:8] = value[rows:]
+
+        substep(state_ref, True, tall, put_middle)
+        for f in range(4):
+            keep_ref[k, f] = middle_ref[f, :, : 8 + tall]
         return carry
 
     def last_level(k, carry):
         before = jnp.maximum(k - 1, 0)
-        start = jnp.where(k > 0, 1.0, 0.0)
+        above, scale = mix_ref[before], scale_ref[k]
+        for f in range(4):
+            middle_ref[f, :, : 8 + tall] = keep_ref[k, f]
+        solve_ref[0] = jnp.where(k > 0, 1.0, 0.0) * above
+        solve_ref[1] = scale
 
         def put_part(f, j, value):
             span = spans[j]
-            above = start * mix_ref[before, :, span]
-            value = (value + above * before_ref[f, :, span]) * scale_ref[k, :, span]
-            before_ref[f, :, span] = value
-            part_ref[k, f, :, span] = value
-
-        substep(middle_ref.at[k], list(range(tiles)) + [tiles], rows, put_part)
+            before_ref[f, :, span] = (
+                value + solve_ref[0, :, span] * before_ref[f, :, span]
+            ) * solve_ref[1, :, span]
+
+        substep(middle_ref, False, rows, put_part)
+        part_ref[k] = before_ref[...]
         pltpu.make_async_copy(part_ref.at[k], part_out.at[k], out_sem.at[0]).start()
         return carry
 
@@ -747,9 +777,12 @@
             pltpu.VMEM((tiles, tall + 16, EDGE), jnp.float32),
             pltpu.VMEM((tiles, tall, EDGE), jnp.float32),
             pltpu.VMEM((4, tiles, tall + 16, EDGE), jnp.float32),
-            pltpu.VMEM((levels, 4, tiles, tall + 16, EDGE), jnp.float32),
+            pltpu.VMEM((4, tiles, tall + 16, EDGE), jnp.float32),
+            pltpu.VMEM((levels, 4, tiles, tall + 8, EDGE), jnp.float32),
+            pltpu.VMEM((2, *plane), jnp.float32),
             pltpu.VMEM((4, *plane), jnp.float32),
-            pltpu.SemaphoreType.DMA((10,)),
+            pltpu.SemaphoreType.DMA((6,)),
+            pltpu.SemaphoreType.DMA((4, levels)),
             pltpu.SemaphoreType.DMA((3,)),
         ],
         compiler_params=pltpu.CompilerParams(vmem_limit_bytes=VMEM_BYTES),

time: 75.5 us -> 73.7 us (0.976)
  Pallas kernels: 44 us -> 42.1 us
    pallas_call x1, Pallas kernels: 15.6 us -> 13.7 us  [per_device(): pl.pallas_call(functools.partial(ocean_kernel, block_rows * stripes), out...]
  transfers between devices with their start and end apart: 7 -> 7, of which waited for: 2 -> 2; matrix products, arithmetic and copies ran while one was open for 0% -> 0% of each run, Pallas kernels for 40% -> 38%
where the time goes in v4:
time: 73.7 us; the launch traced here: 73.3 us
  Pallas kernels  42.1 us (57%)
  starting transfers between devices  24.2 us (33%)
  waiting for transfers between devices  3.74 us (5%)
  local copies, waits for them, and re-layouts  2.43 us (3%)
  between operations  0.86 us (1%)
    pallas_call x6, Pallas kernels, call(): pl.pallas_call(kernel, out_shape=[jax.ShapeDtypeStruct(shape, jnp.float32...  24.8 us
    pallas_call x1, Pallas kernels, per_device(): pl.pallas_call(functools.partial(ocean_kernel, block_rows * stripes), out...  13.7 us
    all_to_all x1, starting transfers between devices, per_device(): lax.all_to_all(outgoing, ('atm', 'ocn'), split_axis=0, concat_axis=0, til...  10.4 us
    all_to_all x1, starting transfers between devices, per_device(): lax.all_to_all(leaving, ('atm', 'ocn'), split_axis=0, concat_axis=0, tile...  6.55 us
    all_to_all x1, waiting for transfers between devices, per_device(): lax.all_to_all(leaving, ('atm', 'ocn'), split_axis=0, concat_axis=0, tile...  3.22 us
    ppermute x1, starting transfers between devices, per_device(): lax.ppermute(east, 'atm', [(i, (i + 1) % columns) for i in range(columns)])  2.99 us
    pallas_call x1, Pallas kernels, per_device(): pl.pallas_call(strip_kernel, out_shape=[jax.ShapeDtypeStruct(strip, jnp.f...  2.49 us
    unnamed x18, local copies, waits for them, and re-layouts  2.43 us
  transfers between devices with their start and end apart: 7, of which 2 were waited for; matrix products, arithmetic and copies ran while one was open for 0% of the time, Pallas kernels for 38%

profile of v4, /device:TPU:0, one launch (start us, length us, event | category | flops | bytes accessed | tf_op | source)
XLA Modules:
  0.0 73.3 jit_solution(17458854208057174236)
XLA Ops:
  0.6 2.4 %shard_map.137 = (f32[10,320]{1,0:T(8,128)}, f32[10,320]{1,0:T(8,128)}) custom-call(f32[20,16,512]{2,1,0:T(8,128)} %t_in.3, f32[20,16,512]{2,1,0:T(8,128)} %s_in.3, f32[20,16,512]{2,1,0:T(8,128)} %u_in.3, f32[20,16,512]{2,1,0:T(8,128)} %v_in.3, s32[16,512]{1,0:T(8,128)} %wet_in.3), custom_call_target="tpu_custom_call" | custom-call | bytes 2679808 | tf_op jit(solution)/shard_map/pallas_call | solution.py:246
  3.0 3.0 %collective-permute-start = (f32[10,320]{1,0:T(8,128)}, f32[10,320]{1,0:T(8,128)S(1)}, u32[]{:S(2)}, u32[]{:S(2)}) collective-permute-start(f32[10,320]{1,0:T(8,128)} %get-tuple-element.26), channel_id=1, source_target_pairs={{0,8},{8,16},{16,24},{24,0},{1,9},{9,17},{17,25},{25,1},{2,10},{10... | collective-permute-start | bytes 38408 | tf_op jit(solution)/shard_map/ppermute | solution.py:676
  6.0 1.0 %collective-permute-start.1 = (f32[10,320]{1,0:T(8,128)}, f32[10,320]{1,0:T(8,128)S(1)}, u32[]{:S(2)}, u32[]{:S(2)}) collective-permute-start(f32[10,320]{1,0:T(8,128)} %get-tuple-element.27), channel_id=1, source_target_pairs={{8,0},{16,8},{24,16},{0,24},{9,1},{17,9},{25,17},{1,25},{10,2},{18... | collective-permute-start | bytes 38408 | tf_op jit(solution)/shard_map/ppermute | solution.py:675
  7.0 2.5 %shard_map.138 = (f32[81,2,640]{2,1,0:T(2,128)}, f32[81,2,640]{2,1,0:T(2,128)}) custom-call(f32[20,16,512]{2,1,0:T(8,128)} %t_in.3, f32[20,16,512]{2,1,0:T(8,128)} %s_in.3, f32[20,16,512]{2,1,0:T(8,128)} %u_in.3, f32[20,16,512]{2,1,0:T(8,128)} %v_in.3, s32[16,512]{1,0:T(8,128)} %wet_in.3), custom_call_target="tpu_custom_call" | custom-call | bytes 3932160 | tf_op jit(solution)/shard_map/pallas_call | solution.py:682
  9.5 0.0 collective-permute-done.from_west_ref
  9.5 0.5 collective-permute-done.1.from_east_ref
  10.0 1.0 %shard_map.139 = (f32[81,2,640]{2,1,0:T(2,128)}, f32[81,2,640]{2,1,0:T(2,128)}, f32[81,16,128]{2,1,0:T(8,128)S(1)}) custom-call(f32[10,320]{1,0:T(8,128)S(1)} %collective-permute-done.from_west_ref, f32[10,320]{1,0:T(8,128)S(1)} %collective-permute-done.1.from_east_ref, ...), custom_call_target="tpu_custom_call", output_to_operand_aliasing={{0}: (2, {}), {1}: (3, {})} | custom-call | tf_op jit(solution)/shard_map/pallas_call | solution.py:701
  11.1 0.0 copy-start
  11.1 0.8 %copy-done = f32[81,16,128]{2,1,0:T(8,128)} copy-done((f32[81,16,128]{2,1,0:T(8,128)}, f32[81,16,128]{2,1,0:T(8,128)S(1)}, u32[]{:S(2)}) %copy-start) | copy-done | bytes 663576
  11.9 1.3 %collective-permute-start.3 = (f32[81,2,640]{2,1,0:T(2,128)}, f32[81,2,640]{2,1,0:T(2,128)S(1)}, u32[]{:S(2)}, u32[]{:S(2)}) collective-permute-start(f32[81,2,640]{2,1,0:T(2,128)} %get-tuple-element.32), channel_id=1, source_target_pairs={{0,1},{1,2},{2,3},{3,4},{4,5},{5,6},{6,7},{8,9},{9,10},{10,11},{11... | collective-permute-start | bytes 1244168 | tf_op jit(solution)/shard_map/ppermute | solution.py:720
  13.2 0.7 collective-permute-start.4
  13.9 1.3 %collective-permute-start.2 = (f32[81,2,640]{2,1,0:T(2,128)}, f32[81,2,640]{2,1,0:T(2,128)S(1)}, u32[]{:S(2)}, u32[]{:S(2)}) collective-permute-start(f32[81,2,640]{2,1,0:T(2,128)} %get-tuple-element.31), channel_id=1, source_target_pairs={{1,0},{2,1},{3,2},{4,3},{5,4},{6,5},{7,6},{9,8},{10,9},{11,10},{12... | collective-permute-start | bytes 1244168 | tf_op jit(solution)/shard_map/ppermute | solution.py:719
  15.2 4.4 %shard_map.140 = f32[32,4,512]{2,1,0:T(4,128)} custom-call(f32[8,6912]{1,0:T(8,128)} %flux_in.1, s32[32,512]{1,0:T(8,128)} %bitcast.4, f32[32,512]{1,0:T(8,128)} %bitcast.7), custom_call_target="tpu_custom_call" | custom-call | flops 1879048192 | bytes 614400 | tf_op jit(solution)/shard_map/pallas_call | solution.py:246
  19.7 0.0 collective-permute-done.3.south_in
  19.7 0.0 copy-start.6
  19.7 0.0 collective-permute-done.4.fold_in
  19.7 0.0 copy-start.7
  19.7 0.0 collective-permute-done.2.north_in
  19.7 0.0 copy-start.8
  19.8 10.4 %all-to-all-start = ((f32[32,4,512]{2,1,0:T(4,128)}), f32[32,4,512]{2,1,0:T(4,128)S(1)}, u32[]{:S(2)}, u32[]{:S(2)}) async-start(f32[32,4,512]{2,1,0:T(4,128)} %shard_map.140), calls=%async_computation | async-start | bytes 524288 | tf_op jit(solution)/shard_map/all_to_all | solution.py:745
  30.2 0.0 copy-start.3
  30.2 0.0 copy-done.6
  30.2 0.0 copy-done.7
  30.2 0.0 copy-done.8
  30.2 13.7 %shard_map.141 = (f32[20,4,16,512]{3,2,1,0:T(8,128)}, f32[20,16,512]{2,1,0:T(8,128)}, f32[20,16,512]{2,1,0:T(8,128)}, f32[5,16,512]{2,1,0:T(8,128)}) custom-call(f32[20,16,512]{2,1,0:T(8,128)} %t_in.3, f32[20,16,512]{2,1,0:T(8,128)} %s_in.3, f32[20,16,512]{2,1,0:T(8,128)} %u_in.3, f32[20,16,512]{2,1,0:T(8,128)} %v_in.3, s32[16,512]{1,0:T(8,128)} %wet_in.3, ...), custom_call_target="tpu_custom_call" | custom-call | flops 104857600 | bytes 8519680 | tf_op jit(solution)/shard_map/pallas_call | solution.py:759
  43.9 0.0 all-to-all-done.come_ref
  44.0 0.0 copy-done.3
  44.0 0.0 copy-start.2
  44.0 0.9 %copy-done.2 = f32[5,16,512]{2,1,0:T(8,128)S(1)} copy-done((f32[5,16,512]{2,1,0:T(8,128)S(1)}, f32[5,16,512]{2,1,0:T(8,128)}, u32[]{:S(2)}) %copy-start.2) | copy-done | bytes 163864
  44.9 0.0 copy-start.4
  44.9 0.0 copy-start.5
  44.9 6.9 %shard_map.142 = (f32[4,16,512]{2,1,0:T(8,128)S(1)}, f32[32,4,512]{2,1,0:T(4,128)}) custom-call(f32[32,4,512]{2,1,0:T(4,128)S(1)} %all-to-all-done.come_ref, s32[32,512]{1,0:T(8,128)S(1)} %bitcast.3, f32[5,16,512]{2,1,0:T(8,128)S(1)} %copy-done.2), custom_call_target="tpu_custom_call" | custom-call | flops 4294967296 | bytes 884736 | tf_op jit(solution)/shard_map/pallas_call | solution.py:246
  51.8 0.0 copy-start.1
  51.8 0.6 copy-done.1
  52.4 6.5 %all-to-all-start.1 = ((f32[32,4,512]{2,1,0:T(4,128)}), f32[32,4,512]{2,1,0:T(4,128)S(1)}, u32[]{:S(2)}, u32[]{:S(2)}) async-start(f32[32,4,512]{2,1,0:T(4,128)} %get-tuple-element.46), calls=%async_computation.1 | async-start | bytes 524288 | tf_op jit(solution)/shard_map/all_to_all | solution.py:807
  59.0 0.0 copy-done.4
  59.0 0.0 copy-done.5
  59.0 3.1 %shard_map.144.inverse_ref = f32[32,256]{1,0:T(8,128)S(1)} custom-call(s32[32,512]{1,0:T(8,128)S(1)} %bitcast.5, f32[32,512]{1,0:T(8,128)S(1)} %bitcast.8), custom_call_target="tpu_custom_call" | custom-call | flops 536870912 | bytes 163840 | tf_op jit(solution)/shard_map/pallas_call | solution.py:246
  62.1 4.0 %shard_map.143 = (f32[20,16,512]{2,1,0:T(8,128)}, f32[20,16,512]{2,1,0:T(8,128)}, f32[20,16,512]{2,1,0:T(8,128)}, f32[20,16,512]{2,1,0:T(8,128)}) custom-call(f32[20,4,16,512]{3,2,1,0:T(8,128)} %get-tuple-element.36.part_ref, f32[20,16,512]{2,1,0:T(8,128)} %get-tuple-element.37.factor_ref, f32[20,16,512]{2,1,0:T(8,128)} %get-tuple-element.38.reply_ref, ...), custom_call_target="tpu_custom_call" | custom-call | bytes 6684672 | tf_op jit(solution)/shard_map/pallas_call | solution.py:246
  66.1 3.2 %all-to-all-done.1.come_ref = f32[32,4,512]{2,1,0:T(4,128)S(1)} async-done(((f32[32,4,512]{2,1,0:T(4,128)}), f32[32,4,512]{2,1,0:T(4,128)S(1)}, u32[]{:S(2)}, u32[]{:S(2)}) %all-to-all-start.1) | async-done | bytes 262176 | tf_op jit(solution)/shard_map/all_to_all | solution.py:807
  69.4 4.0 %shard_map.145 = f32[4,6912]{1,0:T(4,128)} custom-call(f32[32,4,512]{2,1,0:T(4,128)S(1)} %all-to-all-done.1.come_ref, s32[32,512]{1,0:T(8,128)S(1)} %bitcast.6, f32[32,512]{1,0:T(8,128)S(1)} %bitcast.9, f32[32,256]{1,0:T(8,128)S(1)} %shard_map.144.inverse_ref), custom_call_target="tpu_custom_call" | custom-call | flops 1879048192 | bytes 536576 | tf_op jit(solution)/shard_map/pallas_call | solution.py:246
Async XLA Ops:
  3.0 6.5 %collective-permute-start = (f32[10,320]{1,0:T(8,128)}, f32[10,320]{1,0:T(8,128)S(1)}, u32[]{:S(2)}, u32[]{:S(2)}) collective-permute-start(f32[10,320]{1,0:T(8,128)} %get-tuple-element.26), channel_id=1, source_target_pairs={{0,8},{8,16},{16,24},{24,0},{1,9},{9,17},{17,25},{25,1},{2,10},{10... | collective-permute-start | bytes 38408 | tf_op jit(solution)/shard_map/ppermute | solution.py:676
  6.0 4.0 %collective-permute-start.1 = (f32[10,320]{1,0:T(8,128)}, f32[10,320]{1,0:T(8,128)S(1)}, u32[]{:S(2)}, u32[]{:S(2)}) collective-permute-start(f32[10,320]{1,0:T(8,128)} %get-tuple-element.27), channel_id=1, source_target_pairs={{8,0},{16,8},{24,16},{0,24},{9,1},{17,9},{25,17},{1,25},{10,2},{18... | collective-permute-start | bytes 38408 | tf_op jit(solution)/shard_map/ppermute | solution.py:675
  11.1 0.8 %copy-start = (f32[81,16,128]{2,1,0:T(8,128)}, f32[81,16,128]{2,1,0:T(8,128)S(1)}, u32[]{:S(2)}) copy-start(f32[81,16,128]{2,1,0:T(8,128)S(1)} %get-tuple-element.30.side_in) | copy-start | bytes 1990660
  11.9 7.8 %collective-permute-start.3 = (f32[81,2,640]{2,1,0:T(2,128)}, f32[81,2,640]{2,1,0:T(2,128)S(1)}, u32[]{:S(2)}, u32[]{:S(2)}) collective-permute-start(f32[81,2,640]{2,1,0:T(2,128)} %get-tuple-element.32), channel_id=1, source_target_pairs={{0,1},{1,2},{2,3},{3,4},{4,5},{5,6},{6,7},{8,9},{9,10},{10,11},{11... | collective-permute-start | bytes 1244168 | tf_op jit(solution)/shard_map/ppermute | solution.py:720
  13.2 6.5 %collective-permute-start.4 = (f32[81,2,640]{2,1,0:T(2,128)}, f32[81,2,640]{2,1,0:T(2,128)S(1)}, u32[]{:S(2)}, u32[]{:S(2)}) collective-permute-start(f32[81,2,640]{2,1,0:T(2,128)} %get-tuple-element.32), channel_id=1, source_target_pairs={{7,31},{15,23},{23,15},{31,7}} | collective-permute-start | bytes 1244168 | tf_op jit(solution)/shard_map/ppermute | solution.py:722
  13.9 5.8 %collective-permute-start.2 = (f32[81,2,640]{2,1,0:T(2,128)}, f32[81,2,640]{2,1,0:T(2,128)S(1)}, u32[]{:S(2)}, u32[]{:S(2)}) collective-permute-start(f32[81,2,640]{2,1,0:T(2,128)} %get-tuple-element.31), channel_id=1, source_target_pairs={{1,0},{2,1},{3,2},{4,3},{5,4},{6,5},{7,6},{9,8},{10,9},{11,10},{12... | collective-permute-start | bytes 1244168 | tf_op jit(solution)/shard_map/ppermute | solution.py:719
  19.7 10.5 %copy-start.6 = (f32[81,2,640]{2,1,0:T(2,128)}, f32[81,2,640]{2,1,0:T(2,128)S(1)}, u32[]{:S(2)}) copy-start(f32[81,2,640]{2,1,0:T(2,128)S(1)} %collective-permute-done.3.south_in) | copy-start | bytes 1244164
  19.7 10.5 %copy-start.7 = (f32[81,2,640]{2,1,0:T(2,128)}, f32[81,2,640]{2,1,0:T(2,128)S(1)}, u32[]{:S(2)}) copy-start(f32[81,2,640]{2,1,0:T(2,128)S(1)} %collective-permute-done.4.fold_in) | copy-start | bytes 1244164
  19.7 10.4 %copy-start.8 = (f32[81,2,640]{2,1,0:T(2,128)}, f32[81,2,640]{2,1,0:T(2,128)S(1)}, u32[]{:S(2)}) copy-start(f32[81,2,640]{2,1,0:T(2,128)S(1)} %collective-permute-done.2.north_in) | copy-start | bytes 1244164
  19.8 24.2 %all-to-all-start = ((f32[32,4,512]{2,1,0:T(4,128)}), f32[32,4,512]{2,1,0:T(4,128)S(1)}, u32[]{:S(2)}, u32[]{:S(2)}) async-start(f32[32,4,512]{2,1,0:T(4,128)} %shard_map.140), calls=%async_computation | async-start | bytes 524288 | tf_op jit(solution)/shard_map/all_to_all | solution.py:745
  30.2 13.8 %copy-start.3 = (s32[1,32,512]{2,1,0:T(8,128)S(1)}, s32[1,32,512]{2,1,0:T(8,128)}, u32[]{:S(2)}) copy-start(s32[1,32,512]{2,1,0:T(8,128)} %param.13) | copy-start | bytes 196612
  44.0 0.9 %copy-start.2 = (f32[5,16,512]{2,1,0:T(8,128)S(1)}, f32[5,16,512]{2,1,0:T(8,128)}, u32[]{:S(2)}) copy-start(f32[5,16,512]{2,1,0:T(8,128)} %get-tuple-element.40.top_ref) | copy-start | bytes 491524
  44.9 14.1 %copy-start.4 = (s32[1,32,512]{2,1,0:T(8,128)S(1)}, s32[1,32,512]{2,1,0:T(8,128)}, u32[]{:S(2)}) copy-start(s32[1,32,512]{2,1,0:T(8,128)} %param.11) | copy-start | bytes 196612
  44.9 14.1 %copy-start.5 = (f32[1,32,512]{2,1,0:T(8,128)S(1)}, f32[1,32,512]{2,1,0:T(8,128)}, u32[]{:S(2)}) copy-start(f32[1,32,512]{2,1,0:T(8,128)} %param.12) | copy-start | bytes 196612
  51.8 0.6 copy-start.1
  52.4 16.9 %all-to-all-start.1 = ((f32[32,4,512]{2,1,0:T(4,128)}), f32[32,4,512]{2,1,0:T(4,128)S(1)}, u32[]{:S(2)}, u32[]{:S(2)}) async-start(f32[32,4,512]{2,1,0:T(4,128)} %get-tuple-element.46), calls=%async_computation.1 | async-start | bytes 524288 | tf_op jit(solution)/shard_map/all_to_all | solution.py:807

commit v5 on v4

--- a/solution.py
+++ b/solution.py
@@ -300,7 +300,21 @@
     east_ref[HALO * 4 : HALO * 5, :rows] = east
 
 
-def strip_kernel(t_in, s_in, u_in, v_in, wet_in, down_out, up_out,
+def send_strips(even, leaving, act):
+    def go(swapped):
+        for i, (up, down, out, sem) in enumerate(leaving):
+            act(pltpu.make_async_copy(up if i % 2 == swapped else down, out, sem))
+
+    @pl.when(even)
+    def _():
+        go(0)
+
+    @pl.when(jnp.logical_not(even))
+    def _():
+        go(1)
+
+
+def strip_kernel(t_in, s_in, u_in, v_in, wet_in, pair_out, next_out,
                  field_ref, wet_ref, down_ref, up_ref, in_sem, out_sem):
     fields, levels, rows, cols = field_ref.shape
     copies = [
@@ -310,6 +324,7 @@
     copies.append(pltpu.make_async_copy(wet_in, wet_ref, in_sem.at[fields]))
     for copy in copies:
         copy.start()
+    even = lax.axis_index("ocn") % 2 == 0
     leaving = []
     for f in range(fields + 1):
         copies[f].wait()
@@ -322,21 +337,19 @@
             wet = wet_ref[...].astype(jnp.float32)
             down_ref[fields * levels] = wet[:HALO]
             up_ref[fields * levels] = wet[rows - HALO :]
-        for i, (near, far) in enumerate(((down_ref, down_out), (up_ref, up_out))):
-            copy = pltpu.make_async_copy(
-                near.at[span], far.at[span, :, :cols], out_sem.at[2 * f + i]
-            )
-            copy.start()
-            leaving.append(copy)
-    for copy in leaving:
-        copy.wait()
-
-
-def side_kernel(from_west_ref, from_east_ref, down_in, up_in, down_out, up_out, side_out,
+        leaving += [
+            (up_ref.at[span], down_ref.at[span], out.at[span, :, :cols], out_sem.at[2 * f + i])
+            for i, out in enumerate((pair_out, next_out))
+        ]
+        send_strips(even, leaving[-2:], lambda copy: copy.start())
+    send_strips(even, leaving, lambda copy: copy.wait())
+
+
+def side_kernel(from_west_ref, from_east_ref, pair_in, next_in, pair_out, next_out, side_out,
                 side_ref, low_ref, high_ref, sem):
     channels, rows, _ = side_ref.shape
     levels = (channels - 1) // 4
-    cols = down_out.shape[2] - EDGE
+    cols = pair_out.shape[2] - EDGE
 
     def turned(f, count):
         return jnp.concatenate(
@@ -355,19 +368,20 @@
     side_ref[4 * levels] = turned(4, rows)
     low_ref[...] = side_ref[:, :HALO, :]
     high_ref[...] = side_ref[:, rows - HALO :, :]
-    copies = [
-        pltpu.make_async_copy(low_ref, down_out.at[:, :, cols:], sem.at[0]),
-        pltpu.make_async_copy(high_ref, up_out.at[:, :, cols:], sem.at[1]),
-        pltpu.make_async_copy(side_ref, side_out, sem.at[2]),
+    even = lax.axis_index("ocn") % 2 == 0
+    leaving = [
+        (high_ref, low_ref, out.at[:, :, cols:], sem.at[i])
+        for i, out in enumerate((pair_out, next_out))
     ]
-    for copy in copies:
-        copy.start()
-    for copy in copies:
-        copy.wait()
-
-
-def ocean_kernel(total_rows, t_in, s_in, u_in, v_in, wet_in, side_in, north_in, fold_in,
-                 south_in, mix_in, part_out, factor_out, reply_out, top_ref,
+    side_copy = pltpu.make_async_copy(side_ref, side_out, sem.at[2])
+    side_copy.start()
+    send_strips(even, leaving, lambda copy: copy.start())
+    side_copy.wait()
+    send_strips(even, leaving, lambda copy: copy.wait())
+
+
+def ocean_kernel(total_rows, t_in, s_in, u_in, v_in, wet_in, side_in, pair_in, fold_in,
+                 next_in, mix_in, part_out, factor_out, reply_out, top_ref,
                  t_ref, s_ref, u_ref, v_ref, wet_ref, side_ref, north_ref, fold_ref, south_ref,
                  mix_ref, part_ref, scale_ref, factor_ref, reply_ref, east_gate, north_gate,
                  turn_ref, state_ref, middle_ref, keep_ref, solve_ref, before_ref, in_sem, level_sem, out_sem):
@@ -383,21 +397,37 @@
             (
                 (mix_in, mix_ref),
                 (wet_in, wet_ref),
-                (north_in, north_ref),
-                (south_in, south_ref),
                 (side_in, side_ref),
             )
         )
     ]
     fold_copy = pltpu.make_async_copy(fold_in, fold_ref, in_sem.at[5])
-    for copy in copies[:4]:
+    even = stripe % 2 == 0
+    strips = [
+        (north_ref, south_ref, source, in_sem.at[3 + i])
+        for i, source in enumerate((pair_in, next_in))
+    ]
+
+    def take_strips(swapped, act):
+        for i, (north, south, source, sem) in enumerate(strips):
+            act(pltpu.make_async_copy(source, north if i == swapped else south, sem))
+
+    for copy in copies[:2]:
         copy.start()
+
+    @pl.when(even)
+    def _():
+        take_strips(0, lambda copy: copy.start())
+
+    @pl.when(jnp.logical_not(even))
+    def _():
+        take_strips(1, lambda copy: copy.start())
 
     @pl.when(on_top)
     def _():
         fold_copy.start()
 
-    copies[4].start()
+    copies[2].start()
 
     def field_copy(f, k):
         source, target = ((t_in, t_ref), (s_in, s_ref), (u_in, u_ref), (v_in, v_ref))[f]
@@ -436,6 +466,14 @@
     reply_copy.start()
     for copy in copies[2:]:
         copy.wait()
+
+    @pl.when(even)
+    def _():
+        take_strips(0, lambda copy: copy.wait())
+
+    @pl.when(jnp.logical_not(even))
+    def _():
+        take_strips(1, lambda copy: copy.wait())
 
     @pl.when(on_top)
     def _():
@@ -679,7 +717,7 @@
     far = pl.BlockSpec(memory_space=pltpu.HBM)
     vmem = pl.BlockSpec(memory_space=pltpu.VMEM)
     main = (4 * levels + 1, HALO, block_cols)
-    down, up = pl.pallas_call(
+    pair, other = pl.pallas_call(
         strip_kernel,
         out_shape=[jax.ShapeDtypeStruct(strip, jnp.float32)] * 2,
         in_specs=[far] * 5,
@@ -698,7 +736,7 @@
         ),
     )(*ocean, wet_mask)
     side_shape = (4 * levels + 1, block_rows, EDGE)
-    down, up, side = pl.pallas_call(
+    pair, other, side = pl.pallas_call(
         side_kernel,
         out_shape=[
             jax.ShapeDtypeStruct(strip, jnp.float32),
@@ -715,12 +753,16 @@
         ],
         input_output_aliases={2: 0, 3: 1},
         compiler_params=pltpu.CompilerParams(vmem_limit_bytes=SIDE_BYTES),
-    )(from_west, from_east, down, up)
-    north = lax.ppermute(down, "ocn", [(i + 1, i) for i in range(stripes - 1)])
-    south = lax.ppermute(up, "ocn", [(i, i + 1) for i in range(stripes - 1)])
+    )(from_west, from_east, pair, other)
+    swaps = [
+        [(i + d, i + 1 - d) for i in range(first, stripes - 1, 2) for d in (0, 1)]
+        for first in (0, 1)
+    ]
+    south = lax.ppermute(other, "ocn", swaps[1])
+    north = lax.ppermute(pair, "ocn", swaps[0])
     last = stripes - 1
     fold = lax.ppermute(
-        up,
+        other if last % 2 else pair,
         ("atm", "ocn"),
         [(i * stripes + last, (columns - 1 - i) * stripes + last) for i in range(columns)],
     )

time: 73.7 us -> 71.1 us (0.965)
  starting transfers between devices: 24.2 us -> 21.4 us
    all_to_all x1, starting transfers between devices: 10.4 us -> 6.48 us  [per_device(): lax.all_to_all(outgoing, ('atm', 'ocn'), split_axis=0, concat_axis=0, til...]
    ppermute x3, starting transfers between devices: 3.28 us -> 4.34 us  [the longest x1 2.98 us: per_device(): north = lax.ppermute(pair, 'ocn', swaps[0])]
  transfers between devices with their start and end apart: 7 -> 7, of which waited for: 2 -> 2; matrix products, arithmetic and copies ran while one was open for 0% -> 0% of each run, Pallas kernels for 38% -> 39%
where the time goes in v5:
time: 71.1 us; the launch traced here: 70.7 us
  Pallas kernels  42.3 us (59%)
  starting transfers between devices  21.4 us (30%)
  waiting for transfers between devices  3.74 us (5%)
  local copies, waits for them, and re-layouts  2.43 us (3%)
  between operations  0.85 us (1%)
    pallas_call x6, Pallas kernels, call(): pl.pallas_call(kernel, out_shape=[jax.ShapeDtypeStruct(shape, jnp.float32...  24.8 us
    pallas_call x1, Pallas kernels, per_device(): pl.pallas_call(functools.partial(ocean_kernel, block_rows * stripes), out...  13.7 us
    all_to_all x1, starting transfers between devices, per_device(): lax.all_to_all(leaving, ('atm', 'ocn'), split_axis=0, concat_axis=0, tile...  6.53 us
    all_to_all x1, starting transfers between devices, per_device(): lax.all_to_all(outgoing, ('atm', 'ocn'), split_axis=0, concat_axis=0, til...  6.48 us
    all_to_all x1, waiting for transfers between devices, per_device(): lax.all_to_all(leaving, ('atm', 'ocn'), split_axis=0, concat_axis=0, tile...  3.22 us
    ppermute x1, starting transfers between devices, per_device(): lax.ppermute(east, 'atm', [(i, (i + 1) % columns) for i in range(columns)])  2.99 us
    ppermute x1, starting transfers between devices, per_device(): north = lax.ppermute(pair, 'ocn', swaps[0])  2.98 us
    pallas_call x1, Pallas kernels, per_device(): pl.pallas_call(strip_kernel, out_shape=[jax.ShapeDtypeStruct(strip, jnp.f...  2.49 us
  transfers between devices with their start and end apart: 7, of which 2 were waited for; matrix products, arithmetic and copies ran while one was open for 0% of the time, Pallas kernels for 39%

profile of v5, /device:TPU:0, one launch (start us, length us, event | category | flops | bytes accessed | tf_op | source)
XLA Modules:
  0.0 70.7 jit_solution(7770142614927199367)
XLA Ops:
  0.6 2.4 %shard_map.137 = (f32[10,320]{1,0:T(8,128)}, f32[10,320]{1,0:T(8,128)}) custom-call(f32[20,16,512]{2,1,0:T(8,128)} %t_in.3, f32[20,16,512]{2,1,0:T(8,128)} %s_in.3, f32[20,16,512]{2,1,0:T(8,128)} %u_in.3, f32[20,16,512]{2,1,0:T(8,128)} %v_in.3, s32[16,512]{1,0:T(8,128)} %wet_in.3), custom_call_target="tpu_custom_call" | custom-call | bytes 2679808 | tf_op jit(solution)/shard_map/pallas_call | solution.py:246
  3.0 3.0 %collective-permute-start = (f32[10,320]{1,0:T(8,128)}, f32[10,320]{1,0:T(8,128)S(1)}, u32[]{:S(2)}, u32[]{:S(2)}) collective-permute-start(f32[10,320]{1,0:T(8,128)} %get-tuple-element.26), channel_id=1, source_target_pairs={{0,8},{8,16},{16,24},{24,0},{1,9},{9,17},{17,25},{25,1},{2,10},{10... | collective-permute-start | bytes 38408 | tf_op jit(solution)/shard_map/ppermute | solution.py:714
  6.0 1.0 %collective-permute-start.1 = (f32[10,320]{1,0:T(8,128)}, f32[10,320]{1,0:T(8,128)S(1)}, u32[]{:S(2)}, u32[]{:S(2)}) collective-permute-start(f32[10,320]{1,0:T(8,128)} %get-tuple-element.27), channel_id=1, source_target_pairs={{8,0},{16,8},{24,16},{0,24},{9,1},{17,9},{25,17},{1,25},{10,2},{18... | collective-permute-start | bytes 38408 | tf_op jit(solution)/shard_map/ppermute | solution.py:713
  7.0 2.5 %shard_map.138 = (f32[81,2,640]{2,1,0:T(2,128)}, f32[81,2,640]{2,1,0:T(2,128)}) custom-call(f32[20,16,512]{2,1,0:T(8,128)} %t_in.3, f32[20,16,512]{2,1,0:T(8,128)} %s_in.3, f32[20,16,512]{2,1,0:T(8,128)} %u_in.3, f32[20,16,512]{2,1,0:T(8,128)} %v_in.3, s32[16,512]{1,0:T(8,128)} %wet_in.3), custom_call_target="tpu_custom_call" | custom-call | bytes 3932160 | tf_op jit(solution)/shard_map/pallas_call | solution.py:720
  9.5 0.0 collective-permute-done.from_west_ref
  9.5 0.5 collective-permute-done.1.from_east_ref
  10.0 1.3 %shard_map.139 = (f32[81,2,640]{2,1,0:T(2,128)}, f32[81,2,640]{2,1,0:T(2,128)}, f32[81,16,128]{2,1,0:T(8,128)S(1)}) custom-call(f32[10,320]{1,0:T(8,128)S(1)} %collective-permute-done.from_west_ref, f32[10,320]{1,0:T(8,128)S(1)} %collective-permute-done.1.from_east_ref, ...), custom_call_target="tpu_custom_call", output_to_operand_aliasing={{0}: (2, {}), {1}: (3, {})} | custom-call | tf_op jit(solution)/shard_map/pallas_call | solution.py:739
  11.3 0.0 copy-start
  11.3 0.8 %copy-done = f32[81,16,128]{2,1,0:T(8,128)} copy-done((f32[81,16,128]{2,1,0:T(8,128)}, f32[81,16,128]{2,1,0:T(8,128)S(1)}, u32[]{:S(2)}) %copy-start) | copy-done | bytes 663576
  12.1 0.7 collective-permute-start.3
  12.8 0.7 collective-permute-start.4
  13.5 3.0 %collective-permute-start.2 = (f32[81,2,640]{2,1,0:T(2,128)}, f32[81,2,640]{2,1,0:T(2,128)S(1)}, u32[]{:S(2)}, u32[]{:S(2)}) collective-permute-start(f32[81,2,640]{2,1,0:T(2,128)} %get-tuple-element.31), channel_id=1, source_target_pairs={{0,1},{1,0},{2,3},{3,2},{4,5},{5,4},{6,7},{7,6},{8,9},{9,8},{10,11... | collective-permute-start | bytes 1244168 | tf_op jit(solution)/shard_map/ppermute | solution.py:762
  16.5 4.4 %shard_map.140 = f32[32,4,512]{2,1,0:T(4,128)} custom-call(f32[8,6912]{1,0:T(8,128)} %flux_in.1, s32[32,512]{1,0:T(8,128)} %bitcast.4, f32[32,512]{1,0:T(8,128)} %bitcast.7), custom_call_target="tpu_custom_call" | custom-call | flops 1879048192 | bytes 614400 | tf_op jit(solution)/shard_map/pallas_call | solution.py:246
  20.9 0.0 collective-permute-done.3.next_in
  21.0 0.0 copy-start.6
  21.0 0.0 collective-permute-done.4.fold_in
  21.0 0.0 copy-start.7
  21.0 0.0 collective-permute-done.2.pair_in
  21.0 0.0 copy-start.8
  21.0 6.5 %all-to-all-start = ((f32[32,4,512]{2,1,0:T(4,128)}), f32[32,4,512]{2,1,0:T(4,128)S(1)}, u32[]{:S(2)}, u32[]{:S(2)}) async-start(f32[32,4,512]{2,1,0:T(4,128)} %shard_map.140), calls=%async_computation | async-start | bytes 524288 | tf_op jit(solution)/shard_map/all_to_all | solution.py:787
  27.5 0.0 copy-start.3
  27.5 0.0 copy-done.6
  27.5 0.0 copy-done.7
  27.5 0.0 copy-done.8
  27.5 13.7 %shard_map.141 = (f32[20,4,16,512]{3,2,1,0:T(8,128)}, f32[20,16,512]{2,1,0:T(8,128)}, f32[20,16,512]{2,1,0:T(8,128)}, f32[5,16,512]{2,1,0:T(8,128)}) custom-call(f32[20,16,512]{2,1,0:T(8,128)} %t_in.3, f32[20,16,512]{2,1,0:T(8,128)} %s_in.3, f32[20,16,512]{2,1,0:T(8,128)} %u_in.3, f32[20,16,512]{2,1,0:T(8,128)} %v_in.3, s32[16,512]{1,0:T(8,128)} %wet_in.3, ...), custom_call_target="tpu_custom_call" | custom-call | flops 104857600 | bytes 8519680 | tf_op jit(solution)/shard_map/pallas_call | solution.py:801
  41.3 0.0 all-to-all-done.come_ref
  41.3 0.0 copy-done.3
  41.3 0.0 copy-start.2
  41.3 0.9 %copy-done.2 = f32[5,16,512]{2,1,0:T(8,128)S(1)} copy-done((f32[5,16,512]{2,1,0:T(8,128)S(1)}, f32[5,16,512]{2,1,0:T(8,128)}, u32[]{:S(2)}) %copy-start.2) | copy-done | bytes 163864
  42.2 0.0 copy-start.4
  42.2 0.0 copy-start.5
  42.2 6.9 %shard_map.142 = (f32[4,16,512]{2,1,0:T(8,128)S(1)}, f32[32,4,512]{2,1,0:T(4,128)}) custom-call(f32[32,4,512]{2,1,0:T(4,128)S(1)} %all-to-all-done.come_ref, s32[32,512]{1,0:T(8,128)S(1)} %bitcast.3, f32[5,16,512]{2,1,0:T(8,128)S(1)} %copy-done.2), custom_call_target="tpu_custom_call" | custom-call | flops 4294967296 | bytes 884736 | tf_op jit(solution)/shard_map/pallas_call | solution.py:246
  49.1 0.0 copy-start.1
  49.1 0.6 copy-done.1
  49.8 6.5 %all-to-all-start.1 = ((f32[32,4,512]{2,1,0:T(4,128)}), f32[32,4,512]{2,1,0:T(4,128)S(1)}, u32[]{:S(2)}, u32[]{:S(2)}) async-start(f32[32,4,512]{2,1,0:T(4,128)} %get-tuple-element.46), calls=%async_computation.1 | async-start | bytes 524288 | tf_op jit(solution)/shard_map/all_to_all | solution.py:849
  56.3 0.0 copy-done.4
  56.3 0.0 copy-done.5
  56.3 3.1 %shard_map.144.inverse_ref = f32[32,256]{1,0:T(8,128)S(1)} custom-call(s32[32,512]{1,0:T(8,128)S(1)} %bitcast.5, f32[32,512]{1,0:T(8,128)S(1)} %bitcast.8), custom_call_target="tpu_custom_call" | custom-call | flops 536870912 | bytes 163840 | tf_op jit(solution)/shard_map/pallas_call | solution.py:246
  59.4 4.0 %shard_map.143 = (f32[20,16,512]{2,1,0:T(8,128)}, f32[20,16,512]{2,1,0:T(8,128)}, f32[20,16,512]{2,1,0:T(8,128)}, f32[20,16,512]{2,1,0:T(8,128)}) custom-call(f32[20,4,16,512]{3,2,1,0:T(8,128)} %get-tuple-element.36.part_ref, f32[20,16,512]{2,1,0:T(8,128)} %get-tuple-element.37.factor_ref, f32[20,16,512]{2,1,0:T(8,128)} %get-tuple-element.38.reply_ref, ...), custom_call_target="tpu_custom_call" | custom-call | bytes 6684672 | tf_op jit(solution)/shard_map/pallas_call | solution.py:246
  63.5 3.2 %all-to-all-done.1.come_ref = f32[32,4,512]{2,1,0:T(4,128)S(1)} async-done(((f32[32,4,512]{2,1,0:T(4,128)}), f32[32,4,512]{2,1,0:T(4,128)S(1)}, u32[]{:S(2)}, u32[]{:S(2)}) %all-to-all-start.1) | async-done | bytes 262176 | tf_op jit(solution)/shard_map/all_to_all | solution.py:849
  66.7 4.0 %shard_map.145 = f32[4,6912]{1,0:T(4,128)} custom-call(f32[32,4,512]{2,1,0:T(4,128)S(1)} %all-to-all-done.1.come_ref, s32[32,512]{1,0:T(8,128)S(1)} %bitcast.6, f32[32,512]{1,0:T(8,128)S(1)} %bitcast.9, f32[32,256]{1,0:T(8,128)S(1)} %shard_map.144.inverse_ref), custom_call_target="tpu_custom_call" | custom-call | flops 1879048192 | bytes 536576 | tf_op jit(solution)/shard_map/pallas_call | solution.py:246
Async XLA Ops:
  3.0 6.5 %collective-permute-start = (f32[10,320]{1,0:T(8,128)}, f32[10,320]{1,0:T(8,128)S(1)}, u32[]{:S(2)}, u32[]{:S(2)}) collective-permute-start(f32[10,320]{1,0:T(8,128)} %get-tuple-element.26), channel_id=1, source_target_pairs={{0,8},{8,16},{16,24},{24,0},{1,9},{9,17},{17,25},{25,1},{2,10},{10... | collective-permute-start | bytes 38408 | tf_op jit(solution)/shard_map/ppermute | solution.py:714
  6.0 4.0 %collective-permute-start.1 = (f32[10,320]{1,0:T(8,128)}, f32[10,320]{1,0:T(8,128)S(1)}, u32[]{:S(2)}, u32[]{:S(2)}) collective-permute-start(f32[10,320]{1,0:T(8,128)} %get-tuple-element.27), channel_id=1, source_target_pairs={{8,0},{16,8},{24,16},{0,24},{9,1},{17,9},{25,17},{1,25},{10,2},{18... | collective-permute-start | bytes 38408 | tf_op jit(solution)/shard_map/ppermute | solution.py:713
  11.3 0.8 %copy-start = (f32[81,16,128]{2,1,0:T(8,128)}, f32[81,16,128]{2,1,0:T(8,128)S(1)}, u32[]{:S(2)}) copy-start(f32[81,16,128]{2,1,0:T(8,128)S(1)} %get-tuple-element.30.side_in) | copy-start | bytes 1990660
  12.1 8.8 %collective-permute-start.3 = (f32[81,2,640]{2,1,0:T(2,128)}, f32[81,2,640]{2,1,0:T(2,128)S(1)}, u32[]{:S(2)}, u32[]{:S(2)}) collective-permute-start(f32[81,2,640]{2,1,0:T(2,128)} %get-tuple-element.32), channel_id=1, source_target_pairs={{1,2},{2,1},{3,4},{4,3},{5,6},{6,5},{9,10},{10,9},{11,12},{12,11},... | collective-permute-start | bytes 1244168 | tf_op jit(solution)/shard_map/ppermute | solution.py:761
  12.8 8.1 %collective-permute-start.4 = (f32[81,2,640]{2,1,0:T(2,128)}, f32[81,2,640]{2,1,0:T(2,128)S(1)}, u32[]{:S(2)}, u32[]{:S(2)}) collective-permute-start(f32[81,2,640]{2,1,0:T(2,128)} %get-tuple-element.32), channel_id=1, source_target_pairs={{7,31},{15,23},{23,15},{31,7}} | collective-permute-start | bytes 1244168 | tf_op jit(solution)/shard_map/ppermute | solution.py:764
  13.5 7.5 %collective-permute-start.2 = (f32[81,2,640]{2,1,0:T(2,128)}, f32[81,2,640]{2,1,0:T(2,128)S(1)}, u32[]{:S(2)}, u32[]{:S(2)}) collective-permute-start(f32[81,2,640]{2,1,0:T(2,128)} %get-tuple-element.31), channel_id=1, source_target_pairs={{0,1},{1,0},{2,3},{3,2},{4,5},{5,4},{6,7},{7,6},{8,9},{9,8},{10,11... | collective-permute-start | bytes 1244168 | tf_op jit(solution)/shard_map/ppermute | solution.py:762
  21.0 6.6 %copy-start.6 = (f32[81,2,640]{2,1,0:T(2,128)}, f32[81,2,640]{2,1,0:T(2,128)S(1)}, u32[]{:S(2)}) copy-start(f32[81,2,640]{2,1,0:T(2,128)S(1)} %collective-permute-done.3.next_in) | copy-start | bytes 1244164
  21.0 6.5 %copy-start.7 = (f32[81,2,640]{2,1,0:T(2,128)}, f32[81,2,640]{2,1,0:T(2,128)S(1)}, u32[]{:S(2)}) copy-start(f32[81,2,640]{2,1,0:T(2,128)S(1)} %collective-permute-done.4.fold_in) | copy-start | bytes 1244164
  21.0 6.5 %copy-start.8 = (f32[81,2,640]{2,1,0:T(2,128)}, f32[81,2,640]{2,1,0:T(2,128)S(1)}, u32[]{:S(2)}) copy-start(f32[81,2,640]{2,1,0:T(2,128)S(1)} %collective-permute-done.2.pair_in) | copy-start | bytes 1244164
  21.0 20.3 %all-to-all-start = ((f32[32,4,512]{2,1,0:T(4,128)}), f32[32,4,512]{2,1,0:T(4,128)S(1)}, u32[]{:S(2)}, u32[]{:S(2)}) async-start(f32[32,4,512]{2,1,0:T(4,128)} %shard_map.140), calls=%async_computation | async-start | bytes 524288 | tf_op jit(solution)/shard_map/all_to_all | solution.py:787
  27.5 13.8 %copy-start.3 = (s32[1,32,512]{2,1,0:T(8,128)S(1)}, s32[1,32,512]{2,1,0:T(8,128)}, u32[]{:S(2)}) copy-start(s32[1,32,512]{2,1,0:T(8,128)} %param.13) | copy-start | bytes 196612
  41.3 0.9 %copy-start.2 = (f32[5,16,512]{2,1,0:T(8,128)S(1)}, f32[5,16,512]{2,1,0:T(8,128)}, u32[]{:S(2)}) copy-start(f32[5,16,512]{2,1,0:T(8,128)} %get-tuple-element.40.top_ref) | copy-start | bytes 491524
  42.2 14.1 %copy-start.4 = (s32[1,32,512]{2,1,0:T(8,128)S(1)}, s32[1,32,512]{2,1,0:T(8,128)}, u32[]{:S(2)}) copy-start(s32[1,32,512]{2,1,0:T(8,128)} %param.11) | copy-start | bytes 196612
  42.2 14.1 %copy-start.5 = (f32[1,32,512]{2,1,0:T(8,128)S(1)}, f32[1,32,512]{2,1,0:T(8,128)}, u32[]{:S(2)}) copy-start(f32[1,32,512]{2,1,0:T(8,128)} %param.12) | copy-start | bytes 196612
  49.1 0.6 copy-start.1
  49.8 16.9 %all-to-all-start.1 = ((f32[32,4,512]{2,1,0:T(4,128)}), f32[32,4,512]{2,1,0:T(4,128)S(1)}, u32[]{:S(2)}, u32[]{:S(2)}) async-start(f32[32,4,512]{2,1,0:T(4,128)} %get-tuple-element.46), calls=%async_computation.1 | async-start | bytes 524288 | tf_op jit(solution)/shard_map/all_to_all | solution.py:849

commit v6 on v5

--- a/solution.py
+++ b/solution.py
@@ -19,7 +19,7 @@
 
 LANES = 256
 TERMS = 2
-GROUP = 8
+GROUP = 16
 VMEM_BYTES = 60 * 2**20
 SMALL_BYTES = 24 * 2**20
 SIDE_BYTES = 24 * 2**20

time: 71.1 us -> 70 us (0.985)
  Pallas kernels: 42.3 us -> 40.6 us
    pallas_call x6, Pallas kernels: 24.8 us -> 23.1 us  [call(): pl.pallas_call(kernel, out_shape=[jax.ShapeDtypeStruct(shape, jnp.float32...]
where the time goes in v6:
time: 70 us; the launch traced here: 69.6 us
  Pallas kernels  40.6 us (58%)
  starting transfers between devices  21.7 us (31%)
  waiting for transfers between devices  4.01 us (6%)
  local copies, waits for them, and re-layouts  2.43 us (3%)
  between operations  0.85 us (1%)
    pallas_call x6, Pallas kernels, call(): pl.pallas_call(kernel, out_shape=[jax.ShapeDtypeStruct(shape, jnp.float32...  23.1 us
    pallas_call x1, Pallas kernels, per_device(): pl.pallas_call(functools.partial(ocean_kernel, block_rows * stripes), out...  13.7 us
    all_to_all x1, starting transfers between devices, per_device(): lax.all_to_all(outgoing, ('atm', 'ocn'), split_axis=0, concat_axis=0, til...  6.84 us
    all_to_all x1, starting transfers between devices, per_device(): lax.all_to_all(leaving, ('atm', 'ocn'), split_axis=0, concat_axis=0, tile...  6.53 us
    all_to_all x1, waiting for transfers between devices, per_device(): lax.all_to_all(leaving, ('atm', 'ocn'), split_axis=0, concat_axis=0, tile...  3.49 us
    ppermute x1, starting transfers between devices, per_device(): lax.ppermute(east, 'atm', [(i, (i + 1) % columns) for i in range(columns)])  2.99 us
    ppermute x1, starting transfers between devices, per_device(): north = lax.ppermute(pair, 'ocn', swaps[0])  2.98 us
    pallas_call x1, Pallas kernels, per_device(): pl.pallas_call(strip_kernel, out_shape=[jax.ShapeDtypeStruct(strip, jnp.f...  2.49 us
  transfers between devices with their start and end apart: 7, of which 2 were waited for; matrix products, arithmetic and copies ran while one was open for 0% of the time, Pallas kernels for 39%

profile of v6, /device:TPU:0, one launch (start us, length us, event | category | flops | bytes accessed | tf_op | source)
XLA Modules:
  0.0 69.6 jit_solution(9611514544368127759)
XLA Ops:
  0.6 2.4 %shard_map.137 = (f32[10,320]{1,0:T(8,128)}, f32[10,320]{1,0:T(8,128)}) custom-call(f32[20,16,512]{2,1,0:T(8,128)} %t_in.3, f32[20,16,512]{2,1,0:T(8,128)} %s_in.3, f32[20,16,512]{2,1,0:T(8,128)} %u_in.3, f32[20,16,512]{2,1,0:T(8,128)} %v_in.3, s32[16,512]{1,0:T(8,128)} %wet_in.3), custom_call_target="tpu_custom_call" | custom-call | bytes 2679808 | tf_op jit(solution)/shard_map/pallas_call | solution.py:246
  3.0 3.0 %collective-permute-start = (f32[10,320]{1,0:T(8,128)}, f32[10,320]{1,0:T(8,128)S(1)}, u32[]{:S(2)}, u32[]{:S(2)}) collective-permute-start(f32[10,320]{1,0:T(8,128)} %get-tuple-element.26), channel_id=1, source_target_pairs={{0,8},{8,16},{16,24},{24,0},{1,9},{9,17},{17,25},{25,1},{2,10},{10... | collective-permute-start | bytes 38408 | tf_op jit(solution)/shard_map/ppermute | solution.py:714
  6.0 1.0 %collective-permute-start.1 = (f32[10,320]{1,0:T(8,128)}, f32[10,320]{1,0:T(8,128)S(1)}, u32[]{:S(2)}, u32[]{:S(2)}) collective-permute-start(f32[10,320]{1,0:T(8,128)} %get-tuple-element.27), channel_id=1, source_target_pairs={{8,0},{16,8},{24,16},{0,24},{9,1},{17,9},{25,17},{1,25},{10,2},{18... | collective-permute-start | bytes 38408 | tf_op jit(solution)/shard_map/ppermute | solution.py:713
  7.0 2.5 %shard_map.138 = (f32[81,2,640]{2,1,0:T(2,128)}, f32[81,2,640]{2,1,0:T(2,128)}) custom-call(f32[20,16,512]{2,1,0:T(8,128)} %t_in.3, f32[20,16,512]{2,1,0:T(8,128)} %s_in.3, f32[20,16,512]{2,1,0:T(8,128)} %u_in.3, f32[20,16,512]{2,1,0:T(8,128)} %v_in.3, s32[16,512]{1,0:T(8,128)} %wet_in.3), custom_call_target="tpu_custom_call" | custom-call | bytes 3932160 | tf_op jit(solution)/shard_map/pallas_call | solution.py:720
  9.5 0.0 collective-permute-done.from_west_ref
  9.5 0.5 collective-permute-done.1.from_east_ref
  10.0 1.3 %shard_map.139 = (f32[81,2,640]{2,1,0:T(2,128)}, f32[81,2,640]{2,1,0:T(2,128)}, f32[81,16,128]{2,1,0:T(8,128)S(1)}) custom-call(f32[10,320]{1,0:T(8,128)S(1)} %collective-permute-done.from_west_ref, f32[10,320]{1,0:T(8,128)S(1)} %collective-permute-done.1.from_east_ref, ...), custom_call_target="tpu_custom_call", output_to_operand_aliasing={{0}: (2, {}), {1}: (3, {})} | custom-call | tf_op jit(solution)/shard_map/pallas_call | solution.py:739
  11.3 0.0 copy-start
  11.3 0.8 %copy-done = f32[81,16,128]{2,1,0:T(8,128)} copy-done((f32[81,16,128]{2,1,0:T(8,128)}, f32[81,16,128]{2,1,0:T(8,128)S(1)}, u32[]{:S(2)}) %copy-start) | copy-done | bytes 663576
  12.1 0.7 collective-permute-start.3
  12.8 0.7 collective-permute-start.4
  13.5 3.0 %collective-permute-start.2 = (f32[81,2,640]{2,1,0:T(2,128)}, f32[81,2,640]{2,1,0:T(2,128)S(1)}, u32[]{:S(2)}, u32[]{:S(2)}) collective-permute-start(f32[81,2,640]{2,1,0:T(2,128)} %get-tuple-element.31), channel_id=1, source_target_pairs={{0,1},{1,0},{2,3},{3,2},{4,5},{5,4},{6,7},{7,6},{8,9},{9,8},{10,11... | collective-permute-start | bytes 1244168 | tf_op jit(solution)/shard_map/ppermute | solution.py:762
  16.5 4.1 %shard_map.140 = f32[32,4,512]{2,1,0:T(4,128)} custom-call(f32[8,6912]{1,0:T(8,128)} %flux_in.1, s32[32,512]{1,0:T(8,128)} %bitcast.4, f32[32,512]{1,0:T(8,128)} %bitcast.7), custom_call_target="tpu_custom_call" | custom-call | flops 1879048192 | bytes 614400 | tf_op jit(solution)/shard_map/pallas_call | solution.py:246
  20.6 0.0 collective-permute-done.3.next_in
  20.6 0.0 copy-start.6
  20.6 0.0 collective-permute-done.4.fold_in
  20.6 0.0 copy-start.7
  20.6 0.0 collective-permute-done.2.pair_in
  20.6 0.0 copy-start.8
  20.7 6.8 %all-to-all-start = ((f32[32,4,512]{2,1,0:T(4,128)}), f32[32,4,512]{2,1,0:T(4,128)S(1)}, u32[]{:S(2)}, u32[]{:S(2)}) async-start(f32[32,4,512]{2,1,0:T(4,128)} %shard_map.140), calls=%async_computation | async-start | bytes 524288 | tf_op jit(solution)/shard_map/all_to_all | solution.py:787
  27.5 0.0 copy-start.3
  27.5 0.0 copy-done.6
  27.5 0.0 copy-done.7
  27.5 0.0 copy-done.8
  27.5 13.7 %shard_map.141 = (f32[20,4,16,512]{3,2,1,0:T(8,128)}, f32[20,16,512]{2,1,0:T(8,128)}, f32[20,16,512]{2,1,0:T(8,128)}, f32[5,16,512]{2,1,0:T(8,128)}) custom-call(f32[20,16,512]{2,1,0:T(8,128)} %t_in.3, f32[20,16,512]{2,1,0:T(8,128)} %s_in.3, f32[20,16,512]{2,1,0:T(8,128)} %u_in.3, f32[20,16,512]{2,1,0:T(8,128)} %v_in.3, s32[16,512]{1,0:T(8,128)} %wet_in.3, ...), custom_call_target="tpu_custom_call" | custom-call | flops 104857600 | bytes 8519680 | tf_op jit(solution)/shard_map/pallas_call | solution.py:801
  41.3 0.0 all-to-all-done.come_ref
  41.3 0.0 copy-done.3
  41.3 0.0 copy-start.2
  41.3 0.9 %copy-done.2 = f32[5,16,512]{2,1,0:T(8,128)S(1)} copy-done((f32[5,16,512]{2,1,0:T(8,128)S(1)}, f32[5,16,512]{2,1,0:T(8,128)}, u32[]{:S(2)}) %copy-start.2) | copy-done | bytes 163864
  42.2 0.0 copy-start.4
  42.2 0.0 copy-start.5
  42.2 6.2 %shard_map.142 = (f32[4,16,512]{2,1,0:T(8,128)S(1)}, f32[32,4,512]{2,1,0:T(4,128)}) custom-call(f32[32,4,512]{2,1,0:T(4,128)S(1)} %all-to-all-done.come_ref, s32[32,512]{1,0:T(8,128)S(1)} %bitcast.3, f32[5,16,512]{2,1,0:T(8,128)S(1)} %copy-done.2), custom_call_target="tpu_custom_call" | custom-call | flops 4294967296 | bytes 884736 | tf_op jit(solution)/shard_map/pallas_call | solution.py:246
  48.4 0.0 copy-start.1
  48.4 0.6 copy-done.1
  49.0 6.5 %all-to-all-start.1 = ((f32[32,4,512]{2,1,0:T(4,128)}), f32[32,4,512]{2,1,0:T(4,128)S(1)}, u32[]{:S(2)}, u32[]{:S(2)}) async-start(f32[32,4,512]{2,1,0:T(4,128)} %get-tuple-element.46), calls=%async_computation.1 | async-start | bytes 524288 | tf_op jit(solution)/shard_map/all_to_all | solution.py:849
  55.6 0.0 copy-done.4
  55.6 0.0 copy-done.5
  55.6 2.8 %shard_map.144.inverse_ref = f32[32,256]{1,0:T(8,128)S(1)} custom-call(s32[32,512]{1,0:T(8,128)S(1)} %bitcast.5, f32[32,512]{1,0:T(8,128)S(1)} %bitcast.8), custom_call_target="tpu_custom_call" | custom-call | flops 536870912 | bytes 163840 | tf_op jit(solution)/shard_map/pallas_call | solution.py:246
  58.4 4.0 %shard_map.143 = (f32[20,16,512]{2,1,0:T(8,128)}, f32[20,16,512]{2,1,0:T(8,128)}, f32[20,16,512]{2,1,0:T(8,128)}, f32[20,16,512]{2,1,0:T(8,128)}) custom-call(f32[20,4,16,512]{3,2,1,0:T(8,128)} %get-tuple-element.36.part_ref, f32[20,16,512]{2,1,0:T(8,128)} %get-tuple-element.37.factor_ref, f32[20,16,512]{2,1,0:T(8,128)} %get-tuple-element.38.reply_ref, ...), custom_call_target="tpu_custom_call" | custom-call | bytes 6684672 | tf_op jit(solution)/shard_map/pallas_call | solution.py:246
  62.5 3.5 %all-to-all-done.1.come_ref = f32[32,4,512]{2,1,0:T(4,128)S(1)} async-done(((f32[32,4,512]{2,1,0:T(4,128)}), f32[32,4,512]{2,1,0:T(4,128)S(1)}, u32[]{:S(2)}, u32[]{:S(2)}) %all-to-all-start.1) | async-done | bytes 262176 | tf_op jit(solution)/shard_map/all_to_all | solution.py:849
  66.0 3.6 %shard_map.145 = f32[4,6912]{1,0:T(4,128)} custom-call(f32[32,4,512]{2,1,0:T(4,128)S(1)} %all-to-all-done.1.come_ref, s32[32,512]{1,0:T(8,128)S(1)} %bitcast.6, f32[32,512]{1,0:T(8,128)S(1)} %bitcast.9, f32[32,256]{1,0:T(8,128)S(1)} %shard_map.144.inverse_ref), custom_call_target="tpu_custom_call" | custom-call | flops 1879048192 | bytes 536576 | tf_op jit(solution)/shard_map/pallas_call | solution.py:246
Async XLA Ops:
  3.0 6.5 %collective-permute-start = (f32[10,320]{1,0:T(8,128)}, f32[10,320]{1,0:T(8,128)S(1)}, u32[]{:S(2)}, u32[]{:S(2)}) collective-permute-start(f32[10,320]{1,0:T(8,128)} %get-tuple-element.26), channel_id=1, source_target_pairs={{0,8},{8,16},{16,24},{24,0},{1,9},{9,17},{17,25},{25,1},{2,10},{10... | collective-permute-start | bytes 38408 | tf_op jit(solution)/shard_map/ppermute | solution.py:714
  6.0 4.0 %collective-permute-start.1 = (f32[10,320]{1,0:T(8,128)}, f32[10,320]{1,0:T(8,128)S(1)}, u32[]{:S(2)}, u32[]{:S(2)}) collective-permute-start(f32[10,320]{1,0:T(8,128)} %get-tuple-element.27), channel_id=1, source_target_pairs={{8,0},{16,8},{24,16},{0,24},{9,1},{17,9},{25,17},{1,25},{10,2},{18... | collective-permute-start | bytes 38408 | tf_op jit(solution)/shard_map/ppermute | solution.py:713
  11.3 0.8 %copy-start = (f32[81,16,128]{2,1,0:T(8,128)}, f32[81,16,128]{2,1,0:T(8,128)S(1)}, u32[]{:S(2)}) copy-start(f32[81,16,128]{2,1,0:T(8,128)S(1)} %get-tuple-element.30.side_in) | copy-start | bytes 1990660
  12.1 8.4 %collective-permute-start.3 = (f32[81,2,640]{2,1,0:T(2,128)}, f32[81,2,640]{2,1,0:T(2,128)S(1)}, u32[]{:S(2)}, u32[]{:S(2)}) collective-permute-start(f32[81,2,640]{2,1,0:T(2,128)} %get-tuple-element.32), channel_id=1, source_target_pairs={{1,2},{2,1},{3,4},{4,3},{5,6},{6,5},{9,10},{10,9},{11,12},{12,11},... | collective-permute-start | bytes 1244168 | tf_op jit(solution)/shard_map/ppermute | solution.py:761
  12.8 7.8 %collective-permute-start.4 = (f32[81,2,640]{2,1,0:T(2,128)}, f32[81,2,640]{2,1,0:T(2,128)S(1)}, u32[]{:S(2)}, u32[]{:S(2)}) collective-permute-start(f32[81,2,640]{2,1,0:T(2,128)} %get-tuple-element.32), channel_id=1, source_target_pairs={{7,31},{15,23},{23,15},{31,7}} | collective-permute-start | bytes 1244168 | tf_op jit(solution)/shard_map/ppermute | solution.py:764
  13.5 7.1 %collective-permute-start.2 = (f32[81,2,640]{2,1,0:T(2,128)}, f32[81,2,640]{2,1,0:T(2,128)S(1)}, u32[]{:S(2)}, u32[]{:S(2)}) collective-permute-start(f32[81,2,640]{2,1,0:T(2,128)} %get-tuple-element.31), channel_id=1, source_target_pairs={{0,1},{1,0},{2,3},{3,2},{4,5},{5,4},{6,7},{7,6},{8,9},{9,8},{10,11... | collective-permute-start | bytes 1244168 | tf_op jit(solution)/shard_map/ppermute | solution.py:762
  20.6 6.9 %copy-start.6 = (f32[81,2,640]{2,1,0:T(2,128)}, f32[81,2,640]{2,1,0:T(2,128)S(1)}, u32[]{:S(2)}) copy-start(f32[81,2,640]{2,1,0:T(2,128)S(1)} %collective-permute-done.3.next_in) | copy-start | bytes 1244164
  20.6 6.9 %copy-start.7 = (f32[81,2,640]{2,1,0:T(2,128)}, f32[81,2,640]{2,1,0:T(2,128)S(1)}, u32[]{:S(2)}) copy-start(f32[81,2,640]{2,1,0:T(2,128)S(1)} %collective-permute-done.4.fold_in) | copy-start | bytes 1244164
  20.6 6.9 %copy-start.8 = (f32[81,2,640]{2,1,0:T(2,128)}, f32[81,2,640]{2,1,0:T(2,128)S(1)}, u32[]{:S(2)}) copy-start(f32[81,2,640]{2,1,0:T(2,128)S(1)} %collective-permute-done.2.pair_in) | copy-start | bytes 1244164
  20.7 20.6 %all-to-all-start = ((f32[32,4,512]{2,1,0:T(4,128)}), f32[32,4,512]{2,1,0:T(4,128)S(1)}, u32[]{:S(2)}, u32[]{:S(2)}) async-start(f32[32,4,512]{2,1,0:T(4,128)} %shard_map.140), calls=%async_computation | async-start | bytes 524288 | tf_op jit(solution)/shard_map/all_to_all | solution.py:787
  27.5 13.8 %copy-start.3 = (s32[1,32,512]{2,1,0:T(8,128)S(1)}, s32[1,32,512]{2,1,0:T(8,128)}, u32[]{:S(2)}) copy-start(s32[1,32,512]{2,1,0:T(8,128)} %param.13) | copy-start | bytes 196612
  41.3 0.9 %copy-start.2 = (f32[5,16,512]{2,1,0:T(8,128)S(1)}, f32[5,16,512]{2,1,0:T(8,128)}, u32[]{:S(2)}) copy-start(f32[5,16,512]{2,1,0:T(8,128)} %get-tuple-element.40.top_ref) | copy-start | bytes 491524
  42.2 13.3 %copy-start.4 = (s32[1,32,512]{2,1,0:T(8,128)S(1)}, s32[1,32,512]{2,1,0:T(8,128)}, u32[]{:S(2)}) copy-start(s32[1,32,512]{2,1,0:T(8,128)} %param.11) | copy-start | bytes 196612
  42.2 13.3 %copy-start.5 = (f32[1,32,512]{2,1,0:T(8,128)S(1)}, f32[1,32,512]{2,1,0:T(8,128)}, u32[]{:S(2)}) copy-start(f32[1,32,512]{2,1,0:T(8,128)} %param.12) | copy-start | bytes 196612
  48.4 0.6 copy-start.1
  49.0 16.9 %all-to-all-start.1 = ((f32[32,4,512]{2,1,0:T(4,128)}), f32[32,4,512]{2,1,0:T(4,128)S(1)}, u32[]{:S(2)}, u32[]{:S(2)}) async-start(f32[32,4,512]{2,1,0:T(4,128)} %get-tuple-element.46), calls=%async_computation.1 | async-start | bytes 524288 | tf_op jit(solution)/shard_map/all_to_all | solution.py:849
